TPU v7x, 32 devices: a whole 2x2x4 slice. The times are simulated.
32 devices in a mesh: batch: 8 (over z, x), head: 4 (over y, core).
Axes of the slice: x: 2, y: 2, z: 4, core: 2. Of those that a mesh axis runs over, the one named last changes fastest.
Arguments:
- tokens: bfloat16 [16384, 768], P(('batch', 'head')), may hold values from -6 to 6
- cotangent: bfloat16 [16384, 768], P(('batch', 'head')), may hold values from -6 to 6
- lengths: int32 [8, 3], P('batch'), may hold values from 1 to 1024, 2048 in all within a row
- input_weight: float32 [2304, 768], P(('batch', 'head')), may hold values from -0.21875 to 0.21875
- output_weight: float32 [768, 768], P(('batch', 'head')), may hold values from -0.875 to 0.875
- expand_weight: float32 [3072, 768], P(('batch', 'head')), may hold values from -0.21875 to 0.21875
- contract_weight: float32 [768, 3072], P(('batch', 'head')), may hold values from -0.109375 to 0.109375
- vector_params: float32 [9216], replicated, may hold values from -0.8 to 1.6, as said below
- input_first: float32 [2304, 768], P(('batch', 'head')), may hold values from -0.005859375 to 0.005859375
- input_second: float32 [2304, 768], P(('batch', 'head')), may hold values from 1.4128508e-07 to 5.6514034e-07
- output_first: float32 [768, 768], P(('batch', 'head')), may hold values from -0.005859375 to 0.005859375
- output_second: float32 [768, 768], P(('batch', 'head')), may hold values from 1.4128508e-07 to 5.6514034e-07
- expand_first: float32 [3072, 768], P(('batch', 'head')), may hold values from -0.005859375 to 0.005859375
- expand_second: float32 [3072, 768], P(('batch', 'head')), may hold values from 1.4128508e-07 to 5.6514034e-07
- contract_first: float32 [768, 3072], P(('batch', 'head')), may hold values from -0.005859375 to 0.005859375
- contract_second: float32 [768, 3072], P(('batch', 'head')), may hold values from 1.4128508e-07 to 5.6514034e-07
- vector_first: float32 [9216], replicated, may hold values from -0.0234375 to 0.0234375
- vector_second: float32 [9216], replicated, may hold values from 2.2605614e-06 to 9.042245e-06
Outputs:
- block_out: bfloat16 [16384, 768], P(('batch', 'head'))
- input_grad: bfloat16 [16384, 768], P(('batch', 'head'))
- grad_norm: float32 [], replicated
- matrix_norms: float32 [8], replicated
- input_first_new: float32 [2304, 768], P(('batch', 'head'))
- input_second_new: float32 [2304, 768], P(('batch', 'head'))
- input_weight_new: float32 [2304, 768], P(('batch', 'head'))
- input_weight_low: bfloat16 [2304, 768], P(('batch', 'head'))
- output_first_new: float32 [768, 768], P(('batch', 'head'))
- output_second_new: float32 [768, 768], P(('batch', 'head'))
- output_weight_new: float32 [768, 768], P(('batch', 'head'))
- output_weight_low: bfloat16 [768, 768], P(('batch', 'head'))
- expand_first_new: float32 [3072, 768], P(('batch', 'head'))
- expand_second_new: float32 [3072, 768], P(('batch', 'head'))
- expand_weight_new: float32 [3072, 768], P(('batch', 'head'))
- expand_weight_low: bfloat16 [3072, 768], P(('batch', 'head'))
- contract_first_new: float32 [768, 3072], P(('batch', 'head'))
- contract_second_new: float32 [768, 3072], P(('batch', 'head'))
- contract_weight_new: float32 [768, 3072], P(('batch', 'head'))
- contract_weight_low: bfloat16 [768, 3072], P(('batch', 'head'))
- vector_first_new: float32 [9216], replicated
- vector_second_new: float32 [9216], replicated
- vector_params_new: float32 [9216], replicated
Inputs may be any that keep to these rules, and one draw needn't show every extreme that they name: Each row holds 3 lengths summing to 2048; the longest in every row is exactly half of 2048. `vector_params`: entries 0 to 767 and 1536 to 2303 are norm gains near 1; the rest are shifts and biases.
All inputs are finite; a program needn't handle non-finite values.
Results may differ from a plain program's by a relative error of at most 0.012.
Values may be sent and summed in bfloat16 or wider, within the bound.
No kernel may reach another device: no remote copies, remote signals or barrier semaphores. Data moves between devices by JAX's collectives and lax.ppermute only.
A program may use at most 192 MiB of HBM per device.

v0:
```python
from functools import partial

import jax
import jax.numpy as jnp
from jax import lax
from jax.sharding import PartitionSpec as P

D = 768
HD = 64
FF = 3072
STEP = 5


NORM_EPS = 1e-05
ADAM_EPS = 1e-06
DECAY_RATE = 0.01
MATRIX_RATE = 0.5
VECTOR_RATE = 0.1


def layer_norm(values, gain_vec, bias_vec):
    row_mean = jnp.mean(values, axis=-1, keepdims=True)
    centered = values - row_mean
    variance = jnp.mean(centered * centered, axis=-1, keepdims=True)
    return centered * lax.rsqrt(variance + NORM_EPS) * gain_vec + bias_vec


def unpack_vector(params):
    pieces = [params[position * D : (position + 1) * D] for position in range(8)]
    return pieces + [params[8 * D : 8 * D + FF]]


def masked_scores(query_block, key_rows, segment, offset, block_rows, score_scale):
    scores = (
        jnp.einsum("qhd,khd->hqk", query_block, key_rows, preferred_element_type=jnp.float32)
        * score_scale
    )
    query_pos = offset + jnp.arange(block_rows, dtype=jnp.int32)
    key_pos = jnp.arange(key_rows.shape[0], dtype=jnp.int32)
    query_seg = lax.dynamic_slice_in_dim(segment, offset, block_rows, 0)
    allowed = (key_pos[None, :] <= query_pos[:, None]) & (query_seg[:, None] == segment[None, :])
    return jnp.where(allowed[None], scores, -1e30)


def head_forward(head_inputs, segment, block_count, block_rows, score_scale):
    group_rows = head_inputs.shape[1]
    heads_here = head_inputs.shape[2] // HD
    queries = head_inputs[0].reshape(group_rows, heads_here, HD)
    key_rows = head_inputs[1].reshape(group_rows, heads_here, HD)
    value_rows = head_inputs[2].reshape(group_rows, heads_here, HD)

    def one_block(block_index):
        offset = block_index * block_rows
        query_block = lax.dynamic_slice_in_dim(queries, offset, block_rows, 0)
        scores = masked_scores(query_block, key_rows, segment, offset, block_rows, score_scale)
        row_max = jnp.max(scores, axis=-1, keepdims=True)
        exponent = jnp.exp(scores - row_max)
        row_total = jnp.sum(exponent, axis=-1, keepdims=True)
        soft_weights = (exponent / row_total).astype(jnp.bfloat16)
        attended = jnp.einsum(
            "hqk,khd->qhd", soft_weights, value_rows, preferred_element_type=jnp.float32
        )
        return (attended.astype(jnp.bfloat16), row_max + jnp.log(row_total))

    attended, log_totals = lax.map(one_block, jnp.arange(block_count, dtype=jnp.int32))
    return (attended.reshape(group_rows, heads_here * HD), log_totals)


def head_backward(
    head_inputs, grad_heads, log_totals, segment, block_count, block_rows, score_scale
):
    group_rows = head_inputs.shape[1]
    heads_here = head_inputs.shape[2] // HD
    queries = head_inputs[0].reshape(group_rows, heads_here, HD)
    key_rows = head_inputs[1].reshape(group_rows, heads_here, HD)
    value_rows = head_inputs[2].reshape(group_rows, heads_here, HD)
    grad_out = grad_heads.reshape(group_rows, heads_here, HD)

    def one_block(state_pair, scan_item):
        grad_keys, grad_values = state_pair
        block_index, block_logs = scan_item
        offset = block_index * block_rows
        query_block = lax.dynamic_slice_in_dim(queries, offset, block_rows, 0)
        grad_block = lax.dynamic_slice_in_dim(grad_out, offset, block_rows, 0)
        scores = masked_scores(query_block, key_rows, segment, offset, block_rows, score_scale)
        probs = jnp.exp(scores - block_logs)
        grad_values = grad_values + jnp.einsum(
            "hqk,qhd->khd",
            probs.astype(jnp.bfloat16),
            grad_block,
            preferred_element_type=jnp.float32,
        )
        grad_probs = jnp.einsum(
            "qhd,khd->hqk", grad_block, value_rows, preferred_element_type=jnp.float32
        )
        row_delta = jnp.sum(probs * grad_probs, axis=-1, keepdims=True)
        grad_scores = (probs * (grad_probs - row_delta)).astype(jnp.bfloat16)
        grad_queries = (
            jnp.einsum("hqk,khd->qhd", grad_scores, key_rows, preferred_element_type=jnp.float32)
            * score_scale
        )
        grad_keys = (
            grad_keys
            + jnp.einsum(
                "hqk,qhd->khd", grad_scores, query_block, preferred_element_type=jnp.float32
            )
            * score_scale
        )
        return ((grad_keys, grad_values), grad_queries)

    zero_state = jnp.zeros((group_rows, heads_here, HD), jnp.float32)
    final_state, grad_queries = lax.scan(
        one_block, (zero_state, zero_state), (jnp.arange(block_count, dtype=jnp.int32), log_totals)
    )
    width_here = heads_here * HD
    stacked = jnp.stack(
        [
            grad_queries.reshape(group_rows, width_here),
            final_state[0].reshape(group_rows, width_here),
            final_state[1].reshape(group_rows, width_here),
        ]
    )
    return stacked.astype(jnp.bfloat16)


def adam_direction(gradient, first_old, second_old, master, clip_factor):
    clipped = gradient * clip_factor
    first_new = 0.5 * first_old + 0.5 * clipped
    second_new = 0.5 * second_old + 0.5 * clipped * clipped
    correction = 1.0 - 0.5**STEP
    direction = (
        first_new / correction / (jnp.sqrt(second_new / correction) + ADAM_EPS)
        + DECAY_RATE * master
    )
    return (first_new, second_new, direction)


def on_device(
    tokens,
    cotangent,
    lengths,
    input_weight,
    output_weight,
    expand_weight,
    contract_weight,
    vector_params,
    input_first,
    input_second,
    output_first,
    output_second,
    expand_first,
    expand_second,
    contract_first,
    contract_second,
    vector_first,
    vector_second,
):
    head_count = lax.axis_size("head")
    local_rows = tokens.shape[0]
    group_rows = local_rows * head_count
    block_rows = min(512, group_rows)
    block_count = group_rows // block_rows
    score_scale = HD ** (-0.5)
    (
        gain_one,
        bias_one,
        gain_two,
        bias_two,
        bias_query,
        bias_value,
        bias_output,
        bias_contract,
        bias_expand,
    ) = unpack_vector(vector_params)
    full_input, full_output, full_expand, full_contract = (
        lax.all_gather(input_weight.astype(jnp.bfloat16), ("batch", "head"), axis=0, tiled=True),
        lax.all_gather(output_weight.astype(jnp.bfloat16), ("batch", "head"), axis=0, tiled=True),
        lax.all_gather(expand_weight.astype(jnp.bfloat16), ("batch", "head"), axis=0, tiled=True),
        lax.all_gather(contract_weight.astype(jnp.bfloat16), ("batch", "head"), axis=0, tiled=True),
    )
    stacked_input = full_input.reshape(3, D, D)
    doc_ends = jnp.cumsum(lengths[0])
    positions = jnp.arange(group_rows, dtype=jnp.int32)
    segment = jnp.sum((positions[:, None] >= doc_ends[None, :]).astype(jnp.int32), axis=1)
    resid_in = tokens.astype(jnp.float32)
    normed_one = layer_norm(resid_in, gain_one, bias_one).astype(jnp.bfloat16)
    input_bias = jnp.stack([bias_query, jnp.zeros_like(bias_query), bias_value])[:, None, :]
    projected = (
        jnp.einsum("td,cod->cto", normed_one, stacked_input, preferred_element_type=jnp.float32)
        + input_bias
    ).astype(jnp.bfloat16)
    head_inputs = lax.all_to_all(projected, "head", split_axis=2, concat_axis=1, tiled=True)
    head_out, log_totals = head_forward(head_inputs, segment, block_count, block_rows, score_scale)
    attended = lax.all_to_all(head_out, "head", split_axis=0, concat_axis=1, tiled=True)
    branch = (
        jnp.einsum("tc,oc->to", attended, full_output, preferred_element_type=jnp.float32)
        + bias_output
    )
    resid_mid = resid_in + branch
    normed_two = layer_norm(resid_mid, gain_two, bias_two).astype(jnp.bfloat16)
    expanded = (
        jnp.einsum("td,fd->tf", normed_two, full_expand, preferred_element_type=jnp.float32)
        + bias_expand
    )
    activated = jax.nn.gelu(expanded, approximate=True).astype(jnp.bfloat16)
    block_out = (
        resid_mid
        + jnp.einsum("tf,of->to", activated, full_contract, preferred_element_type=jnp.float32)
        + bias_contract
    ).astype(jnp.bfloat16)
    upstream = cotangent.astype(jnp.float32)
    grad_contract = jnp.einsum(
        "to,tf->of", cotangent, activated, preferred_element_type=jnp.float32
    )
    grad_activated = jnp.einsum(
        "to,of->tf", cotangent, full_contract, preferred_element_type=jnp.float32
    )
    unused_gelu, gelu_pull = jax.vjp(partial(jax.nn.gelu, approximate=True), expanded)
    grad_expanded = gelu_pull(grad_activated)[0].astype(jnp.bfloat16)
    grad_expand = jnp.einsum(
        "tf,td->fd", grad_expanded, normed_two, preferred_element_type=jnp.float32
    )
    grad_normed_two = jnp.einsum(
        "tf,fd->td", grad_expanded, full_expand, preferred_element_type=jnp.float32
    )
    unused_second, norm_pull_two = jax.vjp(layer_norm, resid_mid, gain_two, bias_two)
    grad_mid_norm, grad_gain_two, grad_bias_two = norm_pull_two(grad_normed_two)
    grad_mid = upstream + grad_mid_norm
    grad_branch = grad_mid.astype(jnp.bfloat16)
    grad_output = jnp.einsum("to,tc->oc", grad_branch, attended, preferred_element_type=jnp.float32)
    grad_attended = jnp.einsum(
        "to,oc->tc", grad_branch, full_output, preferred_element_type=jnp.float32
    ).astype(jnp.bfloat16)
    grad_heads = lax.all_to_all(grad_attended, "head", split_axis=1, concat_axis=0, tiled=True)
    grad_projected_heads = head_backward(
        head_inputs, grad_heads, log_totals, segment, block_count, block_rows, score_scale
    )
    grad_projected = lax.all_to_all(
        grad_projected_heads, "head", split_axis=1, concat_axis=2, tiled=True
    )
    grad_input = jnp.einsum(
        "cto,td->cod", grad_projected, normed_one, preferred_element_type=jnp.float32
    ).reshape(3 * D, D)
    grad_normed_one = jnp.einsum(
        "cto,cod->td", grad_projected, stacked_input, preferred_element_type=jnp.float32
    )
    unused_first, norm_pull_one = jax.vjp(layer_norm, resid_in, gain_one, bias_one)
    grad_in_norm, grad_gain_one, grad_bias_one = norm_pull_one(grad_normed_one)
    input_grad = (grad_mid + grad_in_norm).astype(jnp.bfloat16)
    projected_sums = jnp.sum(grad_projected.astype(jnp.float32), axis=1)
    vector_local = jnp.concatenate(
        [
            grad_gain_one,
            grad_bias_one,
            grad_gain_two,
            grad_bias_two,
            projected_sums[0],
            projected_sums[2],
            jnp.sum(grad_branch.astype(jnp.float32), axis=0),
            jnp.sum(upstream, axis=0),
            jnp.sum(grad_expanded.astype(jnp.float32), axis=0),
        ]
    )
    shard_grads = (
        lax.psum_scatter(grad_input, ("batch", "head"), scatter_dimension=0, tiled=True),
        lax.psum_scatter(grad_output, ("batch", "head"), scatter_dimension=0, tiled=True),
        lax.psum_scatter(grad_expand, ("batch", "head"), scatter_dimension=0, tiled=True),
        lax.psum_scatter(grad_contract, ("batch", "head"), scatter_dimension=0, tiled=True),
    )
    vector_grads = lax.psum(vector_local, ("batch", "head"))
    masters = (input_weight, output_weight, expand_weight, contract_weight)
    firsts = (input_first, output_first, expand_first, contract_first)
    seconds = (input_second, output_second, expand_second, contract_second)
    local_grad_sq = jnp.sum(
        jnp.stack([jnp.sum(piece_grad * piece_grad) for piece_grad in shard_grads])
    )
    weight_sq = jnp.stack([jnp.sum(master * master) for master in masters])
    grad_total = lax.psum(local_grad_sq, ("batch", "head"))
    grad_norm = jnp.sqrt(grad_total + jnp.sum(vector_grads * vector_grads))
    clip_factor = jnp.minimum(1.0, 1.0 / grad_norm)
    updated = [
        adam_direction(piece_grad, first_old, second_old, master, clip_factor)
        for piece_grad, first_old, second_old, master in zip(shard_grads, firsts, seconds, masters)
    ]
    update_sq = jnp.stack([jnp.sum(entry[2] * entry[2]) for entry in updated])
    weight_total, update_total = lax.psum((weight_sq, update_sq), ("batch", "head"))
    weight_norms = jnp.sqrt(weight_total)
    update_norms = jnp.sqrt(update_total)
    matrix_norms = jnp.concatenate([weight_norms, update_norms])
    results = []
    for position in range(4):
        first_new, second_new, direction = updated[position]
        new_master = (
            masters[position]
            - MATRIX_RATE * (weight_norms[position] / update_norms[position]) * direction
        )
        results.append((first_new, second_new, new_master, new_master.astype(jnp.bfloat16)))
    vector_first_new, vector_second_new, vector_direction = adam_direction(
        vector_grads, vector_first, vector_second, vector_params, clip_factor
    )
    vector_new = vector_params - VECTOR_RATE * vector_direction
    return (
        block_out,
        input_grad,
        grad_norm,
        matrix_norms,
        results[0][0],
        results[0][1],
        results[0][2],
        results[0][3],
        results[1][0],
        results[1][1],
        results[1][2],
        results[1][3],
        results[2][0],
        results[2][1],
        results[2][2],
        results[2][3],
        results[3][0],
        results[3][1],
        results[3][2],
        results[3][3],
        vector_first_new,
        vector_second_new,
        vector_new,
    )


def solution(mesh):
    placed = (
        P(("batch", "head"), None),
        P(("batch", "head"), None),
        P("batch", None),
        P(("batch", "head"), None),
        P(("batch", "head"), None),
        P(("batch", "head"), None),
        P(("batch", "head"), None),
        P(),
        P(("batch", "head"), None),
        P(("batch", "head"), None),
        P(("batch", "head"), None),
        P(("batch", "head"), None),
        P(("batch", "head"), None),
        P(("batch", "head"), None),
        P(("batch", "head"), None),
        P(("batch", "head"), None),
        P(),
        P(),
    )
    return jax.shard_map(
        on_device,
        mesh=mesh,
        in_specs=placed,
        out_specs=(
            P(("batch", "head"), None),
            P(("batch", "head"), None),
            P(),
            P(),
            P(("batch", "head"), None),
            P(("batch", "head"), None),
            P(("batch", "head"), None),
            P(("batch", "head"), None),
            P(("batch", "head"), None),
            P(("batch", "head"), None),
            P(("batch", "head"), None),
            P(("batch", "head"), None),
            P(("batch", "head"), None),
            P(("batch", "head"), None),
            P(("batch", "head"), None),
            P(("batch", "head"), None),
            P(("batch", "head"), None),
            P(("batch", "head"), None),
            P(("batch", "head"), None),
            P(("batch", "head"), None),
            P(),
            P(),
            P(),
        ),
        check_vma=False,
    )
```

profile of v0, /device:TPU:0, one launch (start us, length us, event | category | flops | bytes accessed | tf_op | source)
XLA Modules:
  0.0 1045.7 jit_solution(12122490935082801218)
XLA Ops:
  17.2 57.2 %all-gather.5.cloned.1.call-done = bf16[2304,768]{1,0:T(8,128)(2,1)} async-done(((bf16[72,768]{1,0:T(8,128)(2,1)}), bf16[2304,768]{1,0:T(8,128)(2,1)}) %all-gather.5.cloned.1.call-update) | async-done | bytes 3538960 | tf_op jit(solution)/shard_map/all_gather | solution.py:176
  88.2 38.3 %all-to-all-done = bf16[3,512,768]{1,0,2:T(4,128)(2,1)S(1)} async-done(((bf16[3,512,768]{1,0,2:T(4,128)(2,1)}), bf16[3,512,768]{1,0,2:T(4,128)(2,1)S(1)}, u32[]{:S(2)}, u32[]{:S(2)}) %all-to-all-start) | async-done | bytes 2359328 | tf_op jit(solution)/shard_map/all_to_all | solution.py:192
  130.9 90.1 %while.27 = (s32[]{:T(128)}, bf16[4,512,3,64]{1,3,2,0:T(8,128)(2,1)}, f32[4,3,512,1]{2,1,3,0:T(4,128)S(1)}, s32[4]{0:T(128)S(1)}, s32[2048]{0:T(1024)S(1)}, /*in...) while((s32[]{:T(128)}, ...), condition=%wide.region_7.8_spmd, body=%wide.region_4.7_spmd.sunk | while | flops 846298112 | bytes 43983052 | solution.py:65
  139.2 6.8 fusion.141
  146.1 7.3 fusion.142
  168.6 7.3 fusion.142
  191.2 7.3 fusion.142
  206.9 6.8 fusion.141
  213.7 7.3 fusion.142
  226.2 12.4 %all-to-all-done.1 = bf16[4,512,192]{1,2,0:T(8,128)(2,1)} async-done(((bf16[4,512,192]{1,2,0:T(8,128)(2,1)}), bf16[4,512,192]{1,2,0:T(8,128)(2,1)}, u32[]{:S(2)}, u32[]{:S(2)}) %all-to-all-start.1) | async-done | bytes 786464 | tf_op jit(solution)/shard_map/all_to_all | solution.py:194
  242.7 8.7 fusion.72
  251.3 13.3 %all-gather.11.cloned.1.call-done = bf16[768,3072]{1,0:T(8,128)(2,1)} async-done(((bf16[24,3072]{1,0:T(8,128)(2,1)}), bf16[768,3072]{1,0:T(8,128)(2,1)}) %all-gather.11.cloned.1.call-update) | async-done | bytes 4718608 | tf_op jit(solution)/shard_map/all_gather | solution.py:179
  264.6 10.3 convert_reduce_fusion
  291.2 7.9 all-to-all-done.2
  303.3 140.8 %while.28 = (s32[]{:T(128)}, f32[2048,3,64]{0,2,1:T(8,128)}, f32[2048,3,64]{0,2,1:T(8,128)}, bf16[4,512,3,64]{1,3,2,0:T(8,128)(2,1)}, s32[4]{0:T(128)S(1)}, /*in...) while((s32[]{:T(128)}, f32[2048,3,64]{0,2,1:T(8,128)}, ...), condition=%wide.region_14.15_spmd.clone, body=%wide.region_12.14_spmd.clone.sunk | while | flops 2065660928 | bytes 219607728 | solution.py:112
  309.7 7.4 multiply_reduce_fusion.18
  328.8 6.9 fusion.155
  344.6 7.3 multiply_reduce_fusion.18
  364.0 6.8 fusion.155
  379.7 7.3 multiply_reduce_fusion.18
  414.8 7.3 multiply_reduce_fusion.18
  455.3 53.8 %all_to_all.68 = bf16[3,2048,192]{2,0,1:T(4,128)(2,1)} all-to-all(bf16[3,2048,192]{2,0,1:T(4,128)(2,1)} %copy.155), channel_id=1, replica_groups=mesh['batch'=8,'head'=4] {'head'}, dimensions={1} | all-to-all | bytes 4718592 | tf_op jit(solution)/shard_map/all_to_all | solution.py:238
  521.1 10.0 convolution_bitcast_fusion
  531.1 9.9 copy.165
  542.5 8.4 fusion.71
  551.0 7.5 copy.163
  569.7 68.3 %reduce-scatter.7.cloned.1.call-done = f32[72,768]{1,0:T(8,128)} async-done(((f32[2304,768]{1,0:T(8,128)}), f32[72,768]{1,0:T(8,128)}) %reduce-scatter.7.cloned.1.call-update) | async-done | bytes 221200 | tf_op jit(solution)/shard_map/reduce_scatter | solution.py:265
  640.9 137.9 %reduce-scatter.13.cloned.1.call-done = f32[24,3072]{1,0:T(8,128)} async-done(((f32[768,3072]{1,0:T(8,128)}), f32[24,3072]{1,0:T(8,128)}) %reduce-scatter.13.cloned.1.call-update) | async-done | bytes 294928 | tf_op jit(solution)/shard_map/reduce_scatter | solution.py:268
  781.2 139.2 %reduce-scatter.11.cloned.1.call-done = f32[96,768]{1,0:T(8,128)} async-done(((f32[3072,768]{1,0:T(8,128)}), f32[96,768]{1,0:T(8,128)}) %reduce-scatter.11.cloned.1.call-update) | async-done | bytes 294928 | tf_op jit(solution)/shard_map/reduce_scatter | solution.py:267
  923.5 9.2 add_convert_fusion.2
  932.7 40.5 %all-reduce.1 = (f32[]{:T(128)}, f32[9216]{0:T(1024)S(1)}) all-reduce(f32[]{:T(128)S(6)} %reduce_sum.364, f32[9216]{0:T(1024)S(1)} %constant_dynamic-update-slice_fusion), channel_id=1, replica_groups=mesh['batch'=8,'head'=4] {'batch','head'}, use_global_device_ids=true, to_apply=%region_25.26 | all-reduce | flops 9217 | bytes 73736 | tf_op jit(solution)/shard_map/psum | solution.py:278
  987.0 39.2 %all-reduce = (f32[4]{0:T(128)S(1)}, f32[4]{0:T(128)S(1)}) all-reduce(f32[4]{0:T(128)S(1)} %get-tuple-element.418, f32[4]{0:T(128)S(1)} %get-tuple-element.417), channel_id=1, replica_groups=mesh['batch'=8,'head'=4] {'batch','head'}, use_global_device_ids=true, to_apply=%region_45.46 | all-reduce | flops 8 | bytes 64 | tf_op jit(solution)/shard_map/psum | solution.py:286
  (441 shorter events, 254.9 us)
Async XLA Ops:
  7.2 67.2 %all-gather.5.cloned.1.call-start = ((), (), s32[]{:S(2)}) async-start(), calls=%async_computation.8 | async-start | bytes 3649536 | tf_op jit(solution)/shard_map/all_gather | solution.py:176
  8.9 217.4 %all-gather.7.cloned.1.call-start = ((), (), s32[]{:S(2)}) async-start(), calls=%async_computation.9 | async-start | bytes 1216512 | tf_op jit(solution)/shard_map/all_gather | solution.py:177
  10.4 232.2 %all-gather.9.cloned.1.call-start = ((), (), s32[]{:S(2)}) async-start(), calls=%async_computation.10 | async-start | bytes 4866048 | tf_op jit(solution)/shard_map/all_gather | solution.py:178
  13.6 65.2 %copy-start.49 = (f32[768]{0:T(1024)}, f32[768]{0:T(1024)S(1)}, u32[]{:S(2)}) copy-start(f32[768]{0:T(1024)S(1)} %get-tuple-element.403) | copy-start | bytes 9220
  13.6 65.2 %copy-start.74 = (f32[768]{0:T(1024)}, f32[768]{0:T(1024)S(1)}, u32[]{:S(2)}) copy-start(f32[768]{0:T(1024)S(1)} %get-tuple-element.402) | copy-start | bytes 9220
  15.0 63.8 %copy-start.53 = (f32[512]{0:T(512)}, f32[512]{0:T(512)S(1)}, u32[]{:S(2)}) copy-start(f32[512]{0:T(512)S(1)} %broadcast_multiply_fusion.1) | copy-start | bytes 6148
  17.1 61.7 %copy-start.55 = (f32[512]{0:T(512)}, f32[512]{0:T(512)S(1)}, u32[]{:S(2)}) copy-start(f32[512]{0:T(512)S(1)} %fusion.65) | copy-start | bytes 6148
  83.2 43.4 %all-to-all-start = ((bf16[3,512,768]{1,0,2:T(4,128)(2,1)}), bf16[3,512,768]{1,0,2:T(4,128)(2,1)S(1)}, u32[]{:S(2)}, u32[]{:S(2)}) async-start(bf16[3,512,768]{1,0,2:T(4,128)(2,1)} %copy.147), calls=%async_computation | async-start | bytes 6291456 | tf_op jit(solution)/shard_map/all_to_all | solution.py:192
  87.0 177.6 %all-gather.11.cloned.1.call-start = ((), (), s32[]{:S(2)}) async-start(), calls=%async_computation.11 | async-start | bytes 4866048 | tf_op jit(solution)/shard_map/all_gather | solution.py:179
  130.9 107.8 %copy-start.9 = (bf16[512,768]{1,0:T(8,128)(2,1)S(1)}, bf16[512,768]{1,0:T(8,128)(2,1)}, u32[]{:S(2)}) copy-start(bf16[512,768]{1,0:T(8,128)(2,1)} %param.22) | copy-start | bytes 2359300
  130.9 107.8 %copy-start.76 = (f32[768]{0:T(1024)S(1)}, f32[768]{0:T(1024)}, u32[]{:S(2)}) copy-start(f32[768]{0:T(1024)} %get-tuple-element.399) | copy-start | bytes 9220
  221.1 17.6 %all-to-all-start.1 = ((bf16[4,512,192]{1,2,0:T(8,128)(2,1)}), bf16[4,512,192]{1,2,0:T(8,128)(2,1)}, u32[]{:S(2)}, u32[]{:S(2)}) async-start(bf16[4,512,192]{1,2,0:T(8,128)(2,1)} %bitcast.159), calls=%async_computation.1 | async-start | bytes 1572864 | tf_op jit(solution)/shard_map/all_to_all | solution.py:194
  283.9 15.1 %all-to-all-start.2 = ((bf16[512,4,192]{0,2,1:T(8,128)(2,1)}), bf16[512,4,192]{0,2,1:T(8,128)(2,1)S(1)}, u32[]{:S(2)}, u32[]{:S(2)}) async-start(bf16[512,4,192]{0,2,1:T(8,128)(2,1)} %bitcast.154), calls=%async_computation.2 | async-start | bytes 1572864 | tf_op jit(solution)/shard_map/all_to_all | solution.py:234
  287.4 280.7 %reduce-scatter.9.cloned.1.call-start = ((), (), s32[]{:S(2)}) async-start(), calls=%async_computation.13 | async-start | bytes 2433024 | tf_op jit(solution)/shard_map/reduce_scatter | solution.py:266
  291.1 346.9 %reduce-scatter.7.cloned.1.call-start = ((), (), s32[]{:S(2)}) async-start(), calls=%async_computation.12 | async-start | bytes 7299072 | tf_op jit(solution)/shard_map/reduce_scatter | solution.py:265
  520.0 258.8 %reduce-scatter.13.cloned.1.call-start = ((), (), s32[]{:S(2)}) async-start(), calls=%async_computation.15 | async-start | bytes 9732096 | tf_op jit(solution)/shard_map/reduce_scatter | solution.py:268
  541.1 379.4 %reduce-scatter.11.cloned.1.call-start = ((), (), s32[]{:S(2)}) async-start(), calls=%async_computation.14 | async-start | bytes 9732096 | tf_op jit(solution)/shard_map/reduce_scatter | solution.py:267
  568.1 355.4 %copy-start.16 = (f32[512,768]{1,0:T(8,128)S(1)}, f32[512,768]{1,0:T(8,128)}, u32[]{:S(2)}) copy-start(f32[512,768]{1,0:T(8,128)} %copy-done.13) | copy-start | bytes 4718596
  568.1 355.4 %copy-start.71 = (f32[768]{0:T(1024)S(1)}, f32[768]{0:T(1024)}, u32[]{:S(2)}) copy-start(f32[768]{0:T(1024)} %get-tuple-element.404) | copy-start | bytes 9220
  923.5 53.6 %copy-start.21 = (f32[96,768]{1,0:T(8,128)S(1)}, f32[96,768]{1,0:T(8,128)}, u32[]{:S(2)}) copy-start(f32[96,768]{1,0:T(8,128)} %param.27) | copy-start | bytes 884740
  923.5 53.6 %copy-start.29 = (f32[96,768]{1,0:T(8,128)S(1)}, f32[96,768]{1,0:T(8,128)}, u32[]{:S(2)}) copy-start(f32[96,768]{1,0:T(8,128)} %reduce-scatter.11.cloned.1.call-done) | copy-start | bytes 884740
  932.7 100.6 %copy-start.46 = (f32[9216]{0:T(1024)S(1)}, f32[9216]{0:T(1024)}, u32[]{:S(2)}) copy-start(f32[9216]{0:T(1024)} %param.29) | copy-start | bytes 110596
  932.7 100.6 %copy-start.51 = (f32[9216]{0:T(1024)S(1)}, f32[9216]{0:T(1024)}, u32[]{:S(2)}) copy-start(f32[9216]{0:T(1024)} %param.39) | copy-start | bytes 110596
  973.2 60.2 %copy-start.52 = (f32[9216]{0:T(1024)S(1)}, f32[9216]{0:T(1024)}, u32[]{:S(2)}) copy-start(f32[9216]{0:T(1024)} %param.38) | copy-start | bytes 110596
  977.0 59.5 %copy-start.30 = (f32[24,3072]{1,0:T(8,128)}, f32[24,3072]{1,0:T(8,128)S(1)}, u32[]{:S(2)}) copy-start(f32[24,3072]{1,0:T(8,128)S(1)} %get-tuple-element.378) | copy-start | bytes 884740
  977.0 59.5 %copy-start.31 = (f32[24,3072]{1,0:T(8,128)}, f32[24,3072]{1,0:T(8,128)S(1)}, u32[]{:S(2)}) copy-start(f32[24,3072]{1,0:T(8,128)S(1)} %get-tuple-element.379) | copy-start | bytes 884740
  979.2 58.3 %copy-start.32 = (f32[96,768]{1,0:T(8,128)}, f32[96,768]{1,0:T(8,128)S(1)}, u32[]{:S(2)}) copy-start(f32[96,768]{1,0:T(8,128)S(1)} %get-tuple-element.376) | copy-start | bytes 884740
  979.2 58.3 %copy-start.33 = (f32[96,768]{1,0:T(8,128)}, f32[96,768]{1,0:T(8,128)S(1)}, u32[]{:S(2)}) copy-start(f32[96,768]{1,0:T(8,128)S(1)} %get-tuple-element.377) | copy-start | bytes 884740
  979.9 57.6 %copy-start.43 = (f32[24,768]{1,0:T(8,128)}, f32[24,768]{1,0:T(8,128)S(1)}, u32[]{:S(2)}) copy-start(f32[24,768]{1,0:T(8,128)S(1)} %get-tuple-element.374) | copy-start | bytes 221188
  979.9 57.5 %copy-start.44 = (f32[24,768]{1,0:T(8,128)}, f32[24,768]{1,0:T(8,128)S(1)}, u32[]{:S(2)}) copy-start(f32[24,768]{1,0:T(8,128)S(1)} %get-tuple-element.375) | copy-start | bytes 221188
  981.7 55.8 %copy-start.34 = (f32[72,768]{1,0:T(8,128)}, f32[72,768]{1,0:T(8,128)S(1)}, u32[]{:S(2)}) copy-start(f32[72,768]{1,0:T(8,128)S(1)} %get-tuple-element.372) | copy-start | bytes 663556
  981.7 55.8 %copy-start.35 = (f32[72,768]{1,0:T(8,128)}, f32[72,768]{1,0:T(8,128)S(1)}, u32[]{:S(2)}) copy-start(f32[72,768]{1,0:T(8,128)S(1)} %get-tuple-element.373) | copy-start | bytes 663556
  (106 other events, 1050.2 us)
Sparse Core Ops, SparseCore 0:
  11.5 62.8 all-gather.4
  77.9 54.3 all-gather.6
  135.7 62.5 all-gather.8
  201.7 62.8 all-gather.10
  293.2 99.3 reduce-scatter.8
  520.1 117.8 reduce-scatter.6
  643.9 134.8 reduce-scatter.12
  785.7 134.7 reduce-scatter.10
where the time goes:
time: 1050 us
  waiting for transfers between devices  475 us (45%)
  matrix products  220 us (21%)
  blocking collectives  134 us (13%)
  other arithmetic  108 us (10%)
  local copies, waits for them, and re-layouts  64.5 us (6%)
  between operations  25.8 us (2%)
  starting transfers between devices  12.3 us (1%)
    reduce_scatter x1, waiting for transfers between devices, on_device(): lax.psum_scatter(grad_expand, ('batch', 'head'), scatter_dimension=0, til...  139 us
    reduce_scatter x1, waiting for transfers between devices, on_device(): lax.psum_scatter(grad_contract, ('batch', 'head'), scatter_dimension=0, t...  138 us
    reduce_scatter x1, waiting for transfers between devices, on_device(): lax.psum_scatter(grad_input, ('batch', 'head'), scatter_dimension=0, tile...  68.3 us
    all_gather x1, waiting for transfers between devices, on_device(): lax.all_gather(input_weight.astype(jnp.bfloat16), ('batch', 'head'), axis...  57.2 us
    all_to_all x1, blocking collectives, on_device(): lax.all_to_all(grad_projected_heads, 'head', split_axis=1, concat_axis=2,...  53.8 us
    psum x1, blocking collectives, on_device(): grad_total = lax.psum(local_grad_sq, ('batch', 'head'))  40.5 us
    psum x1, blocking collectives, on_device(): lax.psum((weight_sq, update_sq), ('batch', 'head'))  39.2 us
    all_to_all x1, waiting for transfers between devices, on_device(): lax.all_to_all(projected, 'head', split_axis=2, concat_axis=1, tiled=True)  38.3 us
  transfers between devices with their start and end apart: 11, of which 8 were waited for; matrix products, arithmetic and copies ran while one was open for 32% of the time, Pallas kernels for 0%

commit v1 on v0

--- a/solution.py
+++ b/solution.py
@@ -179,7 +179,7 @@
         lax.all_gather(contract_weight.astype(jnp.bfloat16), ("batch", "head"), axis=0, tiled=True),
     )
     stacked_input = full_input.reshape(3, D, D)
-    doc_ends = jnp.cumsum(lengths[0])
+    doc_ends = jnp.stack([jnp.sum(lengths[0, : position + 1]) for position in range(lengths.shape[1])])
     positions = jnp.arange(group_rows, dtype=jnp.int32)
     segment = jnp.sum((positions[:, None] >= doc_ends[None, :]).astype(jnp.int32), axis=1)
     resid_in = tokens.astype(jnp.float32)

time: 1050 us -> 1050 us (level)
  no operation moved by 1% of the time
where the time goes in v1:
time: 1050 us
  waiting for transfers between devices  472 us (45%)
  matrix products  220 us (21%)
  blocking collectives  134 us (13%)
  other arithmetic  110 us (10%)
  local copies, waits for them, and re-layouts  64.5 us (6%)
  between operations  25.8 us (2%)
  starting transfers between devices  12.3 us (1%)
    reduce_scatter x1, waiting for transfers between devices, on_device(): lax.psum_scatter(grad_expand, ('batch', 'head'), scatter_dimension=0, til...  139 us
    reduce_scatter x1, waiting for transfers between devices, on_device(): lax.psum_scatter(grad_contract, ('batch', 'head'), scatter_dimension=0, t...  138 us
    reduce_scatter x1, waiting for transfers between devices, on_device(): lax.psum_scatter(grad_input, ('batch', 'head'), scatter_dimension=0, tile...  68.3 us
    all_gather x1, waiting for transfers between devices, on_device(): lax.all_gather(input_weight.astype(jnp.bfloat16), ('batch', 'head'), axis...  57.2 us
    all_to_all x1, blocking collectives, on_device(): lax.all_to_all(grad_projected_heads, 'head', split_axis=1, concat_axis=2,...  53.8 us
    psum x1, blocking collectives, on_device(): grad_total = lax.psum(local_grad_sq, ('batch', 'head'))  40.7 us
    psum x1, blocking collectives, on_device(): lax.psum((weight_sq, update_sq), ('batch', 'head'))  39.3 us
    all_to_all x1, waiting for transfers between devices, on_device(): lax.all_to_all(projected, 'head', split_axis=2, concat_axis=1, tiled=True)  35.8 us
  transfers between devices with their start and end apart: 11, of which 8 were waited for; matrix products, arithmetic and copies ran while one was open for 32% of the time, Pallas kernels for 0%

profile of v1, /device:TPU:0, one launch (start us, length us, event | category | flops | bytes accessed | tf_op | source)
XLA Modules:
  0.0 1045.3 jit_solution(83864289830116474)
XLA Ops:
  17.2 57.2 %all-gather.5.cloned.1.call-done = bf16[2304,768]{1,0:T(8,128)(2,1)} async-done(((bf16[72,768]{1,0:T(8,128)(2,1)}), bf16[2304,768]{1,0:T(8,128)(2,1)}) %all-gather.5.cloned.1.call-update) | async-done | bytes 3538960 | tf_op jit(solution)/shard_map/all_gather | solution.py:176
  90.7 35.8 %all-to-all-done = bf16[3,512,768]{1,0,2:T(4,128)(2,1)S(1)} async-done(((bf16[3,512,768]{1,0,2:T(4,128)(2,1)}), bf16[3,512,768]{1,0,2:T(4,128)(2,1)S(1)}, u32[]{:S(2)}, u32[]{:S(2)}) %all-to-all-start) | async-done | bytes 2359328 | tf_op jit(solution)/shard_map/all_to_all | solution.py:192
  130.9 90.2 %while.27 = (s32[]{:T(128)}, bf16[4,512,3,64]{1,3,2,0:T(8,128)(2,1)}, f32[4,3,512,1]{2,1,3,0:T(4,128)S(1)}, s32[4]{0:T(128)S(1)}, s32[2048]{0:T(1024)S(1)}, /*in...) while((s32[]{:T(128)}, ...), condition=%wide.region_8.9_spmd, body=%wide.region_5.8_spmd.sunk | while | flops 846298112 | bytes 43983052 | solution.py:65
  139.3 6.8 fusion.141
  146.1 7.3 fusion.142
  168.7 7.3 fusion.142
  191.2 7.4 fusion.142
  206.9 6.9 fusion.141
  213.8 7.3 fusion.142
  226.3 12.4 %all-to-all-done.1 = bf16[4,512,192]{1,2,0:T(8,128)(2,1)} async-done(((bf16[4,512,192]{1,2,0:T(8,128)(2,1)}), bf16[4,512,192]{1,2,0:T(8,128)(2,1)}, u32[]{:S(2)}, u32[]{:S(2)}) %all-to-all-start.1) | async-done | bytes 786464 | tf_op jit(solution)/shard_map/all_to_all | solution.py:194
  242.8 8.6 fusion.72
  251.4 13.3 %all-gather.11.cloned.1.call-done = bf16[768,3072]{1,0:T(8,128)(2,1)} async-done(((bf16[24,3072]{1,0:T(8,128)(2,1)}), bf16[768,3072]{1,0:T(8,128)(2,1)}) %all-gather.11.cloned.1.call-update) | async-done | bytes 4718608 | tf_op jit(solution)/shard_map/all_gather | solution.py:179
  264.7 10.3 convert_reduce_fusion
  291.2 7.9 all-to-all-done.2
  303.4 140.6 %while.28 = (s32[]{:T(128)}, f32[2048,3,64]{0,2,1:T(8,128)}, f32[2048,3,64]{0,2,1:T(8,128)}, bf16[4,512,3,64]{1,3,2,0:T(8,128)(2,1)}, s32[4]{0:T(128)S(1)}, /*in...) while((s32[]{:T(128)}, f32[2048,3,64]{0,2,1:T(8,128)}, ...), condition=%wide.region_15.16_spmd.clone, body=%wide.region_13.15_spmd.clone.sunk | while | flops 2065660928 | bytes 219607728 | solution.py:112
  309.7 7.4 multiply_reduce_fusion.18
  328.8 6.9 fusion.155
  344.6 7.3 multiply_reduce_fusion.18
  363.9 6.8 fusion.155
  379.6 7.3 multiply_reduce_fusion.18
  414.7 7.3 multiply_reduce_fusion.18
  455.1 53.8 %all_to_all.68 = bf16[3,2048,192]{2,0,1:T(4,128)(2,1)} all-to-all(bf16[3,2048,192]{2,0,1:T(4,128)(2,1)} %copy.155), channel_id=1, replica_groups=mesh['batch'=8,'head'=4] {'head'}, dimensions={1} | all-to-all | bytes 4718592 | tf_op jit(solution)/shard_map/all_to_all | solution.py:238
  520.9 10.0 convolution_bitcast_fusion
  531.0 9.9 copy.165
  542.4 8.5 fusion.71
  550.9 7.5 copy.163
  569.6 68.3 %reduce-scatter.7.cloned.1.call-done = f32[72,768]{1,0:T(8,128)} async-done(((f32[2304,768]{1,0:T(8,128)}), f32[72,768]{1,0:T(8,128)}) %reduce-scatter.7.cloned.1.call-update) | async-done | bytes 221200 | tf_op jit(solution)/shard_map/reduce_scatter | solution.py:265
  640.7 137.9 %reduce-scatter.13.cloned.1.call-done = f32[24,3072]{1,0:T(8,128)} async-done(((f32[768,3072]{1,0:T(8,128)}), f32[24,3072]{1,0:T(8,128)}) %reduce-scatter.13.cloned.1.call-update) | async-done | bytes 294928 | tf_op jit(solution)/shard_map/reduce_scatter | solution.py:268
  781.1 138.7 %reduce-scatter.11.cloned.1.call-done = f32[96,768]{1,0:T(8,128)} async-done(((f32[3072,768]{1,0:T(8,128)}), f32[96,768]{1,0:T(8,128)}) %reduce-scatter.11.cloned.1.call-update) | async-done | bytes 294928 | tf_op jit(solution)/shard_map/reduce_scatter | solution.py:267
  922.9 9.2 add_convert_fusion.2
  932.1 40.7 %all-reduce.1 = (f32[]{:T(128)}, f32[9216]{0:T(1024)S(1)}) all-reduce(f32[]{:T(128)S(6)} %reduce_sum.388, f32[9216]{0:T(1024)S(1)} %constant_dynamic-update-slice_fusion), channel_id=1, replica_groups=mesh['batch'=8,'head'=4] {'batch','head'}, use_global_device_ids=true, to_apply=%region_26.27 | all-reduce | flops 9217 | bytes 73736 | tf_op jit(solution)/shard_map/psum | solution.py:278
  986.6 39.3 %all-reduce = (f32[4]{0:T(128)S(1)}, f32[4]{0:T(128)S(1)}) all-reduce(f32[4]{0:T(128)S(1)} %get-tuple-element.418, f32[4]{0:T(128)S(1)} %get-tuple-element.417), channel_id=1, replica_groups=mesh['batch'=8,'head'=4] {'batch','head'}, use_global_device_ids=true, to_apply=%region_46.47 | all-reduce | flops 8 | bytes 64 | tf_op jit(solution)/shard_map/psum | solution.py:286
  (443 shorter events, 257.3 us)
Async XLA Ops:
  7.2 67.2 %all-gather.5.cloned.1.call-start = ((), (), s32[]{:S(2)}) async-start(), calls=%async_computation.8 | async-start | bytes 3649536 | tf_op jit(solution)/shard_map/all_gather | solution.py:176
  8.9 217.4 %all-gather.7.cloned.1.call-start = ((), (), s32[]{:S(2)}) async-start(), calls=%async_computation.9 | async-start | bytes 1216512 | tf_op jit(solution)/shard_map/all_gather | solution.py:177
  10.4 232.3 %all-gather.9.cloned.1.call-start = ((), (), s32[]{:S(2)}) async-start(), calls=%async_computation.10 | async-start | bytes 4866048 | tf_op jit(solution)/shard_map/all_gather | solution.py:178
  13.6 65.2 %copy-start.49 = (f32[768]{0:T(1024)}, f32[768]{0:T(1024)S(1)}, u32[]{:S(2)}) copy-start(f32[768]{0:T(1024)S(1)} %get-tuple-element.403) | copy-start | bytes 9220
  13.6 65.2 %copy-start.74 = (f32[768]{0:T(1024)}, f32[768]{0:T(1024)S(1)}, u32[]{:S(2)}) copy-start(f32[768]{0:T(1024)S(1)} %get-tuple-element.402) | copy-start | bytes 9220
  15.0 63.8 %copy-start.53 = (f32[512]{0:T(512)}, f32[512]{0:T(512)S(1)}, u32[]{:S(2)}) copy-start(f32[512]{0:T(512)S(1)} %broadcast_multiply_fusion.1) | copy-start | bytes 6148
  17.1 61.7 %copy-start.55 = (f32[512]{0:T(512)}, f32[512]{0:T(512)S(1)}, u32[]{:S(2)}) copy-start(f32[512]{0:T(512)S(1)} %fusion.65) | copy-start | bytes 6148
  83.2 43.4 %all-to-all-start = ((bf16[3,512,768]{1,0,2:T(4,128)(2,1)}), bf16[3,512,768]{1,0,2:T(4,128)(2,1)S(1)}, u32[]{:S(2)}, u32[]{:S(2)}) async-start(bf16[3,512,768]{1,0,2:T(4,128)(2,1)} %copy.147), calls=%async_computation | async-start | bytes 6291456 | tf_op jit(solution)/shard_map/all_to_all | solution.py:192
  87.0 177.7 %all-gather.11.cloned.1.call-start = ((), (), s32[]{:S(2)}) async-start(), calls=%async_computation.11 | async-start | bytes 4866048 | tf_op jit(solution)/shard_map/all_gather | solution.py:179
  130.9 107.8 %copy-start.9 = (bf16[512,768]{1,0:T(8,128)(2,1)S(1)}, bf16[512,768]{1,0:T(8,128)(2,1)}, u32[]{:S(2)}) copy-start(bf16[512,768]{1,0:T(8,128)(2,1)} %param.22) | copy-start | bytes 2359300
  130.9 107.8 %copy-start.76 = (f32[768]{0:T(1024)S(1)}, f32[768]{0:T(1024)}, u32[]{:S(2)}) copy-start(f32[768]{0:T(1024)} %get-tuple-element.399) | copy-start | bytes 9220
  221.1 17.6 %all-to-all-start.1 = ((bf16[4,512,192]{1,2,0:T(8,128)(2,1)}), bf16[4,512,192]{1,2,0:T(8,128)(2,1)}, u32[]{:S(2)}, u32[]{:S(2)}) async-start(bf16[4,512,192]{1,2,0:T(8,128)(2,1)} %bitcast.161), calls=%async_computation.1 | async-start | bytes 1572864 | tf_op jit(solution)/shard_map/all_to_all | solution.py:194
  284.0 15.1 %all-to-all-start.2 = ((bf16[512,4,192]{0,2,1:T(8,128)(2,1)}), bf16[512,4,192]{0,2,1:T(8,128)(2,1)S(1)}, u32[]{:S(2)}, u32[]{:S(2)}) async-start(bf16[512,4,192]{0,2,1:T(8,128)(2,1)} %bitcast.156), calls=%async_computation.2 | async-start | bytes 1572864 | tf_op jit(solution)/shard_map/all_to_all | solution.py:234
  287.5 280.5 %reduce-scatter.9.cloned.1.call-start = ((), (), s32[]{:S(2)}) async-start(), calls=%async_computation.13 | async-start | bytes 2433024 | tf_op jit(solution)/shard_map/reduce_scatter | solution.py:266
  291.2 346.7 %reduce-scatter.7.cloned.1.call-start = ((), (), s32[]{:S(2)}) async-start(), calls=%async_computation.12 | async-start | bytes 7299072 | tf_op jit(solution)/shard_map/reduce_scatter | solution.py:265
  519.8 258.8 %reduce-scatter.13.cloned.1.call-start = ((), (), s32[]{:S(2)}) async-start(), calls=%async_computation.15 | async-start | bytes 9732096 | tf_op jit(solution)/shard_map/reduce_scatter | solution.py:268
  541.0 378.9 %reduce-scatter.11.cloned.1.call-start = ((), (), s32[]{:S(2)}) async-start(), calls=%async_computation.14 | async-start | bytes 9732096 | tf_op jit(solution)/shard_map/reduce_scatter | solution.py:267
  567.9 354.9 %copy-start.16 = (f32[512,768]{1,0:T(8,128)S(1)}, f32[512,768]{1,0:T(8,128)}, u32[]{:S(2)}) copy-start(f32[512,768]{1,0:T(8,128)} %copy-done.13) | copy-start | bytes 4718596
  567.9 354.9 %copy-start.71 = (f32[768]{0:T(1024)S(1)}, f32[768]{0:T(1024)}, u32[]{:S(2)}) copy-start(f32[768]{0:T(1024)} %get-tuple-element.404) | copy-start | bytes 9220
  922.8 53.8 %copy-start.21 = (f32[96,768]{1,0:T(8,128)S(1)}, f32[96,768]{1,0:T(8,128)}, u32[]{:S(2)}) copy-start(f32[96,768]{1,0:T(8,128)} %param.27) | copy-start | bytes 884740
  922.8 53.8 %copy-start.29 = (f32[96,768]{1,0:T(8,128)S(1)}, f32[96,768]{1,0:T(8,128)}, u32[]{:S(2)}) copy-start(f32[96,768]{1,0:T(8,128)} %reduce-scatter.11.cloned.1.call-done) | copy-start | bytes 884740
  932.1 100.9 %copy-start.46 = (f32[9216]{0:T(1024)S(1)}, f32[9216]{0:T(1024)}, u32[]{:S(2)}) copy-start(f32[9216]{0:T(1024)} %param.29) | copy-start | bytes 110596
  932.1 100.9 %copy-start.51 = (f32[9216]{0:T(1024)S(1)}, f32[9216]{0:T(1024)}, u32[]{:S(2)}) copy-start(f32[9216]{0:T(1024)} %param.39) | copy-start | bytes 110596
  972.8 60.2 %copy-start.52 = (f32[9216]{0:T(1024)S(1)}, f32[9216]{0:T(1024)}, u32[]{:S(2)}) copy-start(f32[9216]{0:T(1024)} %param.38) | copy-start | bytes 110596
  976.6 59.5 %copy-start.30 = (f32[24,3072]{1,0:T(8,128)}, f32[24,3072]{1,0:T(8,128)S(1)}, u32[]{:S(2)}) copy-start(f32[24,3072]{1,0:T(8,128)S(1)} %get-tuple-element.378) | copy-start | bytes 884740
  976.6 59.5 %copy-start.31 = (f32[24,3072]{1,0:T(8,128)}, f32[24,3072]{1,0:T(8,128)S(1)}, u32[]{:S(2)}) copy-start(f32[24,3072]{1,0:T(8,128)S(1)} %get-tuple-element.379) | copy-start | bytes 884740
  978.8 58.3 %copy-start.32 = (f32[96,768]{1,0:T(8,128)}, f32[96,768]{1,0:T(8,128)S(1)}, u32[]{:S(2)}) copy-start(f32[96,768]{1,0:T(8,128)S(1)} %get-tuple-element.376) | copy-start | bytes 884740
  978.8 58.3 %copy-start.33 = (f32[96,768]{1,0:T(8,128)}, f32[96,768]{1,0:T(8,128)S(1)}, u32[]{:S(2)}) copy-start(f32[96,768]{1,0:T(8,128)S(1)} %get-tuple-element.377) | copy-start | bytes 884740
  979.5 57.6 %copy-start.43 = (f32[24,768]{1,0:T(8,128)}, f32[24,768]{1,0:T(8,128)S(1)}, u32[]{:S(2)}) copy-start(f32[24,768]{1,0:T(8,128)S(1)} %get-tuple-element.374) | copy-start | bytes 221188
  979.5 57.6 %copy-start.44 = (f32[24,768]{1,0:T(8,128)}, f32[24,768]{1,0:T(8,128)S(1)}, u32[]{:S(2)}) copy-start(f32[24,768]{1,0:T(8,128)S(1)} %get-tuple-element.375) | copy-start | bytes 221188
  981.3 55.8 %copy-start.34 = (f32[72,768]{1,0:T(8,128)}, f32[72,768]{1,0:T(8,128)S(1)}, u32[]{:S(2)}) copy-start(f32[72,768]{1,0:T(8,128)S(1)} %get-tuple-element.372) | copy-start | bytes 663556
  981.3 55.8 %copy-start.35 = (f32[72,768]{1,0:T(8,128)}, f32[72,768]{1,0:T(8,128)S(1)}, u32[]{:S(2)}) copy-start(f32[72,768]{1,0:T(8,128)S(1)} %get-tuple-element.373) | copy-start | bytes 663556
  (106 other events, 1052.4 us)
Sparse Core Ops, SparseCore 0:
  11.5 62.8 all-gather.4
  77.9 54.2 all-gather.6
  135.7 62.6 all-gather.8
  201.7 62.9 all-gather.10
  293.3 99.2 reduce-scatter.8
  520.0 117.8 reduce-scatter.6
  643.7 134.8 reduce-scatter.12
  785.6 134.2 reduce-scatter.10

commit v2 on v1

v2 whole, which is shorter than its diff:
```python
from functools import partial
import jax
import jax.numpy as jnp
from jax import lax
from jax.experimental import pallas as pl
from jax.experimental.pallas import tpu as pltpu
from jax.sharding import PartitionSpec as P

D = 768
HD = 64
FF = 3072
STEP = 5
BLOCK = 256
LANES = 256
NT = (((1,), (1,)), ((), ()))
NN = (((1,), (0,)), ((), ()))
F32 = jnp.float32
BF16 = jnp.bfloat16


def mm(a, b, dims):
    return lax.dot_general(a, b, dims, preferred_element_type=F32)


def block_start(index, per_piece, me):
    piece = index // per_piece
    return pl.multiple_of(((piece ^ me) * per_piece + index % per_piece) * BLOCK, BLOCK)


def starts_of(scalars, docs, positions):
    first = jnp.zeros_like(positions)
    for doc in range(docs - 1):
        end = scalars[1 + doc]
        first = jnp.where(positions >= end, end, first)
    return first


def first_block(scalars, docs, index):
    position = index * BLOCK
    first = jnp.int32(0)
    for doc in range(docs - 1):
        end = scalars[1 + doc]
        first = jnp.where(position >= end, end, first)
    return first // BLOCK


def head_lanes(block, heads):
    lane = lax.broadcasted_iota(jnp.int32, block.shape, 1) // HD
    return [jnp.where(lane == j, block, jnp.zeros_like(block)) for j in range(heads)]


def allowed_mask(index, key_block, doc_first):
    query = index * BLOCK + lax.broadcasted_iota(jnp.int32, (1, BLOCK), 1)
    key = key_block * BLOCK + lax.broadcasted_iota(jnp.int32, (BLOCK, BLOCK), 0)
    return (key <= query) & (key >= doc_first)


def forward_body(heads, docs, per_piece, blocks, scalars, qkv, keep_out, send_out, log_out, values_t, out_t):
    me = scalars[0]
    width = heads * HD

    def transpose_values(i, carry):
        v = qkv[pl.ds(block_start(i, per_piece, me), BLOCK), 2 * LANES : 3 * LANES]
        values_t[:, pl.ds(pl.multiple_of(i * BLOCK, BLOCK), BLOCK)] = v.T[:width]
        return carry

    lax.fori_loop(0, blocks, transpose_values, 0)

    def query_block(i, carry):
        row = block_start(i, per_piece, me)
        q = qkv[pl.ds(row, BLOCK), 0:LANES] * BF16(HD ** -0.5)
        q_heads = head_lanes(q, heads)
        positions = i * BLOCK + lax.broadcasted_iota(jnp.int32, (1, BLOCK), 1)
        doc_first = starts_of(scalars, docs, positions)

        def key_step(kb, state):
            allowed = allowed_mask(i, kb, doc_first)
            k = qkv[pl.ds(block_start(kb, per_piece, me), BLOCK), LANES : 2 * LANES]
            column = pl.ds(pl.multiple_of(kb * BLOCK, BLOCK), BLOCK)
            new = []
            for j in range(heads):
                top, total, acc = state[j]
                s = jnp.where(allowed, mm(k, q_heads[j], NT), -1e30)
                top_new = jnp.maximum(top, jnp.max(s, axis=0, keepdims=True))
                p = jnp.exp(s - top_new)
                fade = jnp.exp(top - top_new)
                total = total * fade + jnp.sum(p, axis=0, keepdims=True)
                v_t = values_t[j * HD : (j + 1) * HD, column]
                acc = acc * fade + mm(v_t, p.astype(BF16), NN)
                new.append((top_new, total, acc))
            return tuple(new)

        init = tuple(
            (jnp.full((1, BLOCK), -1e30, F32), jnp.zeros((1, BLOCK), F32), jnp.zeros((HD, BLOCK), F32))
            for _ in range(heads)
        )
        state = key_step(i, init)
        state = lax.fori_loop(first_block(scalars, docs, i), i, key_step, state)
        column = pl.ds(row, BLOCK)
        for j in range(heads):
            top, total, acc = state[j]
            out_t[j * HD : (j + 1) * HD, column] = (acc / total).astype(BF16)
            log_out[j : j + 1, pl.ds(pl.multiple_of(i * BLOCK, BLOCK), BLOCK)] = top + jnp.log(total)
        return carry

    lax.fori_loop(0, blocks, query_block, 0)
    half = out_t.shape[1] // 2
    keep_out[...] = out_t[:, :half]
    send_out[...] = out_t[:, half:]


def attention_forward(scalars, qkv, heads, docs, piece_rows):
    rows = qkv.shape[0]
    width = heads * HD
    vmem = pl.BlockSpec(memory_space=pltpu.VMEM)
    return pl.pallas_call(
        partial(forward_body, heads, docs, piece_rows // BLOCK, rows // BLOCK),
        out_shape=(
            jax.ShapeDtypeStruct((width, rows // 2), BF16),
            jax.ShapeDtypeStruct((width, rows // 2), BF16),
            jax.ShapeDtypeStruct((8, rows), F32),
        ),
        in_specs=[pl.BlockSpec(memory_space=pltpu.SMEM), vmem],
        out_specs=(vmem, vmem, vmem),
        scratch_shapes=[pltpu.VMEM((width, rows), BF16), pltpu.VMEM((width, rows), BF16)],
        compiler_params=pltpu.CompilerParams(vmem_limit_bytes=40 * 2**20),
        cost_estimate=pl.CostEstimate(flops=4 * rows * rows * width, bytes_accessed=8 * rows * width, transcendentals=rows * rows),
        name="attention_forward",
    )(scalars, qkv)


def backward_body(
    heads, docs, per_piece, blocks, scalars, qkv, out_keep, out_send, grad_keep, grad_recv, logs, d_qkv,
    keys_t, out_t, grad_t, d_keys, d_values
):
    me = scalars[0]
    width = heads * HD
    scale = HD ** -0.5
    half = out_keep.shape[1]
    out_t[:, :half] = out_keep[...]
    out_t[:, half:] = out_send[...]
    grad_t[:, :half] = grad_keep[...]
    grad_t[:, half:] = grad_recv[...]
    d_keys[...] = jnp.zeros_like(d_keys)
    d_values[...] = jnp.zeros_like(d_values)

    def transpose_keys(i, carry):
        k = qkv[pl.ds(block_start(i, per_piece, me), BLOCK), LANES : 2 * LANES]
        keys_t[:, pl.ds(pl.multiple_of(i * BLOCK, BLOCK), BLOCK)] = k.T[:width]
        return carry

    lax.fori_loop(0, blocks, transpose_keys, 0)

    def query_block(i, carry):
        row = block_start(i, per_piece, me)
        q_heads = head_lanes(qkv[pl.ds(row, BLOCK), 0:LANES] * BF16(scale), heads)
        o_t = out_t[:, pl.ds(row, BLOCK)]
        g_t = grad_t[:, pl.ds(row, BLOCK)]
        product = o_t.astype(F32) * g_t.astype(F32)
        deltas = [jnp.sum(product[j * HD : (j + 1) * HD], axis=0, keepdims=True) for j in range(heads)]
        padded = jnp.concatenate([g_t, jnp.zeros((LANES - width, BLOCK), BF16)], axis=0)
        g_heads = head_lanes(padded.T, heads)
        natural = pl.ds(pl.multiple_of(i * BLOCK, BLOCK), BLOCK)
        log_rows = [logs[j : j + 1, natural] for j in range(heads)]
        positions = i * BLOCK + lax.broadcasted_iota(jnp.int32, (1, BLOCK), 1)
        doc_first = starts_of(scalars, docs, positions)

        def key_step(kb, d_q):
            allowed = allowed_mask(i, kb, doc_first)
            key_row = pl.ds(block_start(kb, per_piece, me), BLOCK)
            k = qkv[key_row, LANES : 2 * LANES]
            v = qkv[key_row, 2 * LANES : 3 * LANES]
            column = pl.ds(pl.multiple_of(kb * BLOCK, BLOCK), BLOCK)
            d_k = d_keys[key_row, :]
            d_v = d_values[key_row, :]
            new = []
            for j in range(heads):
                s = jnp.where(allowed, mm(k, q_heads[j], NT), -1e30)
                p = jnp.exp(s - log_rows[j])
                d_v = d_v + mm(p.astype(BF16), g_heads[j], NN)
                d_p = mm(v, g_heads[j], NT)
                d_s = (p * (d_p - deltas[j])).astype(BF16)
                d_k = d_k + mm(d_s, q_heads[j], NN)
                new.append(d_q[j] + mm(keys_t[j * HD : (j + 1) * HD, column], d_s, NN))
            d_keys[key_row, :] = d_k
            d_values[key_row, :] = d_v
            return tuple(new)

        d_q = key_step(i, tuple(jnp.zeros((HD, BLOCK), F32) for _ in range(heads)))
        d_q = lax.fori_loop(first_block(scalars, docs, i), i, key_step, d_q)
        stacked = jnp.concatenate([*d_q, jnp.zeros((LANES - width, BLOCK), F32)], axis=0) * scale
        d_qkv[pl.ds(row, BLOCK), 0:LANES] = stacked.T.astype(BF16)
        return carry

    lax.fori_loop(0, blocks, query_block, 0)
    d_qkv[:, LANES : 2 * LANES] = d_keys[...].astype(BF16)
    d_qkv[:, 2 * LANES : 3 * LANES] = d_values[...].astype(BF16)


def attention_backward(scalars, qkv, out_keep, out_send, grad_keep, grad_recv, logs, heads, docs, piece_rows):
    rows = qkv.shape[0]
    width = heads * HD
    vmem = pl.BlockSpec(memory_space=pltpu.VMEM)
    return pl.pallas_call(
        partial(backward_body, heads, docs, piece_rows // BLOCK, rows // BLOCK),
        out_shape=jax.ShapeDtypeStruct((rows, 3 * LANES), BF16),
        in_specs=[pl.BlockSpec(memory_space=pltpu.SMEM)] + [vmem] * 6,
        out_specs=vmem,
        scratch_shapes=[pltpu.VMEM((width, rows), BF16)] * 3 + [pltpu.VMEM((rows, LANES), F32)] * 2,
        compiler_params=pltpu.CompilerParams(vmem_limit_bytes=48 * 2**20),
        cost_estimate=pl.CostEstimate(flops=10 * rows * rows * width, bytes_accessed=16 * rows * width, transcendentals=rows * rows),
        name="attention_backward",
    )(scalars, qkv, out_keep, out_send, grad_keep, grad_recv, logs)


NORM_EPS = 1e-05
ADAM_EPS = 1e-06
DECAY_RATE = 0.01
MATRIX_RATE = 0.5
VECTOR_RATE = 0.1
ROOT_TWO_OVER_PI = (2.0 / 3.141592653589793) ** 0.5
BOTH = ("batch", "head")
PARTNER = 1
ACROSS = 2


def layer_norm_parts(values):
    row_mean = jnp.mean(values, axis=-1, keepdims=True)
    centered = values - row_mean
    variance = jnp.mean(centered * centered, axis=-1, keepdims=True)
    inverse = lax.rsqrt(variance + NORM_EPS)
    return centered * inverse, inverse


def layer_norm_backward(upstream, normalized, inverse, gain):
    scaled = upstream * gain
    first = jnp.mean(scaled, axis=-1, keepdims=True)
    second = jnp.mean(scaled * normalized, axis=-1, keepdims=True)
    return inverse * (scaled - first - normalized * second)


def unpack_vector(params):
    pieces = [params[position * D : (position + 1) * D] for position in range(8)]
    return pieces + [params[8 * D : 8 * D + FF]]


def dot(a, b, dims):
    return lax.dot_general(a, b, (dims, ((), ())), preferred_element_type=F32)


def swap(values, axis, mask):
    size = lax.axis_size(axis)
    return lax.ppermute(values, axis, [(place, place ^ mask) for place in range(size)])


def bit_of(axis, mask):
    return (lax.axis_index(axis) & mask) != 0


def gather_step(values, axis, mask, position):
    other = swap(values, axis, mask)
    high = bit_of(axis, mask)
    return jnp.stack(
        [jnp.where(high, other, values), jnp.where(high, values, other)], axis=position
    )


def scatter_step(values, axis, mask, position):
    high = bit_of(axis, mask).astype(jnp.int32)
    kept = lax.dynamic_index_in_dim(values, high, position, keepdims=False)
    sent = lax.dynamic_index_in_dim(values, 1 - high, position, keepdims=False)
    arrived = swap(sent.astype(BF16), axis, mask)
    return kept.astype(F32) + arrived.astype(F32)


def all_sum(values):
    for axis in ("head", "batch"):
        mask = 1
        while mask < lax.axis_size(axis):
            values = values + swap(values, axis, mask)
            mask *= 2
    return values


def batch_masks():
    return [1 << bit for bit in range((lax.axis_size("batch") - 1).bit_length())]


def gather_chips(values, across_last):
    masks = batch_masks()[::-1]
    early, late = masks[:-1], masks[-1]
    position = 0
    for mask in early:
        values = gather_step(values, "batch", mask, position)
        position += 1
    if across_last:
        values = gather_step(values, "batch", late, position)
        values = gather_step(values, "head", ACROSS, position + 1)
    else:
        values = gather_step(values, "head", ACROSS, position)
        values = gather_step(values, "batch", late, position)
    return values.reshape((-1,) + values.shape[position + 2 :])


def scatter_chips(values, across_first):
    masks = batch_masks()
    shape = values.shape[1:]
    values = values.reshape((2,) * (len(masks) + 1) + shape)
    position = len(masks)
    if across_first:
        values = scatter_step(values, "head", ACROSS, position)
        values = scatter_step(values, "batch", masks[0], position - 1)
    else:
        values = scatter_step(values, "batch", masks[0], position - 1)
        values = scatter_step(values, "head", ACROSS, position - 1)
    for step, mask in enumerate(masks[1:]):
        values = scatter_step(values, "batch", mask, position - 2 - step)
    return values


def gather_batch(values, position):
    for mask in batch_masks()[::-1]:
        values = gather_step(values, "batch", mask, position)
        position += 1
    return values


def scatter_batch(values, position):
    masks = batch_masks()
    shape = values.shape
    values = values.reshape(
        shape[:position] + (2,) * len(masks) + shape[position + 1 :]
    )
    for step, mask in enumerate(masks):
        values = scatter_step(values, "batch", mask, position + len(masks) - 1 - step)
    return values


def block_permutation(slot, to_owner):
    rows, heads = lax.axis_size("batch"), lax.axis_size("head")
    total = rows * heads
    pairs = []
    for owner in range(total):
        place = (3 * owner + slot) % total
        holder = (place % rows) * heads + place // rows
        pairs.append((holder, owner) if to_owner else (owner, holder))
    return pairs


def holder_place():
    return lax.axis_size("batch") * lax.axis_index("head") + lax.axis_index("batch")


def blocks_to_holders(shard):
    total = lax.axis_size("batch") * lax.axis_size("head")
    blocks = shard.reshape(3, -1, D)
    arrived = jnp.stack(
        [lax.ppermute(blocks[slot], BOTH, block_permutation(slot, False)) for slot in range(3)]
    )
    place = holder_place()
    return jnp.stack(
        [
            lax.dynamic_index_in_dim(arrived, (total * kind + place) % 3, 0, keepdims=False)
            for kind in range(3)
        ]
    )


def blocks_to_owners(blocks):
    total = lax.axis_size("batch") * lax.axis_size("head")
    place = holder_place()
    arrived = []
    for slot in range(3):
        kind = ((slot + 3 * total - place) * total) % 3
        sent = lax.dynamic_index_in_dim(blocks, kind, 0, keepdims=False)
        arrived.append(lax.ppermute(sent, BOTH, block_permutation(slot, True)))
    return jnp.concatenate(arrived, axis=0)


def adam_direction(gradient, first_old, second_old, master, clip_factor):
    clipped = gradient * clip_factor
    first_new = 0.5 * first_old + 0.5 * clipped
    second_new = 0.5 * second_old + 0.5 * clipped * clipped
    correction = 1.0 - 0.5**STEP
    direction = (
        first_new / correction / (jnp.sqrt(second_new / correction) + ADAM_EPS)
        + DECAY_RATE * master
    )
    return (first_new, second_new, direction)


def on_device(
    tokens,
    cotangent,
    lengths,
    input_weight,
    output_weight,
    expand_weight,
    contract_weight,
    vector_params,
    input_first,
    input_second,
    output_first,
    output_second,
    expand_first,
    expand_second,
    contract_first,
    contract_second,
    vector_first,
    vector_second,
):
    rows_of_devices = lax.axis_size("batch")
    head_count = lax.axis_size("head")
    chips = rows_of_devices * head_count // 2
    here = lax.axis_index("head")
    core = here % 2
    side = here // 2
    width = D // head_count
    heads = width // HD
    piece = tokens.shape[0]
    docs = lengths.shape[1]
    hidden_block = FF // (2 * chips)
    half = FF // 2
    (
        gain_one,
        bias_one,
        gain_two,
        bias_two,
        bias_query,
        bias_value,
        bias_output,
        bias_contract,
        bias_expand,
    ) = unpack_vector(vector_params)

    ends = [jnp.sum(lengths[0, : doc + 1]) for doc in range(docs)]
    scalars = jnp.stack([here, *ends]).astype(jnp.int32)

    resid_in = tokens.astype(F32)
    unit_one, inverse_one = layer_norm_parts(resid_in)
    normed_own = (unit_one * gain_one + bias_one).astype(BF16)
    normed_across = swap(normed_own, "head", ACROSS)
    normed_partner = swap(normed_own, "head", PARTNER)
    normed_both = swap(normed_across, "head", PARTNER)
    normed_one = jnp.concatenate([normed_own, normed_partner, normed_across, normed_both])

    kinds = gather_batch(blocks_to_holders(input_weight.astype(BF16)), 1).reshape(3, width, D)
    weight_in = jnp.pad(kinds, ((0, 0), (0, LANES - width), (0, 0))).reshape(3 * LANES, D)

    def of_heads(vector):
        return jnp.pad(lax.dynamic_slice_in_dim(vector, here * width, width), (0, LANES - width))

    bias_in = jnp.concatenate([of_heads(bias_query), jnp.zeros(LANES, F32), of_heads(bias_value)])
    projected = (dot(normed_one, weight_in, ((1,), (1,))) + bias_in).astype(BF16)

    def split_columns(shard, parts):
        return shard.reshape(shard.shape[0], parts, 2, -1)

    def exchange_columns(shard, parts):
        cut = split_columns(shard, parts)
        mine = lax.dynamic_index_in_dim(cut, core, 2, keepdims=False)
        other = swap(lax.dynamic_index_in_dim(cut, 1 - core, 2, keepdims=False), "head", PARTNER)
        high = core == 1
        return jnp.stack([jnp.where(high, other, mine), jnp.where(high, mine, other)])

    out_rows = output_weight.shape[0]
    output_shard = exchange_columns(output_weight.astype(BF16), 2).reshape(2 * out_rows, 2, width)
    output_half = gather_chips(output_shard.transpose(1, 0, 2), True)
    output_half = output_half.transpose(1, 0, 2, 3).reshape(2, D, width)
    output_own = lax.dynamic_index_in_dim(output_half, side, 0, keepdims=False)
    output_across = lax.dynamic_index_in_dim(output_half, 1 - side, 0, keepdims=False)
    expand_half = gather_chips(expand_weight.astype(BF16), True).reshape(half, D)
    contract_shard = exchange_columns(contract_weight.astype(BF16), chips).reshape(2 * out_rows, half)
    contract_half = gather_chips(contract_shard, False).reshape(D, half)
    bias_half = lax.dynamic_index_in_dim(
        bias_expand.reshape(chips, 2, hidden_block), core, 1, keepdims=False
    ).reshape(half)
    upstream_pair = jnp.concatenate([cotangent, swap(cotangent, "head", PARTNER)])

    keep_t, send_t, logs = attention_forward(scalars, projected, heads, docs, piece)
    across_t = swap(send_t, "head", ACROSS)
    branch_pair = dot(keep_t, output_own, ((0,), (1,))) + dot(across_t, output_across, ((0,), (1,)))
    branch = branch_pair[:piece] + swap(branch_pair[piece:], "head", PARTNER) + bias_output
    resid_mid = resid_in + branch
    unit_two, inverse_two = layer_norm_parts(resid_mid)
    normed_two_own = (unit_two * gain_two + bias_two).astype(BF16)
    normed_two = jnp.concatenate([normed_two_own, swap(normed_two_own, "head", PARTNER)])

    expanded = dot(normed_two, expand_half, ((1,), (1,))) + bias_half
    squared = expanded * expanded
    bent = jnp.tanh(ROOT_TWO_OVER_PI * (expanded + 0.044715 * expanded * squared))
    activated = (0.5 * expanded * (1.0 + bent)).astype(BF16)
    slope = 0.5 * (1.0 + bent) + 0.5 * expanded * (1.0 - bent * bent) * ROOT_TWO_OVER_PI * (
        1.0 + 3.0 * 0.044715 * squared
    )
    grad_expanded_wide = dot(upstream_pair, contract_half, ((1,), (0,))) * slope
    grad_expanded = grad_expanded_wide.astype(BF16)
    contract_pair = dot(activated, contract_half, ((1,), (1,)))
    block_out = (
        resid_mid + contract_pair[:piece] + swap(contract_pair[piece:], "head", PARTNER) + bias_contract
    ).astype(BF16)
    grad_normed_pair = dot(grad_expanded, expand_half, ((1,), (0,)))
    grad_normed_two = grad_normed_pair[:piece] + swap(grad_normed_pair[piece:], "head", PARTNER)
    upstream = cotangent.astype(F32)
    grad_mid = upstream + layer_norm_backward(grad_normed_two, unit_two, inverse_two, gain_two)
    grad_gain_two = jnp.sum(grad_normed_two * unit_two, axis=0)
    grad_bias_two = jnp.sum(grad_normed_two, axis=0)
    grad_branch = grad_mid.astype(BF16)
    grad_branch_pair = jnp.concatenate([grad_branch, swap(grad_branch, "head", PARTNER)])

    grad_across_t = dot(output_across, grad_branch_pair, ((0,), (1,))).astype(BF16)
    grad_arrived_t = swap(grad_across_t, "head", ACROSS)
    grad_keep_t = dot(output_own, grad_branch_pair, ((0,), (1,))).astype(BF16)
    grad_projected = attention_backward(
        scalars, projected, keep_t, send_t, grad_keep_t, grad_arrived_t, logs, heads, docs, piece
    )

    expand_sum = dot(grad_expanded, normed_two, ((0,), (0,))).reshape(chips, hidden_block, D)
    expand_grad = scatter_chips(expand_sum, False)
    contract_sum = dot(upstream_pair, activated, ((0,), (0,))).reshape(chips, 2 * out_rows, half)
    contract_mixed = scatter_chips(contract_sum, True)
    own_columns = dot(grad_branch_pair, keep_t, ((0,), (1,)))
    across_columns = dot(grad_branch_pair, across_t, ((0,), (1,)))
    output_sum = jnp.stack(
        [
            jnp.where(side == 1, across_columns, own_columns),
            jnp.where(side == 1, own_columns, across_columns),
        ]
    ).reshape(2, chips, 2 * out_rows, width)
    output_mixed = scatter_chips(output_sum.transpose(1, 0, 2, 3), True)
    output_mixed = output_mixed.transpose(1, 0, 2)

    def return_columns(mixed, parts):
        cut = mixed.reshape(2, out_rows, parts, -1)
        mine = lax.dynamic_index_in_dim(cut, core, 0, keepdims=False)
        other = swap(lax.dynamic_index_in_dim(cut, 1 - core, 0, keepdims=False), "head", PARTNER)
        high = core == 1
        return jnp.stack(
            [jnp.where(high, other, mine), jnp.where(high, mine, other)], axis=2
        ).reshape(out_rows, -1)

    contract_grad = return_columns(contract_mixed, chips)
    output_grad = return_columns(output_mixed, 2)

    grad_normed_all = dot(grad_projected, weight_in, ((1,), (0,))).reshape(4, piece, D)
    reduced_across = grad_normed_all[2] + swap(grad_normed_all[3].astype(BF16), "head", PARTNER).astype(F32)
    arrived_across = swap(reduced_across.astype(BF16), "head", ACROSS)
    grad_normed_one = (
        grad_normed_all[0]
        + swap(grad_normed_all[1].astype(BF16), "head", PARTNER).astype(F32)
        + arrived_across.astype(F32)
    )
    grad_in_sum = dot(grad_projected, normed_one, ((0,), (0,))).reshape(3, LANES, D)[:, :width]
    grad_in_blocks = scatter_batch(grad_in_sum.reshape(3, rows_of_devices, -1, D), 1)
    input_piece_grad = blocks_to_owners(grad_in_blocks)
    input_grad = (grad_mid + layer_norm_backward(grad_normed_one, unit_one, inverse_one, gain_one)).astype(BF16)

    projected_sums = jnp.sum(grad_projected.astype(F32), axis=0).reshape(3, LANES)[:, :width]

    def place_heads(vector):
        return lax.dynamic_update_slice_in_dim(jnp.zeros(D, F32), vector, here * width, 0)

    hidden_sums = jnp.sum(grad_expanded.astype(F32), axis=0).reshape(chips, 1, hidden_block)
    hidden_sums = lax.dynamic_update_slice_in_dim(
        jnp.zeros((chips, 2, hidden_block), F32), hidden_sums, core, 1
    ).reshape(FF)
    masters = (input_weight, output_weight, expand_weight, contract_weight)
    firsts = (input_first, output_first, expand_first, contract_first)
    seconds = (input_second, output_second, expand_second, contract_second)
    shard_grads = (input_piece_grad, output_grad, expand_grad, contract_grad)
    local_sq = jnp.sum(grad_in_blocks * grad_in_blocks) + sum(
        jnp.sum(piece_grad * piece_grad) for piece_grad in shard_grads[1:]
    )
    weight_sq = [jnp.sum(master * master) for master in masters]
    scalars_sq = jnp.pad(jnp.stack([local_sq, *weight_sq]), (0, 1024 - 5))
    local = jnp.concatenate(
        [
            jnp.sum(grad_normed_one * unit_one, axis=0),
            jnp.sum(grad_normed_one, axis=0),
            grad_gain_two,
            grad_bias_two,
            place_heads(projected_sums[0]),
            place_heads(projected_sums[2]),
            jnp.sum(grad_branch.astype(F32), axis=0),
            jnp.sum(upstream, axis=0),
            hidden_sums,
            scalars_sq,
        ]
    ).reshape(-1, 128)
    summed = all_sum(local).reshape(-1)
    vector_grads = summed[: 8 * D + FF]
    grad_norm = jnp.sqrt(summed[8 * D + FF] + jnp.sum(vector_grads * vector_grads))
    weight_norms = jnp.sqrt(summed[8 * D + FF + 1 : 8 * D + FF + 5])
    clip_factor = jnp.minimum(1.0, 1.0 / grad_norm)
    updated = [
        adam_direction(piece_grad, first_old, second_old, master, clip_factor)
        for piece_grad, first_old, second_old, master in zip(shard_grads, firsts, seconds, masters)
    ]
    update_sq = jnp.stack([jnp.sum(entry[2] * entry[2]) for entry in updated])
    update_norms = jnp.sqrt(all_sum(jnp.pad(update_sq, (0, 1020)).reshape(8, 128))[0, :4])
    matrix_norms = jnp.concatenate([weight_norms, update_norms])
    results = []
    for position in range(4):
        first_new, second_new, direction = updated[position]
        new_master = (
            masters[position]
            - MATRIX_RATE * (weight_norms[position] / update_norms[position]) * direction
        )
        results += [first_new, second_new, new_master, new_master.astype(BF16)]
    vector_first_new, vector_second_new, vector_direction = adam_direction(
        vector_grads, vector_first, vector_second, vector_params, clip_factor
    )
    vector_new = vector_params - VECTOR_RATE * vector_direction
    return (
        block_out,
        input_grad,
        grad_norm,
        matrix_norms,
        *results,
        vector_first_new,
        vector_second_new,
        vector_new,
    )


def solution(mesh):
    split = P(BOTH, None)
    return jax.shard_map(
        on_device,
        mesh=mesh,
        in_specs=(split, split, P("batch", None)) + (split,) * 4 + (P(),) + (split,) * 8 + (P(), P()),
        out_specs=(split, split, P(), P()) + (split,) * 16 + (P(), P(), P()),
        check_vma=False,
    )
```

time: 1050 us -> 466 us (0.44)
  waiting for transfers between devices: 472 us -> 170 us
  matrix products: 220 us -> 48.2 us
  blocking collectives: 134 us -> 0 us
  starting transfers between devices: 12.3 us -> 73.4 us
  Pallas kernels: 0 us -> 42.9 us
  other arithmetic: 110 us -> 68 us
  local copies, waits for them, and re-layouts: 64.5 us -> 43.1 us
  between operations: 25.8 us -> 13.1 us
    reduce_scatter x4 -> x0, waiting for transfers between devices: 345 us -> none  [the longest x1 139 us: on_device(): lax.psum_scatter(grad_expand, ('batch', 'head'), scatter_dimension=0, til...]
    dot_general x40 -> x15, matrix products: 220 us -> 48.2 us  [dot(): return lax.dot_general(a, b, (dims, ((), ())), preferred_element_type=F32)]
    ppermute x0 -> x64, waiting for transfers between devices: none -> 170 us  [the longest x58 170 us: swap(): lax.ppermute(values, axis, [(place, place ^ mask) for place in range(size)])]
    psum x2 -> x0, blocking collectives: 79.9 us -> none  [the longest x1 40.7 us: on_device(): grad_total = lax.psum(local_grad_sq, ('batch', 'head'))]
    ppermute x0 -> x64, starting transfers between devices: none -> 73.4 us  [the longest x58 59.9 us: swap(): lax.ppermute(values, axis, [(place, place ^ mask) for place in range(size)])]
    all_gather x4 -> x0, waiting for transfers between devices: 70.5 us -> none  [the longest x1 57.2 us: on_device(): lax.all_gather(input_weight.astype(jnp.bfloat16), ('batch', 'head'), axis...]
    all_to_all x3 -> x0, waiting for transfers between devices: 56.2 us -> none  [the longest x1 35.8 us: on_device(): lax.all_to_all(projected, 'head', split_axis=2, concat_axis=1, tiled=True)]
    all_to_all x1 -> x0, blocking collectives: 53.8 us -> none  [on_device(): lax.all_to_all(grad_projected_heads, 'head', split_axis=1, concat_axis=2,...]
  transfers between devices with their start and end apart: 11 -> 64, of which waited for: 8 -> 35; matrix products, arithmetic and copies ran while one was open for 32% -> 24% of each run, Pallas kernels for 0% -> 9%
where the time goes in v2:
time: 466 us; the launch traced here: 459 us
  waiting for transfers between devices  170 us (36%)
  starting transfers between devices  73.4 us (16%)
  other arithmetic  68 us (15%)
  matrix products  48.2 us (10%)
  local copies, waits for them, and re-layouts  43.1 us (9%)
  Pallas kernels  42.9 us (9%)
  between operations  13.1 us (3%)
    ppermute x58, waiting for transfers between devices, swap(): lax.ppermute(values, axis, [(place, place ^ mask) for place in range(size)])  170 us
    ppermute x58, starting transfers between devices, swap(): lax.ppermute(values, axis, [(place, place ^ mask) for place in range(size)])  59.9 us
    dot_general x15, matrix products, dot(): return lax.dot_general(a, b, (dims, ((), ())), preferred_element_type=F32)  48.2 us
    pallas_call x1, Pallas kernels, attention_backward(): pl.pallas_call(partial(backward_body, heads, docs, piece_rows // BLOCK, r...  28.8 us
    pallas_call x1, Pallas kernels, attention_forward(): pl.pallas_call(partial(forward_body, heads, docs, piece_rows // BLOCK, ro...  14 us
  transfers between devices with their start and end apart: 64, of which 35 were waited for; matrix products, arithmetic and copies ran while one was open for 24% of the time, Pallas kernels for 9%

profile of v2, /device:TPU:0, one launch (start us, length us, event | category | flops | bytes accessed | tf_op | source)
XLA Modules:
  0.0 459.2 jit_solution(12417802822847260061)
XLA Ops:
  23.7 5.0 %collective-permute-start.17 = (bf16[96,768]{1,0:T(8,128)(2,1)S(1)}, bf16[96,768]{1,0:T(8,128)(2,1)S(1)}, u32[]{:S(2)}, u32[]{:S(2)}) collective-permute-start(bf16[96,768]{1,0:T(8,128)(2,1)S(1)} %get-tuple-element.100), channel_id=1, source_target_pairs={{0,16},{4,20},{8,24},{12,28},{16,0},{20,4},{24,8},{28,12},{1,17},{... | collective-permute-start | bytes 442376 | tf_op jit(solution)/shard_map/ppermute | solution.py:253
  31.2 7.6 %collective-permute-done.10 = bf16[2,48,192]{2,1,0:T(8,128)(2,1)S(1)} collective-permute-done((bf16[2,48,192]{2,1,0:T(8,128)(2,1)S(1)}, bf16[2,48,192]{2,1,0:T(8,128)(2,1)S(1)}, u32[]{:S(2)}, u32[]{:S(2)}) %collective-permute-start.10) | collective-permute-done | bytes 36896 | tf_op jit(solution)/shard_map/ppermute | solution.py:253
  45.2 7.6 %collective-permute-done.6 = bf16[3,24,768]{2,1,0:T(8,128)(2,1)S(1)} collective-permute-done((bf16[3,24,768]{2,1,0:T(8,128)(2,1)S(1)}, bf16[3,24,768]{2,1,0:T(8,128)(2,1)S(1)}, u32[]{:S(2)}, u32[]{:S(2)}) %collective-permute-start.6) | collective-permute-done | bytes 110624 | tf_op jit(solution)/shard_map/ppermute | solution.py:253
  54.4 5.6 %collective-permute-done.22 = bf16[48,1536]{1,0:T(8,128)(2,1)S(1)} collective-permute-done((bf16[48,1536]{1,0:T(8,128)(2,1)S(1)}, bf16[48,1536]{1,0:T(8,128)(2,1)S(1)}, u32[]{:S(2)}, u32[]{:S(2)}) %collective-permute-start.22) | collective-permute-done | bytes 147488 | tf_op jit(solution)/shard_map/ppermute | solution.py:253
  62.3 6.1 %collective-permute-done.7 = bf16[3,2,24,768]{3,2,1,0:T(8,128)(2,1)S(1)} collective-permute-done((bf16[3,2,24,768]{3,2,1,0:T(8,128)(2,1)S(1)}, bf16[3,2,24,768]{3,2,1,0:T(8,128)(2,1)S(1)}, u32[]{:S(2)}, u32[]{:S(2)}) %collective-permute-start.7) | collective-permute-done | bytes 221216 | tf_op jit(solution)/shard_map/ppermute | solution.py:253
  68.5 6.2 %collective-permute-done.18 = bf16[2,96,768]{2,1,0:T(8,128)(2,1)S(1)} collective-permute-done((bf16[2,96,768]{2,1,0:T(8,128)(2,1)S(1)}, bf16[2,96,768]{2,1,0:T(8,128)(2,1)S(1)}, u32[]{:S(2)}, u32[]{:S(2)}) %collective-permute-start.18) | collective-permute-done | bytes 294944 | tf_op jit(solution)/shard_map/ppermute | solution.py:253
  78.9 4.0 collective-permute-start.8
  87.2 6.7 %collective-permute-done.8 = bf16[3,2,2,24,768]{4,3,2,1,0:T(8,128)(2,1)S(1)} collective-permute-done((bf16[3,2,2,24,768]{4,3,2,1,0:T(8,128)(2,1)S(1)}, bf16[3,2,2,24,768]{4,3,2,1,0:T(8,128)(2,1)S(1)}, u32[]{:S(2)}, u32[]{:S(2)}) %collective-permute-start.8) | collective-permute-done | bytes 442400 | tf_op jit(solution)/shard_map/ppermute | solution.py:253
  94.2 10.7 %collective-permute-done.19 = bf16[2,2,96,768]{3,2,1,0:T(8,128)(2,1)S(1)} collective-permute-done((bf16[2,2,96,768]{3,2,1,0:T(8,128)(2,1)S(1)}, bf16[2,2,96,768]{3,2,1,0:T(8,128)(2,1)S(1)}, u32[]{:S(2)}, u32[]{:S(2)}) %collective-permute-start.19) | collective-permute-done | bytes 589856 | tf_op jit(solution)/shard_map/ppermute | solution.py:253
  106.0 4.3 add_convert_fusion.qkv
  110.3 14.0 %attention_forward.1 = (bf16[192,1024]{1,0:T(8,128)(2,1)S(1)}, bf16[192,1024]{1,0:T(8,128)(2,1)S(1)}, f32[8,2048]{1,0:T(8,128)S(1)}) custom-call(s32[4]{0:T(128)S(1)} %pad_add_fusion.scalars, bf16[2048,768]{1,0:T(8,128)(2,1)S(1)} %add_convert_fusion.qkv), custom_call_target="tpu_custom_call" | custom-call | flops 3221225472 | bytes 3145728 | tf_op jit(solution)/shard_map/attention_forward/pallas_call | solution.py:116
  128.3 8.2 %collective-permute-done.14 = bf16[192,1024]{1,0:T(8,128)(2,1)S(1)} collective-permute-done((bf16[192,1024]{1,0:T(8,128)(2,1)S(1)}, bf16[192,1024]{1,0:T(8,128)(2,1)S(1)}, u32[]{:S(2)}, u32[]{:S(2)}) %collective-permute-start.14) | collective-permute-done | bytes 393248 | tf_op jit(solution)/shard_map/ppermute | solution.py:253
  142.2 4.3 collective-permute-start.25
  146.4 13.0 %collective-permute-done.20 = bf16[2,2,2,96,768]{4,3,2,1,0:T(8,128)(2,1)} collective-permute-done((bf16[2,2,2,96,768]{4,3,2,1,0:T(8,128)(2,1)}, bf16[2,2,2,96,768]{4,3,2,1,0:T(8,128)(2,1)}, u32[]{:S(2)}, u32[]{:S(2)}) %collective-permute-start.20) | collective-permute-done | bytes 1179680 | tf_op jit(solution)/shard_map/ppermute | solution.py:253
  166.1 7.0 %collective-permute-done.25 = bf16[2,2,2,48,1536]{4,3,2,1,0:T(8,128)(2,1)S(1)} collective-permute-done((bf16[2,2,2,48,1536]{4,3,2,1,0:T(8,128)(2,1)S(1)}, bf16[2,2,2,48,1536]{4,3,2,1,0:T(8,128)(2,1)S(1)}, u32[]{:S(2)}, u32[]{:S(2)}) %collective-permute-start.25) | collective-permute-done | bytes 1179680 | tf_op jit(solution)/shard_map/ppermute | solution.py:253
  173.5 3.7 multiply_convert_fusion.1
  177.2 6.1 %convert_reduce_fusion = (f32[1536]{0:T(1024)S(1)}, bf16[1024,1536]{1,0:T(8,128)(2,1)S(1)}) fusion(f32[1024,1536]{1,0:T(8,128)S(1)} %get-tuple-element.155, f32[1536]{0:T(1024)S(1)} %add.460, bf16[1024,768]{1,0:T(8,128)(2,1)S(1)} %constant_dynamic-update-slice_fusion, bf16[768,1536]{1,0:T(8,128)(2,1)S(1)} %bitcast.324), kind=kOutput, calls=%fused_computation | convolution fusion | flops 2448947712 | bytes 13381632 | tf_op jit(solution)/shard_map/dot_general | solution.py:248
  183.3 4.8 %fusion.23 = f32[1536,768]{1,0:T(8,128)} fusion(bf16[1024,1536]{1,0:T(8,128)(2,1)S(1)} %get-tuple-element.159, bf16[512,768]{1,0:T(8,128)(2,1)S(1)} %collective-permute-done.16, bf16[512,768]{1,0:T(8,128)(2,1)S(1)} %add_convert_fusion.1), kind=kOutput, calls=%fused_computation.70 | convolution fusion | flops 2419064832 | bytes 9437184 | tf_op jit(solution)/shard_map/dot_general | solution.py:248
  207.0 12.1 %collective-permute-done.42 = bf16[2,2,2,96,768]{4,3,0,1,2:T(8,128)(2,1)} collective-permute-done((bf16[2,2,2,96,768]{4,3,0,1,2:T(8,128)(2,1)}, bf16[2,2,2,96,768]{4,3,0,1,2:T(8,128)(2,1)}, u32[]{:S(2)}, u32[]{:S(2)}) %collective-permute-start.42) | collective-permute-done | bytes 1179680 | tf_op jit(solution)/shard_map/ppermute | solution.py:253
  230.6 4.2 convert_reduce_fusion.4
  234.8 5.3 %collective-permute-done.47 = bf16[2,2,48,1536]{3,2,1,0:T(8,128)(2,1)S(1)} collective-permute-done((bf16[2,2,48,1536]{3,2,1,0:T(8,128)(2,1)S(1)}, bf16[2,2,48,1536]{3,2,1,0:T(8,128)(2,1)S(1)}, u32[]{:S(2)}, u32[]{:S(2)}) %collective-permute-start.47) | collective-permute-done | bytes 589856 | tf_op jit(solution)/shard_map/ppermute | solution.py:253
  242.6 8.1 %collective-permute-done.48 = bf16[2,48,1536]{2,1,0:T(8,128)(2,1)S(1)} collective-permute-done((bf16[2,48,1536]{2,1,0:T(8,128)(2,1)S(1)}, bf16[2,48,1536]{2,1,0:T(8,128)(2,1)S(1)}, u32[]{:S(2)}, u32[]{:S(2)}) %collective-permute-start.48) | collective-permute-done | bytes 294944 | tf_op jit(solution)/shard_map/ppermute | solution.py:253
  257.7 3.9 collective-permute-done.49
  282.5 5.9 %collective-permute-done.37 = bf16[2,2,2,2,48,192]{5,4,3,2,1,0:T(8,128)(2,1)S(1)} collective-permute-done((bf16[2,2,2,2,48,192]{5,4,3,2,1,0:T(8,128)(2,1)S(1)}, bf16[2,2,2,2,48,192]{5,4,3,2,1,0:T(8,128)(2,1)S(1)}, u32[]{:S(2)}, u32[]{:S(2)}) %collective-permute-start.37) | collective-permute-done | bytes 294944 | tf_op jit(solution)/shard_map/ppermute | solution.py:253
  291.3 28.8 %attention_backward.1 = bf16[2048,768]{1,0:T(8,128)(2,1)S(1)} custom-call(s32[4]{0:T(128)S(1)} %pad_add_fusion.scalars, bf16[2048,768]{1,0:T(8,128)(2,1)} %copy-done, bf16[192,1024]{1,0:T(8,128)(2,1)S(1)} %get-tuple-element.26.out_keep, bf16[192,1024]{1,0:T(8,128)(2,1)S(1)} %get-tuple-element.27.out_send, ...), custom_call_target="tpu_custom_call" | custom-call | flops 8053063680 | bytes 6291456 | tf_op jit(solution)/shard_map/attention_backward/pallas_call | solution.py:204
  320.2 4.5 fusion.94
  326.4 5.8 %fusion.27 = f32[768,768]{1,0:T(8,128)} fusion(bf16[2048,768]{1,0:T(8,128)(2,1)S(1)} %attention_backward.1, bf16[512,768]{1,0:T(8,128)(2,1)S(1)} %copy-done.75, bf16[512,768]{1,0:T(8,128)(2,1)} %collective-permute-done.1, bf16[512,768]{1,0:T(8,128)(2,1)} %collective-permute-done, bf16[512,768]{1,0:T(8,128)(2,1)} %fusion.7), kind=kOutput, calls=%fused_computation.90 | convolution fusion | flops 2428502016 | bytes 8650752 | tf_op jit(solution)/shard_map/dot_general | solution.py:248
  336.1 5.0 %collective-permute-start.34 = (bf16[3,2,2,24,768]{4,3,0,1,2:T(8,128)(2,1)S(1)}, bf16[3,2,2,24,768]{4,3,0,1,2:T(8,128)(2,1)}, u32[]{:S(2)}, u32[]{:S(2)}) collective-permute-start(bf16[3,2,2,24,768]{4,3,0,1,2:T(8,128)(2,1)S(1)} %fusion.28), channel_id=1, source_target_pairs={{0,4},{4,0},{8,12},{12,8},{16,20},{20,16},{24,28},{28,24},{1,5},{5... | collective-permute-start | bytes 1327112 | tf_op jit(solution)/shard_map/ppermute | solution.py:253
  346.8 4.8 %collective-permute-done.34 = bf16[3,2,2,24,768]{4,3,0,1,2:T(8,128)(2,1)} collective-permute-done((bf16[3,2,2,24,768]{4,3,0,1,2:T(8,128)(2,1)S(1)}, bf16[3,2,2,24,768]{4,3,0,1,2:T(8,128)(2,1)}, u32[]{:S(2)}, u32[]{:S(2)}) %collective-permute-start.34) | collective-permute-done | bytes 442400 | tf_op jit(solution)/shard_map/ppermute | solution.py:253
  371.8 4.0 collective-permute-done.33
  401.2 6.7 %collective-permute-done.55 = f32[80,128]{1,0:T(8,128)S(1)} collective-permute-done((f32[80,128]{1,0:T(8,128)S(1)}, f32[80,128]{1,0:T(8,128)S(1)}, u32[]{:S(2)}, u32[]{:S(2)}) %collective-permute-start.55) | collective-permute-done | bytes 40992 | tf_op jit(solution)/shard_map/ppermute | solution.py:253
  443.9 3.9 collective-permute-done.63
  (453 shorter events, 218.3 us)
Async XLA Ops:
  6.4 80.4 %collective-permute-start.1 = (bf16[512,768]{1,0:T(8,128)(2,1)}, bf16[512,768]{1,0:T(8,128)(2,1)}, u32[]{:S(2)}, u32[]{:S(2)}) collective-permute-start(bf16[512,768]{1,0:T(8,128)(2,1)} %fusion.7), channel_id=1, source_target_pairs={{0,2},{1,3},{2,0},{3,1},{4,6},{5,7},{6,4},{7,5},{8,10},{9,11},{10,... | collective-permute-start | bytes 2359304 | tf_op jit(solution)/shard_map/ppermute | solution.py:253
  9.3 95.7 %collective-permute-start = (bf16[512,768]{1,0:T(8,128)(2,1)}, bf16[512,768]{1,0:T(8,128)(2,1)}, u32[]{:S(2)}, u32[]{:S(2)}) collective-permute-start(bf16[512,768]{1,0:T(8,128)(2,1)} %fusion.7), channel_id=1, source_target_pairs={{0,1},{1,0},{2,3},{3,2},{4,5},{5,4},{6,7},{7,6},{8,9},{9,8},{10,11... | collective-permute-start | bytes 2359304 | tf_op jit(solution)/shard_map/ppermute | solution.py:253
  10.0 13.7 %collective-permute-start.5 = (bf16[24,768]{1,0:T(8,128)(2,1)S(1)}, bf16[24,768]{1,0:T(8,128)(2,1)S(1)}, u32[]{:S(2)}, u32[]{:S(2)}) collective-permute-start(bf16[24,768]{1,0:T(8,128)(2,1)S(1)} %get-tuple-element.124), channel_id=1, source_target_pairs={{0,8},{1,20},{2,1},{3,13},{4,25},{5,6},{6,18},{7,30},{8,11},{9,23}... | collective-permute-start | bytes 110600 | tf_op jit(solution)/shard_map/ppermute | solution.py:358
  13.5 15.2 %collective-permute-start.4 = (bf16[24,768]{1,0:T(8,128)(2,1)S(1)}, bf16[24,768]{1,0:T(8,128)(2,1)S(1)}, u32[]{:S(2)}, u32[]{:S(2)}) collective-permute-start(bf16[24,768]{1,0:T(8,128)(2,1)S(1)} %get-tuple-element.125), channel_id=1, source_target_pairs={{0,4},{1,16},{2,28},{3,9},{4,21},{5,2},{6,14},{7,26},{8,7},{9,19},... | collective-permute-start | bytes 110600 | tf_op jit(solution)/shard_map/ppermute | solution.py:358
  23.7 29.1 %collective-permute-start.17 = (bf16[96,768]{1,0:T(8,128)(2,1)S(1)}, bf16[96,768]{1,0:T(8,128)(2,1)S(1)}, u32[]{:S(2)}, u32[]{:S(2)}) collective-permute-start(bf16[96,768]{1,0:T(8,128)(2,1)S(1)} %get-tuple-element.100), channel_id=1, source_target_pairs={{0,16},{4,20},{8,24},{12,28},{16,0},{20,4},{24,8},{28,12},{1,17},{... | collective-permute-start | bytes 442376 | tf_op jit(solution)/shard_map/ppermute | solution.py:253
  28.7 110.9 %collective-permute-start.27 = (bf16[512,768]{1,0:T(8,128)(2,1)S(1)}, bf16[512,768]{1,0:T(8,128)(2,1)}, u32[]{:S(2)}, u32[]{:S(2)}) collective-permute-start(bf16[512,768]{1,0:T(8,128)(2,1)S(1)} %copy-done.11), channel_id=1, source_target_pairs={{0,1},{1,0},{2,3},{3,2},{4,5},{5,4},{6,7},{7,6},{8,9},{9,8},{10,11... | collective-permute-start | bytes 2359304 | tf_op jit(solution)/shard_map/ppermute | solution.py:253
  60.1 14.6 %collective-permute-start.18 = (bf16[2,96,768]{2,1,0:T(8,128)(2,1)S(1)}, bf16[2,96,768]{2,1,0:T(8,128)(2,1)S(1)}, u32[]{:S(2)}, u32[]{:S(2)}) collective-permute-start(bf16[2,96,768]{2,1,0:T(8,128)(2,1)S(1)} %pad_maximum_fusion.19), channel_id=1, source_target_pairs={{0,8},{4,12},{8,0},{12,4},{16,24},{20,28},{24,16},{28,20},{1,9},{5... | collective-permute-start | bytes 884744 | tf_op jit(solution)/shard_map/ppermute | solution.py:253
  78.9 15.1 %collective-permute-start.8 = (bf16[3,2,2,24,768]{4,3,2,1,0:T(8,128)(2,1)S(1)}, bf16[3,2,2,24,768]{4,3,2,1,0:T(8,128)(2,1)S(1)}, u32[]{:S(2)}, u32[]{:S(2)}) collective-permute-start(bf16[3,2,2,24,768]{4,3,2,1,0:T(8,128)(2,1)S(1)} %pad_maximum_fusion.16), channel_id=1, source_target_pairs={{0,4},{4,0},{8,12},{12,8},{16,20},{20,16},{24,28},{28,24},{1,5},{5... | collective-permute-start | bytes 1327112 | tf_op jit(solution)/shard_map/ppermute | solution.py:253
  83.7 21.2 %collective-permute-start.19 = (bf16[2,2,96,768]{3,2,1,0:T(8,128)(2,1)S(1)}, bf16[2,2,96,768]{3,2,1,0:T(8,128)(2,1)S(1)}, u32[]{:S(2)}, u32[]{:S(2)}) collective-permute-start(bf16[2,2,96,768]{3,2,1,0:T(8,128)(2,1)S(1)} %pad_maximum_fusion.12), channel_id=1, source_target_pairs={{0,4},{4,0},{8,12},{12,8},{16,20},{20,16},{24,28},{28,24},{1,5},{5... | collective-permute-start | bytes 1769480 | tf_op jit(solution)/shard_map/ppermute | solution.py:253
  86.8 18.3 %collective-permute-start.2 = (bf16[512,768]{1,0:T(8,128)(2,1)}, bf16[512,768]{1,0:T(8,128)(2,1)S(1)}, u32[]{:S(2)}, u32[]{:S(2)}) collective-permute-start(bf16[512,768]{1,0:T(8,128)(2,1)} %collective-permute-done.1), channel_id=1, source_target_pairs={{0,1},{1,0},{2,3},{3,2},{4,5},{5,4},{6,7},{7,6},{8,9},{9,8},{10,11... | collective-permute-start | bytes 2359304 | tf_op jit(solution)/shard_map/ppermute | solution.py:253
  93.9 46.9 %collective-permute-start.24 = (bf16[2,2,48,1536]{3,2,1,0:T(8,128)(2,1)}, bf16[2,2,48,1536]{3,2,1,0:T(8,128)(2,1)}, u32[]{:S(2)}, u32[]{:S(2)}) collective-permute-start(bf16[2,2,48,1536]{3,2,1,0:T(8,128)(2,1)} %pad_maximum_fusion.13), channel_id=1, source_target_pairs={{0,2},{1,3},{2,0},{3,1},{4,6},{5,7},{6,4},{7,5},{8,10},{9,11},{10,... | collective-permute-start | bytes 1769480 | tf_op jit(solution)/shard_map/ppermute | solution.py:253
  125.7 33.8 %collective-permute-start.20 = (bf16[2,2,2,96,768]{4,3,2,1,0:T(8,128)(2,1)}, bf16[2,2,2,96,768]{4,3,2,1,0:T(8,128)(2,1)}, u32[]{:S(2)}, u32[]{:S(2)}) collective-permute-start(bf16[2,2,2,96,768]{4,3,2,1,0:T(8,128)(2,1)} %pad_maximum_fusion.6), channel_id=1, source_target_pairs={{0,2},{1,3},{2,0},{3,1},{4,6},{5,7},{6,4},{7,5},{8,10},{9,11},{10,... | collective-permute-start | bytes 3538952 | tf_op jit(solution)/shard_map/ppermute | solution.py:253
  139.4 21.9 %collective-permute-start.15 = (f32[512,768]{1,0:T(8,128)}, f32[512,768]{1,0:T(8,128)}, u32[]{:S(2)}, u32[]{:S(2)}) collective-permute-start(f32[512,768]{1,0:T(8,128)} %slice.197), channel_id=1, source_target_pairs={{0,1},{1,0},{2,3},{3,2},{4,5},{5,4},{6,7},{7,6},{8,9},{9,8},{10,11... | collective-permute-start | bytes 4718600 | tf_op jit(solution)/shard_map/ppermute | solution.py:253
  142.2 30.9 %collective-permute-start.25 = (bf16[2,2,2,48,1536]{4,3,2,1,0:T(8,128)(2,1)S(1)}, bf16[2,2,2,48,1536]{4,3,2,1,0:T(8,128)(2,1)S(1)}, u32[]{:S(2)}, u32[]{:S(2)}) collective-permute-start(bf16[2,2,2,48,1536]{4,3,2,1,0:T(8,128)(2,1)S(1)} %pad_maximum_fusion.7), channel_id=1, source_target_pairs={{0,4},{4,0},{8,12},{12,8},{16,20},{20,16},{24,28},{28,24},{1,5},{5... | collective-permute-start | bytes 3538952 | tf_op jit(solution)/shard_map/ppermute | solution.py:253
  191.0 28.1 %collective-permute-start.42 = (bf16[2,2,2,96,768]{4,3,0,1,2:T(8,128)(2,1)}, bf16[2,2,2,96,768]{4,3,0,1,2:T(8,128)(2,1)}, u32[]{:S(2)}, u32[]{:S(2)}) collective-permute-start(bf16[2,2,2,96,768]{4,3,0,1,2:T(8,128)(2,1)} %fusion.22), channel_id=1, source_target_pairs={{0,4},{4,0},{8,12},{12,8},{16,20},{20,16},{24,28},{28,24},{1,5},{5... | collective-permute-start | bytes 3538952 | tf_op jit(solution)/shard_map/ppermute | solution.py:253
  196.7 28.5 %collective-permute-start.46 = (bf16[2,2,2,48,1536]{4,3,2,1,0:T(8,128)(2,1)}, bf16[2,2,2,48,1536]{4,3,2,1,0:T(8,128)(2,1)}, u32[]{:S(2)}, u32[]{:S(2)}) collective-permute-start(bf16[2,2,2,48,1536]{4,3,2,1,0:T(8,128)(2,1)} %fusion.21), channel_id=1, source_target_pairs={{0,2},{1,3},{2,0},{3,1},{4,6},{5,7},{6,4},{7,5},{8,10},{9,11},{10,... | collective-permute-start | bytes 3538952 | tf_op jit(solution)/shard_map/ppermute | solution.py:253
  201.5 25.8 %collective-permute-start.28 = (f32[512,768]{1,0:T(8,128)}, f32[512,768]{1,0:T(8,128)}, u32[]{:S(2)}, u32[]{:S(2)}) collective-permute-start(f32[512,768]{1,0:T(8,128)} %slice.201), channel_id=1, source_target_pairs={{0,1},{1,0},{2,3},{3,2},{4,5},{5,4},{6,7},{7,6},{8,9},{9,8},{10,11... | collective-permute-start | bytes 4718600 | tf_op jit(solution)/shard_map/ppermute | solution.py:253
  206.3 24.3 %collective-permute-start.26 = (f32[512,768]{1,0:T(8,128)}, f32[512,768]{1,0:T(8,128)}, u32[]{:S(2)}, u32[]{:S(2)}) collective-permute-start(f32[512,768]{1,0:T(8,128)} %slice.199), channel_id=1, source_target_pairs={{0,1},{1,0},{2,3},{3,2},{4,5},{5,4},{6,7},{7,6},{8,9},{9,8},{10,11... | collective-permute-start | bytes 4718600 | tf_op jit(solution)/shard_map/ppermute | solution.py:253
  221.6 18.8 %collective-permute-start.43 = (bf16[2,2,96,768]{3,2,0,1:T(8,128)(2,1)S(1)}, bf16[2,2,96,768]{3,2,0,1:T(8,128)(2,1)S(1)}, u32[]{:S(2)}, u32[]{:S(2)}) collective-permute-start(bf16[2,2,96,768]{3,2,0,1:T(8,128)(2,1)S(1)} %fusion.25), channel_id=1, source_target_pairs={{0,2},{1,3},{2,0},{3,1},{4,6},{5,7},{6,4},{7,5},{8,10},{9,11},{10,... | collective-permute-start | bytes 1769480 | tf_op jit(solution)/shard_map/ppermute | solution.py:253
  234.8 29.0 %collective-permute-start.29 = (bf16[512,768]{1,0:T(8,128)(2,1)}, bf16[512,768]{1,0:T(8,128)(2,1)}, u32[]{:S(2)}, u32[]{:S(2)}) collective-permute-start(bf16[512,768]{1,0:T(8,128)(2,1)} %get-tuple-element.63), channel_id=1, source_target_pairs={{0,1},{1,0},{2,3},{3,2},{4,5},{5,4},{6,7},{7,6},{8,9},{9,8},{10,11... | collective-permute-start | bytes 2359304 | tf_op jit(solution)/shard_map/ppermute | solution.py:253
  240.5 13.3 %collective-permute-start.44 = (bf16[2,96,768]{2,1,0:T(8,128)(2,1)S(1)}, bf16[2,96,768]{2,1,0:T(8,128)(2,1)S(1)}, u32[]{:S(2)}, u32[]{:S(2)}) collective-permute-start(bf16[2,96,768]{2,1,0:T(8,128)(2,1)S(1)} %fusion.42), channel_id=1, source_target_pairs={{0,8},{4,12},{8,0},{12,4},{16,24},{20,28},{24,16},{28,20},{1,9},{5... | collective-permute-start | bytes 884744 | tf_op jit(solution)/shard_map/ppermute | solution.py:253
  262.5 16.0 %collective-permute-start.50 = (f32[24,16,96]{2,1,0:T(8,128)}, f32[24,16,96]{2,1,0:T(8,128)}, u32[]{:S(2)}, u32[]{:S(2)}) collective-permute-start(f32[24,16,96]{2,1,0:T(8,128)} %dynamic-slice_bitcast_fusion), channel_id=1, source_target_pairs={{0,1},{1,0},{2,3},{3,2},{4,5},{5,4},{6,7},{7,6},{8,9},{9,8},{10,11... | collective-permute-start | bytes 442376 | tf_op jit(solution)/shard_map/ppermute | solution.py:253
  266.7 24.7 %collective-permute-start.30 = (bf16[192,1024]{1,0:T(8,128)(2,1)}, bf16[192,1024]{1,0:T(8,128)(2,1)S(1)}, u32[]{:S(2)}, u32[]{:S(2)}) collective-permute-start(bf16[192,1024]{1,0:T(8,128)(2,1)} %convolution_convert_fusion), channel_id=1, source_target_pairs={{0,2},{1,3},{2,0},{3,1},{4,6},{5,7},{6,4},{7,5},{8,10},{9,11},{10,... | collective-permute-start | bytes 1179656 | tf_op jit(solution)/shard_map/ppermute | solution.py:253
  289.2 45.7 %collective-permute-start.38 = (bf16[2,2,2,48,192]{4,3,2,1,0:T(8,128)(2,1)}, bf16[2,2,2,48,192]{4,3,2,1,0:T(8,128)(2,1)}, u32[]{:S(2)}, u32[]{:S(2)}) collective-permute-start(bf16[2,2,2,48,192]{4,3,2,1,0:T(8,128)(2,1)} %fusion.46), channel_id=1, source_target_pairs={{0,4},{4,0},{8,12},{12,8},{16,20},{20,16},{24,28},{28,24},{1,5},{5... | collective-permute-start | bytes 442376 | tf_op jit(solution)/shard_map/ppermute | solution.py:253
  325.9 28.6 %collective-permute-start.32 = (bf16[512,768]{1,0:T(8,128)(2,1)}, bf16[512,768]{1,0:T(8,128)(2,1)}, u32[]{:S(2)}, u32[]{:S(2)}) collective-permute-start(bf16[512,768]{1,0:T(8,128)(2,1)} %get-tuple-element.70), channel_id=1, source_target_pairs={{0,1},{1,0},{2,3},{3,2},{4,5},{5,4},{6,7},{7,6},{8,9},{9,8},{10,11... | collective-permute-start | bytes 2359304 | tf_op jit(solution)/shard_map/ppermute | solution.py:253
  325.9 45.9 %collective-permute-start.31 = (bf16[512,768]{1,0:T(8,128)(2,1)}, bf16[512,768]{1,0:T(8,128)(2,1)}, u32[]{:S(2)}, u32[]{:S(2)}) collective-permute-start(bf16[512,768]{1,0:T(8,128)(2,1)} %get-tuple-element.69), channel_id=1, source_target_pairs={{0,1},{1,0},{2,3},{3,2},{4,5},{5,4},{6,7},{7,6},{8,9},{9,8},{10,11... | collective-permute-start | bytes 2359304 | tf_op jit(solution)/shard_map/ppermute | solution.py:253
  336.1 15.4 %collective-permute-start.34 = (bf16[3,2,2,24,768]{4,3,0,1,2:T(8,128)(2,1)S(1)}, bf16[3,2,2,24,768]{4,3,0,1,2:T(8,128)(2,1)}, u32[]{:S(2)}, u32[]{:S(2)}) collective-permute-start(bf16[3,2,2,24,768]{4,3,0,1,2:T(8,128)(2,1)S(1)} %fusion.28), channel_id=1, source_target_pairs={{0,4},{4,0},{8,12},{12,8},{16,20},{20,16},{24,28},{28,24},{1,5},{5... | collective-permute-start | bytes 1327112 | tf_op jit(solution)/shard_map/ppermute | solution.py:253
  346.7 13.7 %collective-permute-start.41 = (f32[24,2,192]{2,0,1:T(8,128)S(1)}, f32[24,2,192]{2,0,1:T(8,128)S(1)}, u32[]{:S(2)}, u32[]{:S(2)}) collective-permute-start(f32[24,2,192]{2,0,1:T(8,128)S(1)} %dynamic-slice_bitcast_fusion.4), channel_id=1, source_target_pairs={{0,1},{1,0},{2,3},{3,2},{4,5},{5,4},{6,7},{7,6},{8,9},{9,8},{10,11... | collective-permute-start | bytes 110600 | tf_op jit(solution)/shard_map/ppermute | solution.py:253
  357.1 18.6 %collective-permute-start.33 = (bf16[512,768]{1,0:T(8,128)(2,1)}, bf16[512,768]{1,0:T(8,128)(2,1)}, u32[]{:S(2)}, u32[]{:S(2)}) collective-permute-start(bf16[512,768]{1,0:T(8,128)(2,1)} %fusion.15), channel_id=1, source_target_pairs={{0,2},{1,3},{2,0},{3,1},{4,6},{5,7},{6,4},{7,5},{8,10},{9,11},{10,... | collective-permute-start | bytes 2359304 | tf_op jit(solution)/shard_map/ppermute | solution.py:253
  392.8 28.7 %collective-permute-start.58 = (f32[24,768]{1,0:T(8,128)}, f32[24,768]{1,0:T(8,128)}, u32[]{:S(2)}, u32[]{:S(2)}) collective-permute-start(f32[24,768]{1,0:T(8,128)} %get-tuple-element.109), channel_id=1, source_target_pairs={{8,0},{20,1},{1,2},{13,3},{25,4},{6,5},{18,6},{30,7},{11,8},{23,9}... | collective-permute-start | bytes 221192 | tf_op jit(solution)/shard_map/ppermute | solution.py:376
  396.3 25.2 %collective-permute-start.57 = (f32[24,768]{1,0:T(8,128)}, f32[24,768]{1,0:T(8,128)}, u32[]{:S(2)}, u32[]{:S(2)}) collective-permute-start(f32[24,768]{1,0:T(8,128)} %get-tuple-element.108), channel_id=1, source_target_pairs={{4,0},{16,1},{28,2},{9,3},{21,4},{2,5},{14,6},{26,7},{7,8},{19,9},... | collective-permute-start | bytes 221192 | tf_op jit(solution)/shard_map/ppermute | solution.py:376
  396.4 25.2 %collective-permute-start.56 = (f32[24,768]{1,0:T(8,128)}, f32[24,768]{1,0:T(8,128)}, u32[]{:S(2)}, u32[]{:S(2)}) collective-permute-start(f32[24,768]{1,0:T(8,128)} %get-tuple-element.107), channel_id=1, source_target_pairs={{0,0},{12,1},{24,2},{5,3},{17,4},{29,5},{10,6},{22,7},{3,8},{15,9}... | collective-permute-start | bytes 221192 | tf_op jit(solution)/shard_map/ppermute | solution.py:376
  (109 other events, 1054.5 us)

commit v3 on v2

v3 whole, which is shorter than its diff:
```python
from functools import partial
import jax
import jax.numpy as jnp
from jax import lax
from jax.experimental import pallas as pl
from jax.experimental.pallas import tpu as pltpu
from jax.sharding import PartitionSpec as P

D = 768
HD = 64
FF = 3072
STEP = 5
NORM_EPS = 1e-05
ADAM_EPS = 1e-06
DECAY_RATE = 0.01
MATRIX_RATE = 0.5
VECTOR_RATE = 0.1
ROOT_TWO_OVER_PI = (2.0 / 3.141592653589793) ** 0.5
BLOCK = 256
LANES = 256
NT = (((1,), (1,)), ((), ()))
NN = (((1,), (0,)), ((), ()))
F32 = jnp.float32
BF16 = jnp.bfloat16


def mm(a, b, dims):
    return lax.dot_general(a, b, dims, preferred_element_type=F32)


def block_start(index, per_piece, me):
    piece = index // per_piece
    return pl.multiple_of(((piece ^ me) * per_piece + index % per_piece) * BLOCK, BLOCK)


def starts_of(scalars, docs, positions):
    first = jnp.zeros_like(positions)
    for doc in range(docs - 1):
        end = scalars[ENDS + doc]
        first = jnp.where(positions >= end, end, first)
    return first


def first_block(scalars, docs, index):
    position = index * BLOCK
    first = jnp.int32(0)
    for doc in range(docs - 1):
        end = scalars[ENDS + doc]
        first = jnp.where(position >= end, end, first)
    return first // BLOCK


def head_lanes(block, heads):
    if heads == 1:
        return [block]
    lane = lax.broadcasted_iota(jnp.int32, block.shape, 1) // HD
    return [jnp.where(lane == j, block, jnp.zeros_like(block)) for j in range(heads)]


def allowed_mask(index, key_block, doc_first):
    query = index * BLOCK + lax.broadcasted_iota(jnp.int32, (1, BLOCK), 1)
    key = key_block * BLOCK + lax.broadcasted_iota(jnp.int32, (BLOCK, BLOCK), 0)
    return (key <= query) & (key >= doc_first)


def group_lanes(group, kind):
    start = kind * LANES + group * HEAD_LANES
    return slice(start, start + HEAD_LANES)


def forward_body(heads, group, docs, per_piece, blocks, cuts, scalars, qkv, *refs):
    pairs, refs = refs[: 2 * len(cuts)], refs[2 * len(cuts) :]
    keep_out, send_out, log_out = refs[:3]
    values_t, out_t = refs[-2:]
    join_pairs(pairs, refs[3:-2], cuts)
    me = scalars[HERE]
    width = heads * HD

    def transpose_values(i, carry):
        v = qkv[pl.ds(block_start(i, per_piece, me), BLOCK), group_lanes(group, 2)]
        values_t[:, pl.ds(pl.multiple_of(i * BLOCK, BLOCK), BLOCK)] = v.T[:width]
        return carry

    lax.fori_loop(0, blocks, transpose_values, 0)

    def query_block(i, carry):
        row = block_start(i, per_piece, me)
        q_heads = head_lanes(qkv[pl.ds(row, BLOCK), group_lanes(group, 0)] * BF16(HD ** -0.5), heads)
        positions = i * BLOCK + lax.broadcasted_iota(jnp.int32, (1, BLOCK), 1)
        doc_first = starts_of(scalars, docs, positions)

        def key_step(kb, state):
            allowed = allowed_mask(i, kb, doc_first)
            k = qkv[pl.ds(block_start(kb, per_piece, me), BLOCK), group_lanes(group, 1)]
            column = pl.ds(pl.multiple_of(kb * BLOCK, BLOCK), BLOCK)
            new = []
            for j in range(heads):
                top, total, acc = state[j]
                s = jnp.where(allowed, mm(k, q_heads[j], NT), -1e30)
                top_new = jnp.maximum(top, jnp.max(s, axis=0, keepdims=True))
                p = jnp.exp(s - top_new)
                fade = jnp.exp(top - top_new)
                total = total * fade + jnp.sum(p, axis=0, keepdims=True)
                v_t = values_t[j * HD : (j + 1) * HD, column]
                acc = acc * fade + mm(v_t, p.astype(BF16), NN)
                new.append((top_new, total, acc))
            return tuple(new)

        init = tuple(
            (jnp.full((1, BLOCK), -1e30, F32), jnp.zeros((1, BLOCK), F32), jnp.zeros((HD, BLOCK), F32))
            for _ in range(heads)
        )
        state = key_step(i, init)
        state = lax.fori_loop(first_block(scalars, docs, i), i, key_step, state)
        column = pl.ds(row, BLOCK)
        for j in range(heads):
            top, total, acc = state[j]
            out_t[j * HD : (j + 1) * HD, column] = (acc / total).astype(BF16)
            log_out[j : j + 1, pl.ds(pl.multiple_of(i * BLOCK, BLOCK), BLOCK)] = top + jnp.log(total)
        return carry

    lax.fori_loop(0, blocks, query_block, 0)
    half = out_t.shape[1] // 2
    keep_out[...] = out_t[:, :half]
    send_out[...] = out_t[:, half:]


def attention_forward(scalars, qkv, heads, group, docs, piece, pairs, cuts):
    rows = qkv.shape[0]
    width = heads * HD
    flat = [x for pair in pairs for x in pair]
    found = call(
        partial(forward_body, heads, group, docs, piece // BLOCK, rows // BLOCK, cuts),
        [scalars, qkv, *flat],
        [
            shape((width, rows // 2), BF16),
            shape((width, rows // 2), BF16),
            shape((8, rows), F32),
            *join_shapes(pairs, cuts),
        ],
        [pltpu.VMEM((width, rows), BF16), pltpu.VMEM((width, rows), BF16)],
        24,
        "attention_forward",
    )
    return found[:3], found[3:]


def backward_body(
    heads, group, docs, per_piece, blocks, scalars, qkv, out_keep, out_send, grad_keep, grad_recv, logs, grads,
    sums, keys_t, out_t, grad_t, d_keys, d_values
):
    me = scalars[HERE]
    width = heads * HD
    scale = HD ** -0.5
    half = out_keep.shape[1]
    out_t[:, :half] = out_keep[...]
    out_t[:, half:] = out_send[...]
    grad_t[:, :half] = grad_keep[...]
    grad_t[:, half:] = grad_recv[...]
    d_keys[...] = jnp.zeros_like(d_keys)
    d_values[...] = jnp.zeros_like(d_values)

    def transpose_keys(i, carry):
        k = qkv[pl.ds(block_start(i, per_piece, me), BLOCK), group_lanes(group, 1)]
        keys_t[:, pl.ds(pl.multiple_of(i * BLOCK, BLOCK), BLOCK)] = k.T[:width]
        return carry

    lax.fori_loop(0, blocks, transpose_keys, 0)

    def padded(rows, kind):
        if width == HEAD_LANES:
            return rows
        return jnp.concatenate([rows, jnp.zeros((HEAD_LANES - width, BLOCK), kind)], axis=0)

    def query_block(i, carry):
        row = block_start(i, per_piece, me)
        q_heads = head_lanes(qkv[pl.ds(row, BLOCK), group_lanes(group, 0)] * BF16(scale), heads)
        o_t = out_t[:, pl.ds(row, BLOCK)]
        g_t = grad_t[:, pl.ds(row, BLOCK)]
        product = o_t.astype(F32) * g_t.astype(F32)
        deltas = [jnp.sum(product[j * HD : (j + 1) * HD], axis=0, keepdims=True) for j in range(heads)]
        g_heads = head_lanes(padded(g_t, BF16).T, heads)
        natural = pl.ds(pl.multiple_of(i * BLOCK, BLOCK), BLOCK)
        log_rows = [logs[j : j + 1, natural] for j in range(heads)]
        positions = i * BLOCK + lax.broadcasted_iota(jnp.int32, (1, BLOCK), 1)
        doc_first = starts_of(scalars, docs, positions)

        def key_step(kb, d_q):
            allowed = allowed_mask(i, kb, doc_first)
            key_row = pl.ds(block_start(kb, per_piece, me), BLOCK)
            k = qkv[key_row, group_lanes(group, 1)]
            v = qkv[key_row, group_lanes(group, 2)]
            column = pl.ds(pl.multiple_of(kb * BLOCK, BLOCK), BLOCK)
            d_k = d_keys[key_row, :]
            d_v = d_values[key_row, :]
            new = []
            for j in range(heads):
                s = jnp.where(allowed, mm(k, q_heads[j], NT), -1e30)
                p = jnp.exp(s - log_rows[j])
                d_v = d_v + mm(p.astype(BF16), g_heads[j], NN)
                d_p = mm(v, g_heads[j], NT)
                d_s = (p * (d_p - deltas[j])).astype(BF16)
                d_k = d_k + mm(d_s, q_heads[j], NN)
                new.append(d_q[j] + mm(keys_t[j * HD : (j + 1) * HD, column], d_s, NN))
            d_keys[key_row, :] = d_k
            d_values[key_row, :] = d_v
            return tuple(new)

        d_q = key_step(i, tuple(jnp.zeros((HD, BLOCK), F32) for _ in range(heads)))
        d_q = lax.fori_loop(first_block(scalars, docs, i), i, key_step, d_q)
        stacked = padded(jnp.concatenate(d_q, axis=0), F32) * scale
        grads[pl.ds(row, BLOCK), 0:HEAD_LANES] = stacked.T.astype(BF16)
        return carry

    lax.fori_loop(0, blocks, query_block, 0)
    grads[:, HEAD_LANES : 2 * HEAD_LANES] = d_keys[...].astype(BF16)
    grads[:, 2 * HEAD_LANES : 3 * HEAD_LANES] = d_values[...].astype(BF16)
    sums[...] = jnp.zeros_like(sums)
    for line, kind in enumerate((0, 2)):
        columns = grads[:, kind * HEAD_LANES : (kind + 1) * HEAD_LANES].astype(F32)
        sums[line : line + 1, :] = jnp.sum(columns, axis=0, keepdims=True)


def attention_backward(scalars, qkv, outs, grads, logs, heads, group, docs, piece, markers=()):
    rows = qkv.shape[0]
    width = heads * HD
    return call(
        partial(backward_body, heads, group, docs, piece // BLOCK, rows // BLOCK),
        [scalars, qkv, *outs, *grads, logs],
        [shape((rows, 3 * HEAD_LANES), BF16), shape((8, HEAD_LANES), F32)],
        [pltpu.VMEM((width, rows), BF16)] * 3 + [pltpu.VMEM((rows, HEAD_LANES), F32)] * 2,
        26,
        "attention_backward",
        markers=markers,
    )


MICROSECONDS = {
    "prepare": 2,
    "block_kinds": 1,
    "join": 2,
    "project": 5,
    "attention_forward": 16,
    "branch": 2,
    "middle_norm": 2,
    "feed_forward": 18,
    "head_gradients": 2,
    "output_weight_gradient": 2,
    "attention_backward": 32,
    "first_norm_gradient": 2,
    "input_weight_gradient": 4,
    "add_arrived": 1,
    "middle_gradient": 2,
    "first_gradient": 4,
    "payload": 2,
    "moments": 4,
    "weights": 3,
}
COST_SCALE = 4.0


def cost(name):
    flops = int(MICROSECONDS[name] * COST_SCALE * 1.0e9)
    return pl.CostEstimate(flops=flops, bytes_accessed=0, transcendentals=0)


VMEM = pl.BlockSpec(memory_space=pltpu.VMEM)
SMEM = pl.BlockSpec(memory_space=pltpu.SMEM)
LEFT = pl.BlockSpec(memory_space=pl.ANY)
TN = (((0,), (0,)), ((), ()))
HERE, CHIP, ROW, CORE, SIDE, PLACE = range(6)
ENDS = 6


class Places:
    def __init__(self, lengths=None):
        self.lengths = lengths

    def __getitem__(self, number):
        here, row = lax.axis_index("head"), lax.axis_index("batch")
        heads, rows = lax.axis_size("head"), lax.axis_size("batch")
        if number == HERE:
            return here
        if number == CHIP:
            return row * (heads // 2) + here // 2
        if number == ROW:
            return row
        if number == CORE:
            return here % 2
        if number == SIDE:
            return here // 2
        if number == PLACE:
            return rows * here + row
        return sum(self.lengths[0, doc] for doc in range(number - ENDS + 1))


def call(body, inputs, outputs, scratch, mib, name, markers=()):
    lengths, inputs = inputs[0].lengths, inputs[1:]
    lead = [] if lengths is None else [lengths]
    count = len(lead) + len(inputs)

    def whole(*refs):
        places = Places(refs[0] if lead else None)
        body(places, *refs[len(lead) : count], *refs[count + len(markers) :])

    return pl.pallas_call(
        whole,
        out_shape=tuple(outputs),
        in_specs=[SMEM] * len(lead) + [VMEM] * len(inputs) + [LEFT] * len(markers),
        out_specs=(VMEM,) * len(outputs),
        scratch_shapes=scratch,
        compiler_params=pltpu.CompilerParams(vmem_limit_bytes=mib * 2**20),
        cost_estimate=cost(name),
        name=name,
    )(*lead, *inputs, *markers)


def lines_row(lines, first, count):
    return jnp.concatenate([lines[pl.ds(first + i, 1), :] for i in range(count)], axis=1)


def vector_row(lines, number):
    return lines_row(lines, number * (D // 128), D // 128)


def heads_row(lines, number, here):
    width = D // lax.axis_size("head")
    row = lines_row(lines, number * (D // 128) + (width * here) // 128, LANES // 128)
    row = jnp.where((width * here) % 128 != 0, pltpu.roll(row, LANES - HD, 1), row)
    lane = lax.broadcasted_iota(jnp.int32, row.shape, 1)
    return jnp.where(lane < width, row, 0.0)


def shape(dims, kind):
    return jax.ShapeDtypeStruct(tuple(dims), kind)


def join_pairs(ins, outs, cuts):
    outs = list(outs)
    for i, cut in enumerate(cuts):
        own, arrived = ins[2 * i], ins[2 * i + 1]
        half = own.shape[0]
        if cut == 0:
            out = outs.pop(0)
            out[:half] = own[...]
            out[half:] = arrived[...]
            continue
        rows = own.shape[1] // cut
        for part in range(cut):
            out = outs.pop(0)
            out[:half] = own[:, part * rows : (part + 1) * rows]
            out[half:] = arrived[:, part * rows : (part + 1) * rows]


def join_body(cuts, scalars, *refs):
    count = 2 * len(cuts)
    join_pairs(refs[:count], refs[count:], cuts)


def join_shapes(pairs, cuts):
    shapes = []
    for (own, _), cut in zip(pairs, cuts):
        dims = (2 * own.shape[0],) + own.shape[1:]
        if cut == 0:
            shapes.append(shape(dims, own.dtype))
        else:
            shapes += [shape((dims[0], dims[1] // cut, dims[2]), own.dtype)] * cut
    return shapes


def join(scalars, pairs, cuts, markers=()):
    flat = [x for pair in pairs for x in pair]
    return call(
        partial(join_body, cuts), [scalars, *flat], join_shapes(pairs, cuts), [], 24, "join", markers=markers
    )


def prepare_body(scalars, weight_in, weight_expand, weight_out, tokens, lines, *outs):
    blocks, (expand, mine, other, normed) = outs[:3], outs[3:]
    rows = blocks[0].shape[0]
    for slot, out in enumerate(blocks):
        out[...] = weight_in[slot * rows : (slot + 1) * rows, :].astype(BF16)
    expand[...] = weight_expand[...].astype(BF16)
    quarter = D // 4
    wide = weight_out[...]
    even = jnp.concatenate([wide[:, :quarter], wide[:, 2 * quarter : 3 * quarter]], axis=1)
    odd = jnp.concatenate([wide[:, quarter : 2 * quarter], wide[:, 3 * quarter :]], axis=1)
    high = scalars[CORE] == 1
    mine[...] = jnp.where(high, odd, even).astype(BF16)
    other[...] = jnp.where(high, even, odd).astype(BF16)
    gain, shift = vector_row(lines, 0), vector_row(lines, 1)
    step = min(128, tokens.shape[0])
    for start in range(0, tokens.shape[0], step):
        unit, _ = row_norm(tokens[start : start + step, :].astype(F32))
        normed[start : start + step, :] = (unit * gain + shift).astype(BF16)


def prepare(scalars, weight_in, weight_expand, weight_out, tokens, lines):
    rows, out_rows = weight_in.shape[0] // 3, weight_out.shape[0]
    return call(
        prepare_body,
        [scalars, weight_in, weight_expand, weight_out, tokens, lines],
        [shape((rows, D), BF16)] * 3
        + [
            shape(weight_expand.shape, BF16),
            shape((out_rows, D // 2), BF16),
            shape((out_rows, D // 2), BF16),
            shape(tokens.shape, BF16),
        ],
        [],
        60,
        "prepare",
    )


def kinds_body(total, scalars, first, second, third, out):
    place = scalars[PLACE]
    rows = first.shape[0]
    for slot, block in enumerate((first, second, third)):
        kind = ((slot + 3 * total - place) * total) % 3
        out[kind] = block[...]


def block_kinds(scalars, blocks, total):
    rows = blocks[0].shape[0]
    outs = [shape((3, rows, D), BF16)]
    return call(partial(kinds_body, total), [scalars, *blocks], outs, [], 8, "block_kinds")[0]


def spread(scalars, base, parts, masks, put):
    origin = scalars[base] if base is not None else 0
    for ref, own in zip(parts, masks):
        for r, mask in enumerate(own):
            put(origin ^ mask if base is not None else mask, ref[r])


def project_body(base, masks, cuts, scalars, mine, other, lines, *refs):
    parts, refs = refs[: len(masks)], refs[len(masks) :]
    pairs, refs = refs[: 2 * len(cuts)], refs[2 * len(cuts) :]
    out, weight_out, weight = refs[0], refs[1], refs[-1]
    join_pairs(pairs, refs[2:-1], cuts)
    weight[...] = jnp.zeros_like(weight)

    def put(place, chunk):
        rows = chunk.shape[0] // 3
        wide = chunk.astype(F32)
        for kind in range(3):
            start = kind * LANES + place * rows
            if base is not None:
                start = pl.multiple_of(start, 8)
            weight[pl.ds(start, rows), :] = wide[kind * rows : (kind + 1) * rows]

    spread(scalars, base, parts, masks, put)
    low = weight[...].astype(BF16)
    weight_out[...] = low
    piece = mine.shape[0] // 2
    here = scalars[HERE]
    bias = jnp.concatenate(
        [heads_row(lines, 4, here), jnp.zeros((1, LANES), F32), heads_row(lines, 5, here)], axis=1
    )
    for place, (source, lead) in enumerate(((mine, 0), (other, 0), (mine, piece), (other, piece))):
        rows = source[lead : lead + piece, :]
        out[place * piece : (place + 1) * piece, :] = (mm(rows, low, NT) + bias).astype(BF16)


def project(scalars, mine, other, lines, base, parts, masks, pairs, cuts, markers):
    rows = 2 * mine.shape[0]
    flat = [x for pair in pairs for x in pair]
    outs = [shape((rows, 3 * LANES), BF16), shape((3 * LANES, D), BF16), *join_shapes(pairs, cuts)]
    found = call(
        partial(project_body, base, masks, cuts),
        [scalars, mine, other, lines, *parts, *flat],
        outs,
        [pltpu.VMEM((3 * LANES, D), F32)],
        24,
        "project",
        markers=markers,
    )
    return found[0], found[1], found[2:]


def branch_body(base, masks, scalars, keep, across_t, *refs):
    parts, refs = refs[: len(masks)], refs[len(masks) :]
    sent_a, sent_b, kept, own_out, across_out, weight = refs
    width = own_out.shape[1]

    def put(place, chunk):
        rows = chunk.shape[0]
        start = pl.multiple_of(place * rows, 16) if base is not None else place * rows
        for group in range(2):
            weight[group, pl.ds(start, rows), :] = chunk[:, group * width : (group + 1) * width]

    spread(scalars, base, parts, masks, put)
    side = scalars[SIDE]
    own_out[...] = weight[side]
    across_out[...] = weight[1 - side]
    piece = kept.shape[0]
    def rows_of(columns):
        return mm(keep[:, columns].T, own_out[...], NT) + mm(across_t[:, columns].T, across_out[...], NT)

    half = piece // 2
    sent_a[...] = rows_of(slice(piece, piece + half)).astype(BF16)
    sent_b[...] = rows_of(slice(piece + half, 2 * piece)).astype(BF16)
    kept[...] = rows_of(slice(0, piece))


def middle_norm_body(scalars, tokens, kept, arrived_a, arrived_b, lines, middle, normed_a, normed_b):
    bias, gain, shift = vector_row(lines, 6), vector_row(lines, 2), vector_row(lines, 3)
    half = normed_a.shape[0]
    step = min(128, half)
    for lead, arrived, normed in ((0, arrived_a, normed_a), (half, arrived_b, normed_b)):
        for start in range(0, half, step):
            rows = slice(lead + start, lead + start + step)
            values = tokens[rows, :].astype(F32) + kept[rows, :]
            values = values + arrived[start : start + step, :].astype(F32) + bias
            middle[rows, :] = values
            unit, _ = row_norm(values)
            normed[start : start + step, :] = (unit * gain + shift).astype(BF16)


def middle_norm(scalars, tokens, kept, arrived, lines):
    piece = tokens.shape[0]
    return call(
        middle_norm_body,
        [scalars, tokens, kept, *arrived, lines],
        [shape((piece, D), F32), shape((piece // 2, D), BF16), shape((piece // 2, D), BF16)],
        [],
        16,
        "middle_norm",
    )


def branch(scalars, keep, across_t, base, parts, masks, markers):
    width, rows = keep.shape
    piece = rows // 2
    return call(
        partial(branch_body, base, masks),
        [scalars, keep, across_t, *parts],
        [shape((piece // 2, D), BF16)] * 2
        + [shape((piece, D), F32), shape((D, width), BF16), shape((D, width), BF16)],
        [pltpu.VMEM((2, D, width), BF16)],
        24,
        "branch",
        markers=markers,
    )


MLP_ROWS = 256
MLP_LANES = 512


def feed_body(
    bases, masks, count, scalars, own_a, own_b, other_a, other_b, grad_own, grad_other, lines, *refs
):
    parts, refs = refs[: sum(map(len, masks))], refs[sum(map(len, masks)) :]
    activated, grad_hidden, normed_sent, normed_kept, out_sent, out_kept, sums, pair, grad_pair = refs[:9]
    expand, contract = refs[9:]
    half = expand.shape[0]
    piece = grad_own.shape[0]
    for lead, rows in enumerate((own_a, own_b, other_a, other_b)):
        pair[lead * (piece // 2) : (lead + 1) * (piece // 2), :] = rows[...]
    grad_pair[:piece, :] = grad_own[...]
    grad_pair[piece:, :] = grad_other[...]
    bias = lines_row(lines, 8 * (D // 128) + scalars[CORE] * (half // 128), half // 128)

    def put_expand(index):
        def put(place, chunk):
            rows = chunk.shape[0]
            start = place * 2 * rows + index * rows
            if bases[index] is not None:
                start = pl.multiple_of(start, 16)
            expand[pl.ds(start, rows), :] = chunk

        return put

    def put_contract(place, chunk):
        rows = chunk.shape[0]
        start = pl.multiple_of(place * rows, 16) if bases[-1] is not None else place * rows
        contract[pl.ds(start, rows), :] = chunk

    taken = 0
    for index, own_masks in enumerate(masks):
        put = put_contract if index == len(masks) - 1 else put_expand(index)
        spread(scalars, bases[index], parts[taken : taken + len(own_masks)], own_masks, put)
        taken += len(own_masks)
    sums[...] = jnp.zeros_like(sums)
    step = min(MLP_ROWS, piece)

    def block(start, lead, normed_out, contract_out):
        rows = pl.ds(start, step)
        target = pl.ds(pl.multiple_of(lead + start, step), step)
        normed = pair[target, :]
        grad = grad_pair[target, :]
        back = jnp.zeros((step, D), F32)
        result = jnp.zeros((step, D), F32)
        for lanes in range(0, half, MLP_LANES):
            span = slice(lanes, lanes + MLP_LANES)
            expanded = mm(normed, expand[span, :], NT) + bias[:, span]
            squared = expanded * expanded
            bent = jnp.tanh(ROOT_TWO_OVER_PI * (expanded + 0.044715 * (expanded * squared)))
            rise = 0.5 * (1.0 + bent)
            act = (expanded * rise).astype(BF16)
            slope = rise + (0.5 * ROOT_TWO_OVER_PI) * expanded * (1.0 - bent * bent) * (
                1.0 + (3.0 * 0.044715) * squared
            )
            hidden = (mm(grad, contract[:, span], NN) * slope).astype(BF16)
            activated[target, span] = act
            grad_hidden[target, span] = hidden
            sums[0:1, span] += jnp.sum(hidden.astype(F32), axis=0, keepdims=True)
            back = back + mm(hidden, expand[span, :], NN)
            result = result + mm(act, contract[:, span], NT)
        normed_out[rows, :] = back.astype(normed_out.dtype)
        contract_out[rows, :] = result.astype(contract_out.dtype)

    def own_block(i, carry):
        start = pl.multiple_of(i * step, step)
        block(start, 0, normed_kept, out_kept)
        return carry

    def other_block(i, carry):
        start = pl.multiple_of(i * step, step)
        block(start, piece, normed_sent, out_sent)
        return carry

    lax.fori_loop(0, piece // step, other_block, 0)
    lax.fori_loop(0, piece // step, own_block, 0)


def feed_forward(scalars, normed, grads, lines, bases, parts, masks):
    piece = grads[0].shape[0]
    half = FF // 2
    flat = [x for group in parts for x in group]
    return call(
        partial(feed_body, bases, masks, len(flat)),
        [scalars, *normed, *grads, lines, *flat],
        [
            shape((2 * piece, half), BF16),
            shape((2 * piece, half), BF16),
            shape((piece, D), BF16),
            shape((piece, D), F32),
            shape((piece, D), BF16),
            shape((piece, D), F32),
            shape((8, half), F32),
            shape((2 * piece, D), BF16),
            shape((2 * piece, D), BF16),
        ],
        [pltpu.VMEM((half, D), BF16), pltpu.VMEM((D, half), BF16)],
        36,
        "feed_forward",
    )


def head_grads_body(scalars, own, other, weight_own, weight_across, keep, sent):
    piece = own.shape[0]
    for matrix, out in ((weight_across, sent), (weight_own, keep)):
        for place, rows in enumerate((own, other)):
            features = mm(rows[...], matrix[...], NN).T.astype(BF16)
            out[:, place * piece : (place + 1) * piece] = features


def head_grads(scalars, grads, weight_own, weight_across):
    piece = grads[0].shape[0]
    outs = [shape((weight_own.shape[1], 2 * piece), BF16)] * 2
    return call(head_grads_body, [scalars, *grads, weight_own, weight_across], outs, [], 24, "head_gradients")


def output_weight_body(scalars, own, other, keep, across_t, out, stacked):
    side = scalars[SIDE]
    piece = own.shape[0]
    width = keep.shape[0]
    for place, features in ((side, keep), (1 - side, across_t)):
        product = mm(features[:, :piece], own[...], NN) + mm(features[:, piece:], other[...], NN)
        stacked[pl.ds(pl.multiple_of(place * width, 8), width), :] = product
    out[...] = stacked[...].T.astype(out.dtype)


def output_weight_grad(scalars, grads, keep, across_t, markers):
    width = keep.shape[0]
    return call(
        output_weight_body,
        [scalars, *grads, keep, across_t],
        [shape((D, 2 * width), BF16)],
        [pltpu.VMEM((2 * width, D), F32)],
        24,
        "output_weight_gradient",
        markers=markers,
    )[0]


def input_weight_body(aligned, rows_of_devices, scalars, grads, mine, other, *refs):
    total = refs[-1]
    piece = mine.shape[0] // 2
    step = min(MLP_ROWS, piece)
    total[...] = jnp.zeros_like(total)
    for place, (source, lead) in enumerate(((mine, 0), (other, 0), (mine, piece), (other, piece))):
        for start in range(0, piece, step):
            rows = grads[place * piece + start : place * piece + start + step, :]
            total[...] += mm(rows.T, source[lead + start : lead + start + step, :], NN)
    if not aligned:
        natural = refs[0]
        for kind in range(3):
            natural[kind] = total[kind * LANES : kind * LANES + natural.shape[1], :]
        return
    rows = refs[0].shape[1]
    half = D // 2
    row = scalars[ROW]
    for part, position in enumerate((0, 1)):
        sent, kept = refs[2 * part], refs[2 * part + 1]
        columns = slice(part * half, (part + 1) * half)
        low = 1 << position
        bit = (row >> position) & 1
        count = rows_of_devices // 2
        for kind in range(3):
            for e in range(count):
                base = (e // low) * 2 * low + e % low
                for out, chosen in ((sent, 1 - bit), (kept, bit)):
                    start = kind * LANES + (base + chosen * low) * rows
                    block = total[pl.ds(pl.multiple_of(start, 8), rows), columns]
                    out[kind * count + e] = block.astype(out.dtype)


def input_weight_grad(scalars, grads, mine, other, rows_of_devices, block):
    aligned = block % 8 == 0
    part = (3 * rows_of_devices // 2, block, D // 2)
    outs = [shape(part, BF16), shape(part, F32)] * 2
    if not aligned:
        outs = [shape((3, block * rows_of_devices, D), F32)]
    return call(
        partial(input_weight_body, aligned, rows_of_devices),
        [scalars, grads, mine, other],
        outs,
        [pltpu.VMEM((3 * LANES, D), F32)],
        32,
        "input_weight_gradient",
    )


def first_grads_body(places, scalars, grads, weight, *refs):
    *far, sent, kept = refs
    piece = sent.shape[0]
    if far:
        far_kept, far_arrived, reduced = far
        reduced[...] = (far_kept[...] + far_arrived[...].astype(F32)).astype(BF16)
    for place, out in zip(places, (sent, kept)):
        out[...] = mm(grads[place * piece : (place + 1) * piece, :], weight[...], NN).astype(out.dtype)


def first_grads(scalars, grads, weight, places, far=(), markers=()):
    piece = grads.shape[0] // 4
    outs = [shape((piece, D), BF16), shape((piece, D), F32)]
    return call(
        partial(first_grads_body, places),
        [scalars, grads, weight, *far],
        outs[:1] * bool(far) + outs,
        [],
        20,
        "first_norm_gradient",
        markers=markers,
    )


def payload_body(hidden_rows, scalars, left, right, expand, contract, first, middle, heads, hidden, out):
    six = D // 128
    out[...] = jnp.zeros_like(out)
    out[: 2 * six, :] = first[: 2 * six, :]
    out[2 * six : 4 * six, :] = middle[: 2 * six, :]
    out[6 * six : 8 * six, :] = middle[2 * six : 4 * six, :]
    here = scalars[HERE]
    for line in range(2):
        row = heads[line : line + 1, :]
        row = jnp.where(here % 2 == 1, pltpu.roll(row, HD, 1), row)
        start = (4 + line) * six + (3 * here) // 2
        for part in range(2):
            out[pl.ds(start + part, 1), :] = row[:, part * 128 : (part + 1) * 128]
    for part in range(hidden_rows):
        line = 8 * six + scalars[CORE] * hidden_rows + part
        out[pl.ds(line, 1), :] = hidden[0:1, part * 128 : (part + 1) * 128]
    total = jnp.zeros((1, 1), F32)
    for gradients in (left, right, expand, contract):
        for i in range(gradients.shape[0]):
            values = gradients[i]
            rows = jnp.sum(values * values, axis=1, keepdims=True)
            total += jnp.sum(rows, axis=0, keepdims=True)
    lane = lax.broadcasted_iota(jnp.int32, (1, 128), 1)
    out[VECTOR_ROWS : VECTOR_ROWS + 1, :] = jnp.where(lane == 0, total, 0.0)


def make_payload(scalars, gradients, first, middle, heads, hidden):
    return call(
        partial(payload_body, hidden.shape[1] // 128),
        [scalars, *gradients, first, middle, heads, hidden],
        [shape((VECTOR_ROWS + 8, 128), F32)],
        [],
        16,
        "payload",
    )[0]


def reduce_body(plans, scalars, *refs):
    count = 2 * sum(len(sources) for sources, _ in plans)
    ins, outs = list(refs[:count]), list(refs[count:])
    for sources, split in plans:
        terms = []
        column = 0
        for full in sources:
            kept, arrived = ins.pop(0), ins.pop(0)
            columns = slice(column, column + arrived.shape[2])
            column += arrived.shape[2]

            def total(index, kept=kept, arrived=arrived, full=full):
                source = index
                if full is not None:
                    which, shift, size = full
                    bit = (scalars[which] >> shift) & 1
                    source = (index // size) * 2 * size + bit * size + index % size
                return kept[source].astype(F32) + arrived[index].astype(F32)

            terms.append((columns, total))
        if split is None:
            out = outs.pop(0)

            def whole(m, carry, out=out, terms=terms):
                for columns, total in terms:
                    out[m, :, columns] = total(m)
                return carry

            lax.fori_loop(0, out.shape[0], whole, 0)
        else:
            which, shift, size = split
            sent_out, kept_out = outs.pop(0), outs.pop(0)

            def halves(m, carry, sent_out=sent_out, kept_out=kept_out, terms=terms):
                bit = (scalars[which] >> shift) & 1
                base = (m // size) * 2 * size + m % size
                for columns, total in terms:
                    kept_out[m, :, columns] = total(base + bit * size)
                    sent_out[m, :, columns] = total(base + (1 - bit) * size).astype(BF16)
                return carry

            lax.fori_loop(0, kept_out.shape[0], halves, 0)


HEAD_LANES = LANES


VECTOR_ROWS = (8 * D + FF) // 128


def row_norm(values):
    mean = jnp.mean(values, axis=1, keepdims=True)
    centered = values - mean
    variance = jnp.mean(centered * centered, axis=1, keepdims=True)
    inverse = lax.rsqrt(variance + NORM_EPS)
    return centered * inverse, inverse


def norm_input_gradient(upstream, values, gain):
    unit, inverse = row_norm(values)
    scaled = upstream * gain
    first = jnp.mean(scaled, axis=1, keepdims=True)
    second = jnp.mean(scaled * unit, axis=1, keepdims=True)
    return inverse * (scaled - first - unit * second), unit


def stack_rows(sums, rows):
    for place, row in enumerate(rows):
        total = jnp.sum(row, axis=0, keepdims=True)
        for part in range(D // 128):
            line = place * (D // 128) + part
            sums[line : line + 1, :] += total[:, part * 128 : (part + 1) * 128]


def middle_body(own, arrived, middle, cotangent, lines, grad_mid, grad_branch, sums):
    @pl.when(pl.program_id(0) == 0)
    def _():
        sums[...] = jnp.zeros_like(sums)

    upstream = own[...] + arrived[...].astype(F32)
    passed, unit = norm_input_gradient(upstream, middle[...], vector_row(lines, 2))
    outer = cotangent[...].astype(F32)
    total = outer + passed
    rounded = total.astype(BF16)
    grad_mid[...] = total
    grad_branch[...] = rounded
    stack_rows(sums, [upstream * unit, upstream, rounded.astype(F32), outer])


def first_body(own, arrived, across, tokens, grad_mid, lines, input_grad, sums):
    @pl.when(pl.program_id(0) == 0)
    def _():
        sums[...] = jnp.zeros_like(sums)

    upstream = own[...] + arrived[...].astype(F32) + across[...].astype(F32)
    passed, unit = norm_input_gradient(upstream, tokens[...].astype(F32), vector_row(lines, 0))
    input_grad[...] = (grad_mid[...] + passed).astype(BF16)
    stack_rows(sums, [upstream * unit, upstream])


def norm_backward(body, arrays, lines, outputs, name):
    rows = arrays[0].shape[0]
    step = min(128, rows)
    tile = pl.BlockSpec((step, D), lambda i: (i, 0))
    row = pl.BlockSpec(lines.shape, lambda i: (0, 0))
    sums = pl.BlockSpec((24, 128), lambda i: (0, 0))
    return pl.pallas_call(
        body,
        grid=(rows // step,),
        out_shape=tuple(jax.ShapeDtypeStruct((rows, D), kind) for kind in outputs)
        + (jax.ShapeDtypeStruct((24, 128), F32),),
        in_specs=[tile] * len(arrays) + [row],
        out_specs=tuple(tile for _ in outputs) + (sums,),
        compiler_params=pltpu.CompilerParams(vmem_limit_bytes=24 * 2**20),
        cost_estimate=cost(name),
        name=name,
    )(*arrays, lines)


def moments_body(*refs):
    payload, refs = refs[0], refs[1:]
    grads, firsts, seconds, masters = refs[0:5], refs[5:10], refs[10:15], refs[15:20]
    first_outs, second_outs, direction_outs = refs[20:25], refs[25:30], refs[30:35]
    squares = refs[35]
    vector = payload[0:VECTOR_ROWS, :]
    total = payload[VECTOR_ROWS : VECTOR_ROWS + 1, 0:1] + jnp.sum(
        jnp.sum(vector * vector, axis=1, keepdims=True), axis=0, keepdims=True
    )
    clip = jnp.minimum(1.0, 1.0 / jnp.sqrt(total))
    correction = 1.0 - 0.5**STEP
    lane = lax.broadcasted_iota(jnp.int32, squares.shape, 1)
    row = lax.broadcasted_iota(jnp.int32, squares.shape, 0)
    found = jnp.zeros(squares.shape, F32)
    for place in range(5):
        gradient = grads[place][...] if place < 4 else vector
        master = masters[place][...]
        clipped = gradient * clip
        first_new = 0.5 * firsts[place][...] + 0.5 * clipped
        second_new = 0.5 * seconds[place][...] + 0.5 * clipped * clipped
        direction = (
            first_new / correction / (jnp.sqrt(second_new / correction) + ADAM_EPS)
            + DECAY_RATE * master
        )
        first_outs[place][...] = first_new
        second_outs[place][...] = second_new
        if place < 4:
            direction_outs[place][...] = direction
            for offset, values in ((0, direction), (4, master)):
                square = jnp.sum(
                    jnp.sum(values * values, axis=1, keepdims=True), axis=0, keepdims=True
                )
                found = found + jnp.where((lane == place + offset) & (row == 0), square, 0.0)
        else:
            direction_outs[place][...] = master - VECTOR_RATE * direction
    squares[...] = found


def moments_step(payload, grads, firsts, seconds, masters):
    vmem = pl.BlockSpec(memory_space=pltpu.VMEM)
    shapes = [jax.ShapeDtypeStruct(master.shape, F32) for master in masters]
    outs = pl.pallas_call(
        moments_body,
        out_shape=tuple(shapes * 3) + (jax.ShapeDtypeStruct((8, 128), F32),),
        in_specs=[vmem] * 21,
        out_specs=(vmem,) * 16,
        compiler_params=pltpu.CompilerParams(vmem_limit_bytes=60 * 2**20),
        cost_estimate=cost("moments"),
        name="moments",
    )(payload, *grads, payload, *firsts, *seconds, *masters)
    return outs[0:5], outs[5:10], outs[10:15], outs[15]


def weights_body(*refs):
    squares, refs = refs[0], refs[1:]
    directions, masters, outs, lows = refs[0:4], refs[4:8], refs[8:12], refs[12:16]
    norms = refs[16]
    norms[...] = jnp.zeros_like(norms)
    weight = jnp.sqrt(squares[0:1, 4:8])
    update = jnp.sqrt(squares[0:1, 0:4])
    for place in range(4):
        ratio = MATRIX_RATE * (weight[:, place : place + 1] / update[:, place : place + 1])
        new = masters[place][...] - ratio * directions[place][...]
        outs[place][...] = new
        lows[place][...] = new.astype(BF16)
    norms[0:1, 0:4] = weight
    norms[1:2, 0:4] = update


def weights_step(squares, directions, masters):
    vmem = pl.BlockSpec(memory_space=pltpu.VMEM)
    outs = pl.pallas_call(
        weights_body,
        out_shape=tuple(jax.ShapeDtypeStruct(m.shape, F32) for m in masters)
        + tuple(jax.ShapeDtypeStruct(m.shape, BF16) for m in masters)
        + (jax.ShapeDtypeStruct((8, 128), F32),),
        in_specs=[vmem] * 9,
        out_specs=(vmem,) * 9,
        compiler_params=pltpu.CompilerParams(vmem_limit_bytes=60 * 2**20),
        cost_estimate=cost("weights"),
        name="weights",
    )(squares, *directions, *masters)
    return outs[0:4], outs[4:8], outs[8]


BOTH = ("batch", "head")
PARTNER = 1
ACROSS = 2


def dot(a, b, dims):
    return lax.dot_general(a, b, (dims, ((), ())), preferred_element_type=F32)


def swap(values, axis, mask):
    size = lax.axis_size(axis)
    return lax.ppermute(values, axis, [(place, place ^ mask) for place in range(size)])


def partner(values):
    return swap(values, "head", PARTNER)


def across(values):
    return swap(values, "head", ACROSS)


def batch_masks():
    return [1 << bit for bit in range((lax.axis_size("batch") - 1).bit_length())][::-1]


class Chain:
    def __init__(self, scalars, chunk, order, chips):
        self.scalars, self.values, self.order, self.chips = scalars, chunk[None], list(order), chips
        self.masks, self.flip, self.arrived = [0], 0, None

    def start(self):
        axis, mask = self.order.pop(0)
        self.flip = mask if not self.chips else (2 * mask if axis == "batch" else 1)
        self.arrived = swap(self.values, axis, mask)

    def pair(self):
        return self.values, self.arrived

    def take(self, joined):
        self.values = joined
        self.masks = self.masks + [mask ^ self.flip for mask in self.masks]
        self.arrived = None
        if self.order:
            self.start()

    def drain(self, left):
        while len(self.order) > left:
            self.take(join(self.scalars, [self.pair()], [0])[0])

    def halves(self, joined, orders):
        chains = []
        for values, order in zip(joined, orders):
            chain = Chain(self.scalars, values[0], order, self.chips)
            chain.values = values
            chain.masks = self.masks + [mask ^ self.flip for mask in self.masks]
            chain.start()
            chains.append(chain)
        return chains

    def parts(self, multiple, kinds=1):
        rows = self.values.shape[1] // kinds
        source = CHIP if self.chips else ROW
        arrays, masks = [self.values], [self.masks]
        if self.arrived is not None:
            arrays.append(self.arrived)
            masks.append([mask ^ self.flip for mask in self.masks])
        if rows % multiple == 0:
            return source, arrays, masks
        chunks = [array[r] for array in arrays for r in range(array.shape[0])]
        order = [mask for group in masks for mask in group]
        count = len(order)
        natural = jnp.stack([chunks[order.index(place)] for place in range(count)])
        size = 1
        while size < count:
            cut = natural.reshape((-1, 2, size) + natural.shape[1:])
            flipped = jnp.concatenate([cut[:, 1:], cut[:, :1]], axis=1)
            cut = jnp.where((self.scalars[source] & size) != 0, flipped, cut)
            natural = cut.reshape(natural.shape)
            size *= 2
        natural = natural.reshape(count, kinds, rows, -1).transpose(1, 0, 2, 3)
        return None, [natural.reshape(1, kinds * count * rows, -1)], [[0]]


def join_all(scalars, chains, extra=(), markers=()):
    pairs = [chain.pair() for chain in chains] + list(extra)
    joined = join(scalars, pairs, [0] * len(pairs), markers)
    for chain, values in zip(chains, joined):
        chain.take(values)
    return joined[len(chains) :]


def bit_source(bit):
    axis, mask = bit
    return (ROW, mask.bit_length() - 1) if axis == "batch" else (SIDE, 0)


class Reduce:
    def __init__(self, bits, order, *values):
        self.left, self.order, self.values, self.full = list(bits), list(order), values, None

    def split(self):
        bit = self.order.pop(0)
        size = 1 << (len(self.left) - 1 - self.left.index(bit))
        self.left.remove(bit)
        self.bit = bit
        return (*bit_source(bit), size)

    def begin(self, scalars):
        self.full = self.split()
        self.sources = []
        for values in self.values:
            self.send(scalars, values)

    def send(self, scalars, values):
        which, shift, size = self.full
        bit = (scalars[which] >> shift) & 1
        rows = values.shape[1:]
        cut = values.reshape((-1, 2, size) + rows)
        sent = lax.dynamic_index_in_dim(cut, 1 - bit, 1, keepdims=False).reshape((-1,) + rows)
        self.sources.append((values, swap(sent.astype(BF16), *self.bit)))

    def begin_with(self, sent, kept):
        self.full = None
        self.sources = [(kept, swap(sent, *self.bit))]

    @property
    def kept(self):
        return self.sources[0][0]


def reduce_all(scalars, chains, markers=()):
    plans, inputs, outs = [], [scalars], []
    for chain in chains:
        full = chain.full
        for source in chain.sources:
            inputs += source
        plan = chain.split() if chain.order else None
        plans.append(([full] * len(chain.sources), plan))
        count, rows, _ = chain.sources[0][1].shape
        columns = sum(arrived.shape[2] for _, arrived in chain.sources)
        if plan is None:
            outs.append(shape((count, rows, columns), F32))
        else:
            outs.append(shape((count // 2, rows, columns), BF16))
            outs.append(shape((count // 2, rows, columns), F32))
    found = list(call(partial(reduce_body, plans), inputs, outs, [], 40, "add_arrived", markers=markers))
    for chain, (_, plan) in zip(chains, plans):
        if plan is None:
            chain.values = found.pop(0)
        else:
            sent, kept = found.pop(0), found.pop(0)
            chain.begin_with(sent, kept)


def all_sum(values):
    for mask in (PARTNER, ACROSS):
        values = values + swap(values, "head", mask)
    masks = batch_masks()[::-1]
    if len(masks) % 2:
        values = values + swap(values, "batch", masks[0])
        masks = masks[1:]
    for low, high in zip(masks[::2], masks[1::2]):
        near = values + swap(values, "batch", low)
        far = swap(values, "batch", high) + swap(values, "batch", low | high)
        values = near + far
    return values


def block_permutation(slot, to_owner):
    rows, heads = lax.axis_size("batch"), lax.axis_size("head")
    total = rows * heads
    pairs = []
    for owner in range(total):
        place = (3 * owner + slot) % total
        holder = (place % rows) * heads + place // rows
        pairs.append((holder, owner) if to_owner else (owner, holder))
    return pairs


def holder_place():
    return lax.axis_size("batch") * lax.axis_index("head") + lax.axis_index("batch")


def blocks_to_holders(shard):
    blocks = shard.reshape(3, -1, D)
    return [lax.ppermute(blocks[slot], BOTH, block_permutation(slot, False)) for slot in range(3)]


def blocks_to_owners(blocks):
    total = lax.axis_size("batch") * lax.axis_size("head")
    place = holder_place()
    arrived = []
    for slot in range(3):
        kind = ((slot + 3 * total - place) * total) % 3
        sent = lax.dynamic_index_in_dim(blocks, kind, 0, keepdims=False)
        arrived.append(lax.ppermute(sent, BOTH, block_permutation(slot, True)))
    return jnp.concatenate(arrived, axis=0)


def on_device(
    tokens,
    cotangent,
    lengths,
    input_weight,
    output_weight,
    expand_weight,
    contract_weight,
    vector_params,
    input_first,
    input_second,
    output_first,
    output_second,
    expand_first,
    expand_second,
    contract_first,
    contract_second,
    vector_first,
    vector_second,
):
    rows_of_devices = lax.axis_size("batch")
    head_count = lax.axis_size("head")
    chips = rows_of_devices * head_count // 2
    here = lax.axis_index("head")
    core = here % 2
    side = here // 2
    width = D // head_count
    heads = width // HD
    piece = tokens.shape[0]
    docs = lengths.shape[1]
    hidden_block = FF // (2 * chips)
    half = FF // 2
    out_rows = output_weight.shape[0]
    total_devices = rows_of_devices * head_count
    batch_bits = [("batch", mask) for mask in batch_masks()]
    far, near = batch_bits[:-1], batch_bits[-1]
    side_bit = ("head", ACROSS)
    bits = batch_bits + [side_bit]
    bias_contract = vector_params[7 * D : 8 * D]

    def by_core(mine, other, axis):
        high = core == 1
        return jnp.stack([jnp.where(high, other, mine), jnp.where(high, mine, other)], axis=axis)

    def pick(values, index, axis):
        return lax.dynamic_index_in_dim(values, index, axis, keepdims=False)

    scalars, sequences = Places(), Places(lengths)
    lines = vector_params.reshape(VECTOR_ROWS, 128)

    *in_blocks, expand_low, output_mine, output_cut, normed_own = prepare(
        scalars, input_weight, expand_weight, output_weight, tokens, lines
    )
    in_arrived = [
        lax.ppermute(block, BOTH, block_permutation(slot, False)) for slot, block in enumerate(in_blocks)
    ]
    expands = Chain(scalars, expand_low, far, True)
    expands.start()
    normed_across = across(normed_own)
    output_other = partner(output_cut)
    contract_cut = contract_weight.astype(BF16).reshape(out_rows, chips, 2, hidden_block)
    contract_other = partner(pick(contract_cut, 1 - core, 2))
    contract_shard = by_core(pick(contract_cut, core, 2), contract_other, 0).reshape(2 * out_rows, half)
    output_shard = by_core(output_mine, output_other, 0).reshape(2 * out_rows, 2 * width)
    contracts = Chain(scalars, contract_shard, [near, side_bit] + far, True)
    contracts.start()

    kinds = block_kinds(scalars, in_arrived, total_devices).reshape(-1, D)
    inputs = Chain(scalars, kinds, batch_bits, False)
    outputs = Chain(scalars, output_shard, far + [near, side_bit], True)
    inputs.start()
    outputs.start()
    inputs.drain(2)
    outputs.drain(3)
    join_all(scalars, [inputs, outputs, contracts], (), (expands.arrived,))
    expands.drain(1)
    (normed_mine,) = join_all(
        scalars, [inputs, outputs, contracts, expands], [(normed_own, normed_across)]
    )
    contracts.drain(1)
    normed_other = partner(normed_mine)

    def cores_first(vectors):
        hidden = vectors[:, 8 * D :].reshape(-1, chips, 2, hidden_block).transpose(0, 2, 1, 3)
        return jnp.concatenate([vectors[:, : 8 * D], hidden.reshape(-1, FF)], axis=1).reshape(-1, VECTOR_ROWS, 128)

    def cores_back(rows):
        vectors = rows.reshape(-1, 8 * D + FF)
        hidden = vectors[:, 8 * D :].reshape(-1, 2, chips, hidden_block).transpose(0, 2, 1, 3)
        return jnp.concatenate([vectors[:, : 8 * D], hidden.reshape(-1, FF)], axis=1)

    vector_state = cores_first(jnp.stack([vector_first, vector_second, vector_params]))
    projected, weight_in, joined = project(
        scalars,
        normed_mine,
        normed_other,
        lines,
        *inputs.parts(8, 3),
        [outputs.pair(), expands.pair()],
        [0, 2],
        (vector_state,),
    )
    outputs.take(joined[0])
    expands = expands.halves(joined[1:], ([near, side_bit], [side_bit, near]))

    keep_t, send_t, logs = attention_forward(sequences, projected, heads, 0, docs, piece, [], [])[0]
    across_t = across(send_t)
    join_all(scalars, [*expands, contracts, outputs], (), (keep_t,))
    *branch_sent, branch_kept, output_own, output_across = branch(
        scalars, keep_t, across_t, *outputs.parts(16), (contracts.values,)
    )
    resid_mid, *normed_two = middle_norm(
        scalars, tokens, branch_kept, [partner(rows) for rows in branch_sent], lines
    )
    arrived_two = [partner(rows) for rows in normed_two]
    cotangent_other = partner(cotangent)

    found = [chain.parts(16) for chain in (*expands, contracts)]
    activated, grad_hidden, normed_sent, normed_kept, out_sent, out_kept, hidden_sums, *pairs = feed_forward(
        scalars,
        (*normed_two, *arrived_two),
        (cotangent, cotangent_other),
        vector_state[2],
        [part[0] for part in found],
        [part[1] for part in found],
        [part[2] for part in found],
    )
    normed_arrived = partner(normed_sent)
    out_arrived = partner(out_sent)
    block_out = (resid_mid + out_kept + out_arrived.astype(F32) + bias_contract).astype(BF16)

    normed_pair, cotangent_pair = pairs
    expand_sum = Reduce(
        bits,
        [near] + far[-1:] + [side_bit] + far[:-1][::-1],
        dot(grad_hidden, normed_pair, ((0,), (0,))).astype(BF16).reshape(chips, hidden_block, D),
    )
    expand_sum.begin(scalars)
    grad_mid, grad_branch, middle_sums = norm_backward(
        middle_body,
        [normed_kept, normed_arrived, resid_mid, cotangent],
        lines,
        (F32, BF16),
        "middle_gradient",
    )
    grads = (grad_branch, partner(grad_branch))
    contract_total = dot(cotangent_pair, activated, ((0,), (0,))).astype(BF16)
    contract_sum = Reduce(
        bits, far[-1:] + [near, side_bit] + far[:-1][::-1], contract_total.reshape(chips, 2 * out_rows, half)
    )
    contract_sum.begin(scalars)

    grad_keep_t, grad_sent_t = head_grads(scalars, grads, output_own, output_across)
    grad_arrived_t = across(grad_sent_t)
    output_total = output_weight_grad(scalars, grads, keep_t, across_t, (grad_sent_t,))
    contract_sum.send(scalars, output_total.reshape(chips, 2 * out_rows, 2 * width))
    sums = [expand_sum, contract_sum]
    grad_heads, head_sums = attention_backward(
        sequences, projected, (keep_t, send_t), (grad_keep_t, grad_arrived_t), logs, heads, 0, docs, piece,
        [chain.sources[-1][0] for chain in sums],
    )

    far_sent, far_kept = first_grads(scalars, grad_heads, weight_in, (3, 2))
    far_arrived = partner(far_sent)
    in_found = input_weight_grad(
        scalars, grad_heads, normed_mine, normed_other, rows_of_devices, D // total_devices
    )
    in_orders = ([near] + far[::-1], far[::-1] + [near])
    if len(in_found) == 4:
        in_sums = [Reduce(batch_bits, order) for order in in_orders]
        for part, sent, kept in zip(in_sums, in_found[::2], in_found[1::2]):
            part.split()
            part.begin_with(sent, kept)
    else:
        natural = in_found[0].reshape(3 * rows_of_devices, -1, D)
        in_sums = [
            Reduce(batch_bits, in_orders[0], natural[..., : D // 2]),
            Reduce(batch_bits, in_orders[1], natural[..., D // 2 :]),
        ]
        for part in in_sums:
            part.begin(scalars)
    reduced_far, near_sent, near_kept = first_grads(
        scalars, grad_heads, weight_in, (1, 0), (far_kept, far_arrived), (in_sums[0].kept,)
    )
    first_arrived = across(reduced_far)
    near_arrived = partner(near_sent)
    reduce_all(scalars, sums, (reduced_far,))
    while in_sums[0].order:
        reduce_all(scalars, in_sums, (sums[0].kept,))
        if sums[0].order:
            reduce_all(scalars, sums, (in_sums[0].kept,))
    while sums[0].order:
        reduce_all(scalars, sums)
    reduce_all(scalars, in_sums, (first_arrived,))
    reduce_all(scalars, sums, (in_sums[0].values,))
    expand_grad = expand_sum.values.reshape(hidden_block, D)
    contract_mixed = contract_sum.values[0, :, :half]
    output_mixed = contract_sum.values[0, :, half:]
    in_blocks = jnp.concatenate([part.values for part in in_sums], axis=-1)

    def columns_other(mixed, parts):
        cut = mixed.reshape(2, out_rows, parts, -1)
        return pick(cut, core, 0), partner(pick(cut, 1 - core, 0))

    contract_grad = by_core(*columns_other(contract_mixed, chips), 2).reshape(out_rows, -1)
    output_grad = by_core(*columns_other(output_mixed, 2), 2).reshape(out_rows, -1)
    input_piece_grad = blocks_to_owners(in_blocks)
    input_grad, first_sums = norm_backward(
        first_body,
        [near_kept, near_arrived, first_arrived, tokens, grad_mid],
        lines,
        (BF16,),
        "first_gradient",
    )

    masters = (input_weight, output_weight, expand_weight, contract_weight)
    gradients = [part.values for part in (*in_sums, expand_sum, contract_sum)]
    payload = all_sum(
        make_payload(scalars, gradients, first_sums, middle_sums, head_sums, hidden_sums)
    )
    vector_grads = payload[:VECTOR_ROWS]
    grad_norm = jnp.sqrt(payload[VECTOR_ROWS, 0] + jnp.sum(vector_grads * vector_grads))
    first_new, second_new, directions, squares = moments_step(
        payload,
        (input_piece_grad, output_grad, expand_grad, contract_grad),
        (input_first, output_first, expand_first, contract_first, vector_state[0]),
        (input_second, output_second, expand_second, contract_second, vector_state[1]),
        (*masters, vector_state[2]),
    )
    squares = all_sum(squares)
    vector_news = cores_back(jnp.stack([first_new[4], second_new[4], directions[4]]))
    news, lows, norms = weights_step(squares, directions[:4], masters)
    results = []
    for position in range(4):
        results += [first_new[position], second_new[position], news[position], lows[position]]
    return (
        block_out,
        input_grad,
        grad_norm,
        norms[:2, :4].reshape(8),
        *results,
        vector_news[0],
        vector_news[1],
        vector_news[2],
    )


def solution(mesh):
    split = P(BOTH, None)
    return jax.shard_map(
        on_device,
        mesh=mesh,
        in_specs=(split, split, P("batch", None)) + (split,) * 4 + (P(),) + (split,) * 8 + (P(), P()),
        out_specs=(split, split, P(), P()) + (split,) * 16 + (P(), P(), P()),
        check_vma=False,
    )
```

time: 466 us -> 365 us (0.78)
  Pallas kernels: 42.9 us -> 104 us
  other arithmetic: 68 us -> 9.59 us
  waiting for transfers between devices: 170 us -> 125 us
  matrix products: 48.2 us -> 8.1 us
  local copies, waits for them, and re-layouts: 43.1 us -> 26.6 us
  starting transfers between devices: 73.4 us -> 84.3 us
  between operations: 13.1 us -> 4.44 us
    pallas_call x2 -> x28, Pallas kernels: 42.9 us -> 104 us  [the longest x24 89.9 us: call(): pl.pallas_call(whole, out_shape=tuple(outputs), in_specs=[SMEM] * len(lea...]
    ppermute x58 -> x63, waiting for transfers between devices: 170 us -> 124 us  [swap(): lax.ppermute(values, axis, [(place, place ^ mask) for place in range(size)])]
    dot_general x15 -> x2, matrix products: 48.2 us -> 8.1 us  [dot(): return lax.dot_general(a, b, (dims, ((), ())), preferred_element_type=F32)]
    reduce_sum x22 -> x0, other arithmetic: 28.8 us -> none  [the longest x4 5.41 us: on_device(): update_sq = jnp.stack([jnp.sum(entry[2] * entry[2]) for entry in updated])]
    add x23 -> x8, other arithmetic: 13.6 us -> 1.92 us  [the longest x2 1.22 us: all_sum(): values = near + far]
    another operation x40 -> x10, other arithmetic: 10.6 us -> 1.3 us  [the longest x1 0.91 us: on_device(): jnp.stack([first_new[4], second_new[4], directions[4]])]
    slice x13 -> x7, local copies, waits for them, and re-layouts: 10.1 us -> 1.9 us  [the longest x1 0.68 us: on_device(): norms[:2, :4].reshape(8)]
    unnamed x163 -> x129, local copies, waits for them, and re-layouts: 6.82 us -> 14.8 us
  transfers between devices with their start and end apart: 64 -> 69, of which waited for: 35 -> 25; matrix products, arithmetic and copies ran while one was open for 24% -> 7% of each run, Pallas kernels for 9% -> 19%
where the time goes in v3:
time: 365 us; the launch traced here: 362 us
  waiting for transfers between devices  125 us (34%)
  Pallas kernels  104 us (28%)
  starting transfers between devices  84.3 us (23%)
  local copies, waits for them, and re-layouts  26.6 us (7%)
  other arithmetic  9.59 us (3%)
  matrix products  8.1 us (2%)
  between operations  4.44 us (1%)
    ppermute x63, waiting for transfers between devices, swap(): lax.ppermute(values, axis, [(place, place ^ mask) for place in range(size)])  124 us
    pallas_call x24, Pallas kernels, call(): pl.pallas_call(whole, out_shape=tuple(outputs), in_specs=[SMEM] * len(lea...  89.9 us
    ppermute x63, starting transfers between devices, swap(): lax.ppermute(values, axis, [(place, place ^ mask) for place in range(size)])  64.1 us
    unnamed x129, local copies, waits for them, and re-layouts  14.8 us
    ppermute x3, starting transfers between devices, on_device(): lax.ppermute(block, BOTH, block_permutation(slot, False))  11.5 us
    ppermute x3, starting transfers between devices, blocks_to_owners(): arrived.append(lax.ppermute(sent, BOTH, block_permutation(slot, True)))  8.65 us
    dot_general x2, matrix products, dot(): return lax.dot_general(a, b, (dims, ((), ())), preferred_element_type=F32)  8.1 us
  transfers between devices with their start and end apart: 69, of which 25 were waited for; matrix products, arithmetic and copies ran while one was open for 7% of the time, Pallas kernels for 19%

profile of v3, /device:TPU:0, one launch (start us, length us, event | category | flops | bytes accessed | tf_op | source)
XLA Modules:
  0.0 361.9 jit_solution(10536558308322919621)
XLA Ops:
  5.5 6.5 %collective-permute-start.1 = (bf16[24,768]{1,0:T(8,128)(2,1)S(1)}, bf16[24,768]{1,0:T(8,128)(2,1)S(1)}, u32[]{:S(2)}, u32[]{:S(2)}) collective-permute-start(bf16[24,768]{1,0:T(8,128)(2,1)S(1)} %copy-done.60), channel_id=1, source_target_pairs={{0,4},{1,16},{2,28},{3,9},{4,21},{5,2},{6,14},{7,26},{8,7},{9,19},... | collective-permute-start | bytes 110600 | tf_op jit(solution)/shard_map/ppermute | solution.py:1257
  12.0 4.4 %collective-permute-start.2 = (bf16[24,768]{1,0:T(8,128)(2,1)S(1)}, bf16[24,768]{1,0:T(8,128)(2,1)S(1)}, u32[]{:S(2)}, u32[]{:S(2)}) collective-permute-start(bf16[24,768]{1,0:T(8,128)(2,1)S(1)} %copy-done.59), channel_id=1, source_target_pairs={{0,8},{1,20},{2,1},{3,13},{4,25},{5,6},{6,18},{7,30},{8,11},{9,23}... | collective-permute-start | bytes 110600 | tf_op jit(solution)/shard_map/ppermute | solution.py:1257
  23.9 3.0 collective-permute-start.12
  26.9 3.0 collective-permute-done.5.refs_3_
  29.9 3.9 %collective-permute-start.11 = (bf16[2,48,1536]{2,1,0:T(8,128)(2,1)S(1)}, bf16[2,48,1536]{2,1,0:T(8,128)(2,1)S(1)}, u32[]{:S(2)}, u32[]{:S(2)}) collective-permute-start(bf16[2,48,1536]{2,1,0:T(8,128)(2,1)S(1)} %get-tuple-element.142.refs_4_), channel_id=1, source_target_pairs={{0,2},{1,3},{2,0},{3,1},{4,6},{5,7},{6,4},{7,5},{8,10},{9,11},{10,... | collective-permute-start | bytes 884744 | tf_op jit(solution)/shard_map/ppermute | solution.py:1014
  36.4 5.9 %collective-permute-done.10.refs_3_ = bf16[2,48,384]{2,1,0:T(8,128)(2,1)S(1)} collective-permute-done((bf16[2,48,384]{2,1,0:T(8,128)(2,1)S(1)}, bf16[2,48,384]{2,1,0:T(8,128)(2,1)S(1)}, u32[]{:S(2)}, u32[]{:S(2)}) %collective-permute-start.10) | collective-permute-done | bytes 73760 | tf_op jit(solution)/shard_map/ppermute | solution.py:1014
  42.3 8.3 %collective-permute-done.11.refs_5_ = bf16[2,48,1536]{2,1,0:T(8,128)(2,1)S(1)} collective-permute-done((bf16[2,48,1536]{2,1,0:T(8,128)(2,1)S(1)}, bf16[2,48,1536]{2,1,0:T(8,128)(2,1)S(1)}, u32[]{:S(2)}, u32[]{:S(2)}) %collective-permute-start.11) | collective-permute-done | bytes 294944 | tf_op jit(solution)/shard_map/ppermute | solution.py:1014
  61.1 8.1 %collective-permute-done.15.refs_6_ = bf16[4,48,384]{2,1,0:T(8,128)(2,1)} collective-permute-done((bf16[4,48,384]{2,1,0:T(8,128)(2,1)}, bf16[4,48,384]{2,1,0:T(8,128)(2,1)}, u32[]{:S(2)}, u32[]{:S(2)}) %collective-permute-start.15) | collective-permute-done | bytes 147488 | tf_op jit(solution)/shard_map/ppermute | solution.py:1014
  69.3 4.9 %project.1 = (bf16[2048,768]{1,0:T(8,128)(2,1)S(1)}, bf16[768,768]{1,0:T(8,128)(2,1)S(1)}, bf16[8,48,384]{2,1,0:T(8,128)(2,1)S(1)}, bf16[4,48,768]{2,1,0:T(8,128)(2,1)S(1)}, bf16[4,48,768]{2,1,0:T(8,128)(2,1)S(1)}) custom-call(bf16[1024,768]{1,0:T(8,128)(2,1)S(1)} %get-tuple-element.144.refs_0_.refs_1_, ...), custom_call_target="tpu_custom_call" | custom-call | flops 20000000000 | tf_op jit(solution)/shard_map/project/pallas_call | solution.py:306
  79.5 15.5 %attention_forward.1 = (bf16[192,1024]{1,0:T(8,128)(2,1)S(1)}, bf16[192,1024]{1,0:T(8,128)(2,1)S(1)}, f32[8,2048]{1,0:T(8,128)S(1)}) custom-call(s32[1,3]{1,0:T(1,128)S(1)} %copy-done.24, bf16[2048,768]{1,0:T(8,128)(2,1)S(1)} %get-tuple-element.148.refs_1_), custom_call_target="tpu_custom_call" | custom-call | flops 64000000000 | tf_op jit(solution)/shard_map/attention_forward/pallas_call | solution.py:306
  97.3 7.8 %collective-permute-done.17.refs_1_.refs_3_ = bf16[192,1024]{1,0:T(8,128)(2,1)S(1)} collective-permute-done((bf16[192,1024]{1,0:T(8,128)(2,1)S(1)}, bf16[192,1024]{1,0:T(8,128)(2,1)S(1)}, u32[]{:S(2)}, u32[]{:S(2)}) %collective-permute-start.17) | collective-permute-done | bytes 393248 | tf_op jit(solution)/shard_map/ppermute | solution.py:1014
  110.9 11.9 %collective-permute-done.27.refs_8_ = bf16[8,48,768]{2,1,0:T(8,128)(2,1)S(1)} collective-permute-done((bf16[8,48,768]{2,1,0:T(8,128)(2,1)S(1)}, bf16[8,48,768]{2,1,0:T(8,128)(2,1)S(1)}, u32[]{:S(2)}, u32[]{:S(2)}) %collective-permute-start.27) | collective-permute-done | bytes 589856 | tf_op jit(solution)/shard_map/ppermute | solution.py:1014
  124.2 11.2 %collective-permute-done.29.refs_12_ = bf16[8,48,1536]{2,1,0:T(8,128)(2,1)S(1)} collective-permute-done((bf16[8,48,1536]{2,1,0:T(8,128)(2,1)S(1)}, bf16[8,48,1536]{2,1,0:T(8,128)(2,1)S(1)}, u32[]{:S(2)}, u32[]{:S(2)}) %collective-permute-start.29) | collective-permute-done | bytes 1179680 | tf_op jit(solution)/shard_map/ppermute | solution.py:1014
  135.4 16.5 %feed_forward.1 = (bf16[1024,1536]{1,0:T(8,128)(2,1)}, bf16[1024,1536]{1,0:T(8,128)(2,1)}, bf16[512,768]{1,0:T(8,128)(2,1)}, f32[512,768]{1,0:T(8,128)S(1)}, bf1...) custom-call(bf16[256,768]{1,0:T(8,128)(2,1)S(1)} %get-tuple-element., ...), custom_call_target="tpu_custom_call" | custom-call | flops 71999995904 | tf_op jit(solution)/shard_map/feed_forward/pallas_call | solution.py:306
  156.3 5.1 %convolution_convert_fusion = bf16[768,1536]{1,0:T(8,128)(2,1)S(1)} fusion(bf16[1024,768]{1,0:T(8,128)(2,1)} %copy-done.26, bf16[1024,1536]{1,0:T(8,128)(2,1)} %get-tuple-element.191), kind=kOutput, calls=%fused_computation | convolution fusion | flops 2417098752 | bytes 7077888 | tf_op jit(solution)/shard_map/dot_general | solution.py:1009
  161.5 3.8 %middle_gradient.1 = (f32[512,768]{1,0:T(8,128)S(1)}, bf16[512,768]{1,0:T(8,128)(2,1)S(1)}, f32[24,128]{1,0:T(8,128)S(1)}) custom-call(f32[512,768]{1,0:T(8,128)S(1)} %copy-done.42, bf16[512,768]{1,0:T(8,128)(2,1)} %collective-permute-done.31.arrived, f32[512,768]{1,0:T(8,128)S(1)} %get-tuple-element.160.middle, bf16[512,768]{1,0:T(8,128)(2,1)S(1)} %copy-done.9, ...), custom_call_target="tpu_custom_call" | custom-call | flops 8000000000 | tf_op jit(solution)/shard_map/middle_gradient/pallas_call | solution.py:905
  179.2 6.2 %collective-permute-done.33.refs_5_ = bf16[192,1024]{1,0:T(8,128)(2,1)S(1)} collective-permute-done((bf16[192,1024]{1,0:T(8,128)(2,1)S(1)}, bf16[192,1024]{1,0:T(8,128)(2,1)S(1)}, u32[]{:S(2)}, u32[]{:S(2)}) %collective-permute-start.33) | collective-permute-done | bytes 393248 | tf_op jit(solution)/shard_map/ppermute | solution.py:1014
  185.4 30.5 %attention_backward.1 = (bf16[2048,768]{1,0:T(8,128)(2,1)S(1)}, f32[8,256]{1,0:T(8,128)S(1)}) custom-call(s32[1,3]{1,0:T(1,128)S(1)} %copy-done.24, bf16[2048,768]{1,0:T(8,128)(2,1)S(1)} %copy-done.46, bf16[192,1024]{1,0:T(8,128)(2,1)S(1)} %copy-done.48, bf16[192,1024]{1,0:T(8,128)(2,1)S(1)} %copy-done.20, bf16[192,1024]{1,0:T(8,128)(2,1)S(1)} %get-tuple-element.172.refs_4_, ...), custom_call_target="tpu_custom_call" | custom-call | flops 128000000000 | tf_op jit(solution)/shard_map/attention_backward/pallas_call | solution.py:306
  217.8 3.7 %input_weight_gradient.1 = (bf16[12,24,384]{2,1,0:T(8,128)(2,1)}, f32[12,24,384]{2,1,0:T(8,128)S(1)}, bf16[12,24,384]{2,1,0:T(8,128)(2,1)S(1)}, f32[12,24,384]{2,1,0:T(8,128)S(1)}) custom-call(bf16[2048,768]{1,0:T(8,128)(2,1)S(1)} %get-tuple-element.177.refs_0_, bf16[1024,768]{1,0:T(8,128)(2,1)S(1)} %copy-done.5, bf16[1024,768]{1,0:T(8,128)(2,1)S(1)} %copy-done.7), custom_call_target="tpu_custom_call" | custom-call | flops 16000000000 | tf_op jit(solution)/shard_map/input_weight_gradient/pallas_call | solution.py:306
  224.3 4.0 %add_arrived.7 = (bf16[4,96,768]{2,1,0:T(8,128)(2,1)}, f32[4,96,768]{2,1,0:T(8,128)S(1)}, bf16[4,48,1920]{2,1,0:T(8,128)(2,1)}, f32[4,48,1920]{2,1,0:T(8,128)S(1)}) custom-call(bf16[16,96,768]{2,1,0:T(8,128)(2,1)S(1)} %bitcast.100, bf16[8,96,768]{2,1,0:T(8,128)(2,1)} %collective-permute-done.39.refs_1_, bf16[16,48,1536]{2,1,0:T(8,128)(2,1)S(1)} %bitcast.97, ...), custom_call_target="tpu_custom_call" | custom-call | flops 4000000000 | tf_op jit(solution)/shard_map/add_arrived/pallas_call | solution.py:306
  232.6 3.5 collective-permute-start.38
  236.1 18.0 %collective-permute-done.37.refs_1_ = bf16[12,24,384]{2,1,0:T(8,128)(2,1)} collective-permute-done((bf16[12,24,384]{2,1,0:T(8,128)(2,1)}, bf16[12,24,384]{2,1,0:T(8,128)(2,1)}, u32[]{:S(2)}, u32[]{:S(2)}) %collective-permute-start.37) | collective-permute-done | bytes 221216 | tf_op jit(solution)/shard_map/ppermute | solution.py:1014
  260.5 3.6 collective-permute-start.42
  267.4 3.6 collective-permute-done.43.refs_3_
  277.0 3.7 %collective-permute-start.59 = (f32[24,768]{1,0:T(8,128)S(1)}, f32[24,768]{1,0:T(8,128)S(1)}, u32[]{:S(2)}, u32[]{:S(2)}) collective-permute-start(f32[24,768]{1,0:T(8,128)S(1)} %get-tuple-element.251), channel_id=1, source_target_pairs={{4,0},{16,1},{28,2},{9,3},{21,4},{2,5},{14,6},{26,7},{7,8},{19,9},... | collective-permute-start | bytes 221192 | tf_op jit(solution)/shard_map/ppermute | solution.py:1199
  280.6 11.4 %collective-permute-done.48.refs_1_ = bf16[2,96,768]{2,1,0:T(8,128)(2,1)S(1)} collective-permute-done((bf16[2,96,768]{2,1,0:T(8,128)(2,1)S(1)}, bf16[2,96,768]{2,1,0:T(8,128)(2,1)S(1)}, u32[]{:S(2)}, u32[]{:S(2)}) %collective-permute-start.48) | collective-permute-done | bytes 294944 | tf_op jit(solution)/shard_map/ppermute | solution.py:1014
  292.0 4.3 %collective-permute-start.60 = (f32[24,768]{1,0:T(8,128)S(1)}, f32[24,768]{1,0:T(8,128)S(1)}, u32[]{:S(2)}, u32[]{:S(2)}) collective-permute-start(f32[24,768]{1,0:T(8,128)S(1)} %get-tuple-element.250), channel_id=1, source_target_pairs={{8,0},{20,1},{1,2},{13,3},{25,4},{6,5},{18,6},{30,7},{11,8},{23,9}... | collective-permute-start | bytes 221192 | tf_op jit(solution)/shard_map/ppermute | solution.py:1199
  303.2 11.8 %collective-permute-done.50.refs_1_ = bf16[1,96,768]{2,1,0:T(8,128)(2,1)S(1)} collective-permute-done((bf16[1,96,768]{2,1,0:T(8,128)(2,1)S(1)}, bf16[1,96,768]{2,1,0:T(8,128)(2,1)S(1)}, u32[]{:S(2)}, u32[]{:S(2)}) %collective-permute-start.50) | collective-permute-done | bytes 147488 | tf_op jit(solution)/shard_map/ppermute | solution.py:1014
  317.6 3.8 %collective-permute-done.53 = f32[80,128]{1,0:T(8,128)S(1)} collective-permute-done((f32[80,128]{1,0:T(8,128)S(1)}, f32[80,128]{1,0:T(8,128)S(1)}, u32[]{:S(2)}, u32[]{:S(2)}) %collective-permute-start.53) | collective-permute-done | bytes 40992 | tf_op jit(solution)/shard_map/ppermute | solution.py:1014
  322.3 3.1 collective-permute-done.54
  333.5 4.3 %moments.1 = (f32[72,768]{1,0:T(8,128)}, f32[24,768]{1,0:T(8,128)}, f32[96,768]{1,0:T(8,128)}, f32[24,3072]{1,0:T(8,128)}, f32[72,128]{1,0:T(8,128)}, /*index=5*...) custom-call(f32[80,128]{1,0:T(8,128)} %add_add_fusion.refs_0_.refs_5, ...), custom_call_target="tpu_custom_call" | custom-call | flops 16000000000 | tf_op jit(solution)/shard_map/moments/pallas_call | solution.py:959
  347.2 3.3 collective-permute-start.67
  (323 shorter events, 118.9 us)
Async XLA Ops:
  4.7 16.9 %collective-permute-start.6 = (bf16[24,16,96]{2,1,0:T(8,128)(2,1)S(1)}, bf16[24,16,96]{2,1,0:T(8,128)(2,1)S(1)}, u32[]{:S(2)}, u32[]{:S(2)}) collective-permute-start(bf16[24,16,96]{2,1,0:T(8,128)(2,1)S(1)} %bitcast.133), channel_id=1, source_target_pairs={{0,1},{1,0},{2,3},{3,2},{4,5},{5,4},{6,7},{7,6},{8,9},{9,8},{10,11... | collective-permute-start | bytes 221192 | tf_op jit(solution)/shard_map/ppermute | solution.py:1014
  23.9 26.8 %collective-permute-start.12 = (bf16[512,768]{1,0:T(8,128)(2,1)S(1)}, bf16[512,768]{1,0:T(8,128)(2,1)S(1)}, u32[]{:S(2)}, u32[]{:S(2)}) collective-permute-start(bf16[512,768]{1,0:T(8,128)(2,1)S(1)} %copy-done.16), channel_id=1, source_target_pairs={{0,2},{1,3},{2,0},{3,1},{4,6},{5,7},{6,4},{7,5},{8,10},{9,11},{10,... | collective-permute-start | bytes 2359304 | tf_op jit(solution)/shard_map/ppermute | solution.py:1014
  29.9 20.7 %collective-permute-start.11 = (bf16[2,48,1536]{2,1,0:T(8,128)(2,1)S(1)}, bf16[2,48,1536]{2,1,0:T(8,128)(2,1)S(1)}, u32[]{:S(2)}, u32[]{:S(2)}) collective-permute-start(bf16[2,48,1536]{2,1,0:T(8,128)(2,1)S(1)} %get-tuple-element.142.refs_4_), channel_id=1, source_target_pairs={{0,2},{1,3},{2,0},{3,1},{4,6},{5,7},{6,4},{7,5},{8,10},{9,11},{10,... | collective-permute-start | bytes 884744 | tf_op jit(solution)/shard_map/ppermute | solution.py:1014
  52.5 16.8 %collective-permute-start.13 = (bf16[1024,768]{1,0:T(8,128)(2,1)S(1)}, bf16[1024,768]{1,0:T(8,128)(2,1)S(1)}, u32[]{:S(2)}, u32[]{:S(2)}) collective-permute-start(bf16[1024,768]{1,0:T(8,128)(2,1)S(1)} %get-tuple-element.144.refs_0_.refs_1_), channel_id=1, source_target_pairs={{0,1},{1,0},{2,3},{3,2},{4,5},{5,4},{6,7},{7,6},{8,9},{9,8},{10,11... | collective-permute-start | bytes 4718600 | tf_op jit(solution)/shard_map/ppermute | solution.py:1014
  53.4 15.9 %collective-permute-start.14 = (bf16[4,72,768]{2,1,0:T(8,128)(2,1)}, bf16[4,72,768]{2,1,0:T(8,128)(2,1)}, u32[]{:S(2)}, u32[]{:S(2)}) collective-permute-start(bf16[4,72,768]{2,1,0:T(8,128)(2,1)} %get-tuple-element.145.refs_3_), channel_id=1, source_target_pairs={{0,4},{4,0},{8,12},{12,8},{16,20},{20,16},{24,28},{28,24},{1,5},{5... | collective-permute-start | bytes 1327112 | tf_op jit(solution)/shard_map/ppermute | solution.py:1014
  55.4 13.8 %collective-permute-start.16 = (bf16[2,96,768]{2,1,0:T(8,128)(2,1)S(1)}, bf16[2,96,768]{2,1,0:T(8,128)(2,1)}, u32[]{:S(2)}, u32[]{:S(2)}) collective-permute-start(bf16[2,96,768]{2,1,0:T(8,128)(2,1)S(1)} %get-tuple-element.147.refs_7_), channel_id=1, source_target_pairs={{0,8},{4,12},{8,0},{12,4},{16,24},{20,28},{24,16},{28,20},{1,9},{5... | collective-permute-start | bytes 884744 | tf_op jit(solution)/shard_map/ppermute | solution.py:1014
  55.4 13.8 %collective-permute-start.15 = (bf16[4,48,384]{2,1,0:T(8,128)(2,1)}, bf16[4,48,384]{2,1,0:T(8,128)(2,1)}, u32[]{:S(2)}, u32[]{:S(2)}) collective-permute-start(bf16[4,48,384]{2,1,0:T(8,128)(2,1)} %get-tuple-element.146.refs_5_), channel_id=1, source_target_pairs={{0,4},{4,0},{8,12},{12,8},{16,20},{20,16},{24,28},{28,24},{1,5},{5... | collective-permute-start | bytes 442376 | tf_op jit(solution)/shard_map/ppermute | solution.py:1014
  60.3 36.8 %collective-permute-start.20 = (bf16[4,48,1536]{2,1,0:T(8,128)(2,1)}, bf16[4,48,1536]{2,1,0:T(8,128)(2,1)S(1)}, u32[]{:S(2)}, u32[]{:S(2)}) collective-permute-start(bf16[4,48,1536]{2,1,0:T(8,128)(2,1)} %copy-done.17), channel_id=1, source_target_pairs={{0,16},{4,20},{8,24},{12,28},{16,0},{20,4},{24,8},{28,12},{1,17},{... | collective-permute-start | bytes 1769480 | tf_op jit(solution)/shard_map/ppermute | solution.py:1014
  75.3 21.8 %collective-permute-start.18 = (bf16[4,48,768]{2,1,0:T(8,128)(2,1)S(1)}, bf16[4,48,768]{2,1,0:T(8,128)(2,1)S(1)}, u32[]{:S(2)}, u32[]{:S(2)}) collective-permute-start(bf16[4,48,768]{2,1,0:T(8,128)(2,1)S(1)} %get-tuple-element.151.refs_0_), channel_id=1, source_target_pairs={{0,4},{4,0},{8,12},{12,8},{16,20},{20,16},{24,28},{28,24},{1,5},{5... | collective-permute-start | bytes 884744 | tf_op jit(solution)/shard_map/ppermute | solution.py:1014
  77.0 20.1 %collective-permute-start.19 = (bf16[4,48,768]{2,1,0:T(8,128)(2,1)S(1)}, bf16[4,48,768]{2,1,0:T(8,128)(2,1)S(1)}, u32[]{:S(2)}, u32[]{:S(2)}) collective-permute-start(bf16[4,48,768]{2,1,0:T(8,128)(2,1)S(1)} %get-tuple-element.152.refs_2_), channel_id=1, source_target_pairs={{0,2},{1,3},{2,0},{3,1},{4,6},{5,7},{6,4},{7,5},{8,10},{9,11},{10,... | collective-permute-start | bytes 884744 | tf_op jit(solution)/shard_map/ppermute | solution.py:1014
  79.4 17.7 %collective-permute-start.21 = (bf16[8,48,384]{2,1,0:T(8,128)(2,1)S(1)}, bf16[8,48,384]{2,1,0:T(8,128)(2,1)S(1)}, u32[]{:S(2)}, u32[]{:S(2)}) collective-permute-start(bf16[8,48,384]{2,1,0:T(8,128)(2,1)S(1)} %get-tuple-element.154.refs_6_), channel_id=1, source_target_pairs={{0,2},{1,3},{2,0},{3,1},{4,6},{5,7},{6,4},{7,5},{8,10},{9,11},{10,... | collective-permute-start | bytes 884744 | tf_op jit(solution)/shard_map/ppermute | solution.py:1014
  107.1 28.3 %collective-permute-start.29 = (bf16[8,48,1536]{2,1,0:T(8,128)(2,1)S(1)}, bf16[8,48,1536]{2,1,0:T(8,128)(2,1)S(1)}, u32[]{:S(2)}, u32[]{:S(2)}) collective-permute-start(bf16[8,48,1536]{2,1,0:T(8,128)(2,1)S(1)} %get-tuple-element.156.refs_3_.refs_11_), channel_id=1, source_target_pairs={{0,8},{4,12},{8,0},{12,4},{16,24},{20,28},{24,16},{28,20},{1,9},{5... | collective-permute-start | bytes 3538952 | tf_op jit(solution)/shard_map/ppermute | solution.py:1014
  107.1 15.7 %collective-permute-start.27 = (bf16[8,48,768]{2,1,0:T(8,128)(2,1)S(1)}, bf16[8,48,768]{2,1,0:T(8,128)(2,1)S(1)}, u32[]{:S(2)}, u32[]{:S(2)}) collective-permute-start(bf16[8,48,768]{2,1,0:T(8,128)(2,1)S(1)} %get-tuple-element.163.refs_7_), channel_id=1, source_target_pairs={{0,2},{1,3},{2,0},{3,1},{4,6},{5,7},{6,4},{7,5},{8,10},{9,11},{10,... | collective-permute-start | bytes 1769480 | tf_op jit(solution)/shard_map/ppermute | solution.py:1014
  108.8 15.4 %collective-permute-start.28 = (bf16[8,48,768]{2,1,0:T(8,128)(2,1)S(1)}, bf16[8,48,768]{2,1,0:T(8,128)(2,1)S(1)}, u32[]{:S(2)}, u32[]{:S(2)}) collective-permute-start(bf16[8,48,768]{2,1,0:T(8,128)(2,1)S(1)} %get-tuple-element.164.refs_9_), channel_id=1, source_target_pairs={{0,4},{4,0},{8,12},{12,8},{16,20},{20,16},{24,28},{28,24},{1,5},{5... | collective-permute-start | bytes 1769480 | tf_op jit(solution)/shard_map/ppermute | solution.py:1014
  109.6 14.6 %collective-permute-start.24 = (bf16[256,768]{1,0:T(8,128)(2,1)S(1)}, bf16[256,768]{1,0:T(8,128)(2,1)S(1)}, u32[]{:S(2)}, u32[]{:S(2)}) collective-permute-start(bf16[256,768]{1,0:T(8,128)(2,1)S(1)} %get-tuple-element.161.refs_0_), channel_id=1, source_target_pairs={{0,1},{1,0},{2,3},{3,2},{4,5},{5,4},{6,7},{7,6},{8,9},{9,8},{10,11... | collective-permute-start | bytes 1179656 | tf_op jit(solution)/shard_map/ppermute | solution.py:1014
  109.9 14.3 %collective-permute-start.25 = (bf16[256,768]{1,0:T(8,128)(2,1)S(1)}, bf16[256,768]{1,0:T(8,128)(2,1)S(1)}, u32[]{:S(2)}, u32[]{:S(2)}) collective-permute-start(bf16[256,768]{1,0:T(8,128)(2,1)S(1)} %get-tuple-element.162.refs_1_), channel_id=1, source_target_pairs={{0,1},{1,0},{2,3},{3,2},{4,5},{5,4},{6,7},{7,6},{8,9},{9,8},{10,11... | collective-permute-start | bytes 1179656 | tf_op jit(solution)/shard_map/ppermute | solution.py:1014
  168.1 56.1 %collective-permute-start.40 = (bf16[8,48,1536]{2,1,0:T(8,128)(2,1)}, bf16[8,48,1536]{2,1,0:T(8,128)(2,1)}, u32[]{:S(2)}, u32[]{:S(2)}) collective-permute-start(bf16[8,48,1536]{2,1,0:T(8,128)(2,1)} %bitcast.19), channel_id=1, source_target_pairs={{0,8},{4,12},{8,0},{12,4},{16,24},{20,28},{24,16},{28,20},{1,9},{5... | collective-permute-start | bytes 3538952 | tf_op jit(solution)/shard_map/ppermute | solution.py:1014
  172.5 51.8 %collective-permute-start.39 = (bf16[8,96,768]{2,1,0:T(8,128)(2,1)}, bf16[8,96,768]{2,1,0:T(8,128)(2,1)}, u32[]{:S(2)}, u32[]{:S(2)}) collective-permute-start(bf16[8,96,768]{2,1,0:T(8,128)(2,1)} %bitcast.16), channel_id=1, source_target_pairs={{0,4},{4,0},{8,12},{12,8},{16,20},{20,16},{24,28},{28,24},{1,5},{5... | collective-permute-start | bytes 3538952 | tf_op jit(solution)/shard_map/ppermute | solution.py:1014
  177.5 46.8 %collective-permute-start.41 = (bf16[8,48,384]{2,1,0:T(8,128)(2,1)}, bf16[8,48,384]{2,1,0:T(8,128)(2,1)}, u32[]{:S(2)}, u32[]{:S(2)}) collective-permute-start(bf16[8,48,384]{2,1,0:T(8,128)(2,1)} %bitcast.21), channel_id=1, source_target_pairs={{0,8},{4,12},{8,0},{12,4},{16,24},{20,28},{24,16},{28,20},{1,9},{5... | collective-permute-start | bytes 884744 | tf_op jit(solution)/shard_map/ppermute | solution.py:1014
  230.5 34.1 %collective-permute-start.45 = (bf16[4,48,1920]{2,1,0:T(8,128)(2,1)}, bf16[4,48,1920]{2,1,0:T(8,128)(2,1)}, u32[]{:S(2)}, u32[]{:S(2)}) collective-permute-start(bf16[4,48,1920]{2,1,0:T(8,128)(2,1)} %get-tuple-element.199), channel_id=1, source_target_pairs={{0,4},{4,0},{8,12},{12,8},{16,20},{20,16},{24,28},{28,24},{1,5},{5... | collective-permute-start | bytes 2211848 | tf_op jit(solution)/shard_map/ppermute | solution.py:1014
  230.5 23.6 %collective-permute-start.37 = (bf16[12,24,384]{2,1,0:T(8,128)(2,1)}, bf16[12,24,384]{2,1,0:T(8,128)(2,1)}, u32[]{:S(2)}, u32[]{:S(2)}) collective-permute-start(bf16[12,24,384]{2,1,0:T(8,128)(2,1)} %get-tuple-element.187), channel_id=1, source_target_pairs={{0,4},{4,0},{8,12},{12,8},{16,20},{20,16},{24,28},{28,24},{1,5},{5... | collective-permute-start | bytes 663560 | tf_op jit(solution)/shard_map/ppermute | solution.py:1014
  232.6 23.2 %collective-permute-start.38 = (bf16[12,24,384]{2,1,0:T(8,128)(2,1)S(1)}, bf16[12,24,384]{2,1,0:T(8,128)(2,1)}, u32[]{:S(2)}, u32[]{:S(2)}) collective-permute-start(bf16[12,24,384]{2,1,0:T(8,128)(2,1)S(1)} %get-tuple-element.189), channel_id=1, source_target_pairs={{0,8},{4,12},{8,0},{12,4},{16,24},{20,28},{24,16},{28,20},{1,9},{5... | collective-permute-start | bytes 663560 | tf_op jit(solution)/shard_map/ppermute | solution.py:1014
  236.1 28.0 %collective-permute-start.44 = (bf16[4,96,768]{2,1,0:T(8,128)(2,1)}, bf16[4,96,768]{2,1,0:T(8,128)(2,1)}, u32[]{:S(2)}, u32[]{:S(2)}) collective-permute-start(bf16[4,96,768]{2,1,0:T(8,128)(2,1)} %get-tuple-element.197), channel_id=1, source_target_pairs={{0,8},{4,12},{8,0},{12,4},{16,24},{20,28},{24,16},{28,20},{1,9},{5... | collective-permute-start | bytes 1769480 | tf_op jit(solution)/shard_map/ppermute | solution.py:1014
  236.1 36.1 %collective-permute-start.30 = (bf16[512,768]{1,0:T(8,128)(2,1)}, bf16[512,768]{1,0:T(8,128)(2,1)S(1)}, u32[]{:S(2)}, u32[]{:S(2)}) collective-permute-start(bf16[512,768]{1,0:T(8,128)(2,1)} %copy-done.12), channel_id=1, source_target_pairs={{0,1},{1,0},{2,3},{3,2},{4,5},{5,4},{6,7},{7,6},{8,9},{9,8},{10,11... | collective-permute-start | bytes 2359304 | tf_op jit(solution)/shard_map/ppermute | solution.py:1014
  254.1 19.9 %collective-permute-start.36 = (bf16[512,768]{1,0:T(8,128)(2,1)}, bf16[512,768]{1,0:T(8,128)(2,1)S(1)}, u32[]{:S(2)}, u32[]{:S(2)}) collective-permute-start(bf16[512,768]{1,0:T(8,128)(2,1)} %copy-done.15), channel_id=1, source_target_pairs={{0,2},{1,3},{2,0},{3,1},{4,6},{5,7},{6,4},{7,5},{8,10},{9,11},{10,... | collective-permute-start | bytes 2359304 | tf_op jit(solution)/shard_map/ppermute | solution.py:1014
  273.5 25.6 %collective-permute-start.35 = (bf16[512,768]{1,0:T(8,128)(2,1)S(1)}, bf16[512,768]{1,0:T(8,128)(2,1)S(1)}, u32[]{:S(2)}, u32[]{:S(2)}) collective-permute-start(bf16[512,768]{1,0:T(8,128)(2,1)S(1)} %copy-done.14), channel_id=1, source_target_pairs={{0,1},{1,0},{2,3},{3,2},{4,5},{5,4},{6,7},{7,6},{8,9},{9,8},{10,11... | collective-permute-start | bytes 2359304 | tf_op jit(solution)/shard_map/ppermute | solution.py:1014
  273.5 22.9 %collective-permute-start.49 = (bf16[2,48,1920]{2,1,0:T(8,128)(2,1)S(1)}, bf16[2,48,1920]{2,1,0:T(8,128)(2,1)S(1)}, u32[]{:S(2)}, u32[]{:S(2)}) collective-permute-start(bf16[2,48,1920]{2,1,0:T(8,128)(2,1)S(1)} %get-tuple-element.209), channel_id=1, source_target_pairs={{0,2},{1,3},{2,0},{3,1},{4,6},{5,7},{6,4},{7,5},{8,10},{9,11},{10,... | collective-permute-start | bytes 1105928 | tf_op jit(solution)/shard_map/ppermute | solution.py:1014
  274.0 18.0 %collective-permute-start.48 = (bf16[2,96,768]{2,1,0:T(8,128)(2,1)S(1)}, bf16[2,96,768]{2,1,0:T(8,128)(2,1)S(1)}, u32[]{:S(2)}, u32[]{:S(2)}) collective-permute-start(bf16[2,96,768]{2,1,0:T(8,128)(2,1)S(1)} %get-tuple-element.207), channel_id=1, source_target_pairs={{0,2},{1,3},{2,0},{3,1},{4,6},{5,7},{6,4},{7,5},{8,10},{9,11},{10,... | collective-permute-start | bytes 884744 | tf_op jit(solution)/shard_map/ppermute | solution.py:1014
  276.3 26.1 %collective-permute-start.58 = (f32[24,768]{1,0:T(8,128)S(1)}, f32[24,768]{1,0:T(8,128)S(1)}, u32[]{:S(2)}, u32[]{:S(2)}) collective-permute-start(f32[24,768]{1,0:T(8,128)S(1)} %get-tuple-element.249), channel_id=1, source_target_pairs={{0,0},{12,1},{24,2},{5,3},{17,4},{29,5},{10,6},{22,7},{3,8},{15,9}... | collective-permute-start | bytes 221192 | tf_op jit(solution)/shard_map/ppermute | solution.py:1199
  277.0 25.5 %collective-permute-start.59 = (f32[24,768]{1,0:T(8,128)S(1)}, f32[24,768]{1,0:T(8,128)S(1)}, u32[]{:S(2)}, u32[]{:S(2)}) collective-permute-start(f32[24,768]{1,0:T(8,128)S(1)} %get-tuple-element.251), channel_id=1, source_target_pairs={{4,0},{16,1},{28,2},{9,3},{21,4},{2,5},{14,6},{26,7},{7,8},{19,9},... | collective-permute-start | bytes 221192 | tf_op jit(solution)/shard_map/ppermute | solution.py:1199
  296.6 18.4 %collective-permute-start.51 = (bf16[1,48,1920]{2,1,0:T(8,128)(2,1)S(1)}, bf16[1,48,1920]{2,1,0:T(8,128)(2,1)S(1)}, u32[]{:S(2)}, u32[]{:S(2)}) collective-permute-start(bf16[1,48,1920]{2,1,0:T(8,128)(2,1)S(1)} %get-tuple-element.213), channel_id=1, source_target_pairs={{0,16},{4,20},{8,24},{12,28},{16,0},{20,4},{24,8},{28,12},{1,17},{... | collective-permute-start | bytes 552968 | tf_op jit(solution)/shard_map/ppermute | solution.py:1014
  299.1 15.8 %collective-permute-start.50 = (bf16[1,96,768]{2,1,0:T(8,128)(2,1)S(1)}, bf16[1,96,768]{2,1,0:T(8,128)(2,1)S(1)}, u32[]{:S(2)}, u32[]{:S(2)}) collective-permute-start(bf16[1,96,768]{2,1,0:T(8,128)(2,1)S(1)} %get-tuple-element.211), channel_id=1, source_target_pairs={{0,16},{4,20},{8,24},{12,28},{16,0},{20,4},{24,8},{28,12},{1,17},{... | collective-permute-start | bytes 442376 | tf_op jit(solution)/shard_map/ppermute | solution.py:1014
  (100 other events, 643.8 us)
